TPU v7x, 512 devices: a whole 4x8x8 slice. The times are simulated.
512 devices in a mesh: gx: 64 (over z, x, core), gy: 8 (over y).
Axes of the slice: x: 4, y: 8, z: 8, core: 2. Of those that a mesh axis runs over, the one named last changes fastest.
Arguments:
- velocity: float32 [3, 128, 1536, 128], P(None, 'gx', 'gy'), may hold values from -0.8 to 2.3
- stiffness: float32 [8], P('gy'), may hold values from 100 to 100000
- block_inverse: float32 [3, 1536, 192], P(None, 'gy'), as said below
Outputs:
- velocity_next: float32 [3, 128, 1536, 128], P(None, 'gx', 'gy')
Inputs may be any that keep to these rules, and one draw needn't show every extreme that they name: block_inverse[s] for block k is, to float32 rounding, the inverse of the 192-row matrix with 1 + 2 b on its diagonal and -b beside it, b = alpha_s stiffness[k].
All inputs are finite; a program needn't handle non-finite values.
Results may differ from a plain program's by a relative error of at most 0.0003.
Values sent between devices are 32-bit elements; how exact they have to be, the bound alone decides.
No kernel may reach another device: no remote copies, remote signals or barrier semaphores. Data moves between devices by JAX's collectives and lax.ppermute only.
A program may use at most 64 MiB of HBM per device.

v0:
```python
import functools

import jax
import jax.numpy as jnp
from jax import lax
from jax.experimental import pallas as pl
from jax.experimental.pallas import tpu as pltpu
from jax.sharding import PartitionSpec as P


SUBSTEPS = 3
implicit_share = (8.0 / 15.0, 2.0 / 15.0, 1.0 / 3.0)
new_weight = (8.0 / 15.0, 5.0 / 12.0, 3.0 / 4.0)
old_weight = (0.0, -17.0 / 60.0, -5.0 / 12.0)
courant = (0.3, 0.2, 0.3)

CY = 192
LANES = 128
CHUNK = 32
ENDS = (0, 1, CY - 2, CY - 1)

VMEM = pl.BlockSpec(memory_space=pltpu.VMEM)
HBM = pl.BlockSpec(memory_space=pltpu.HBM)
SMEM = pl.BlockSpec(memory_space=pltpu.SMEM)


def swaps(count, offset, closed):
    pairs = []
    for a in range(offset, count + offset - 1, 2):
        b = a + 1
        if b < count:
            pairs += [(a, b), (b, a)]
        elif closed:
            pairs += [(a, 0), (0, a)]
    return pairs


def lines():
    return [(c, x) for c in range(3) for x in range(2)]


def pack_kernel(velocity, u_ref, send_ref, top, bottom, sems):
    copies = [
        pltpu.make_async_copy(velocity.at[:, :, pl.ds(0, 8), :], top, sems.at[0]),
        pltpu.make_async_copy(velocity.at[:, :, pl.ds(CY - 8, 8), :], bottom, sems.at[1]),
        pltpu.make_async_copy(velocity, u_ref, sems.at[2]),
    ]
    for copy in copies:
        copy.start()
    copies[0].wait()
    copies[1].wait()
    for t, (source, row) in enumerate(((top, 0), (top, 1), (bottom, 6), (bottom, 7))):
        picked = [source[c, x, row : row + 1, :] for c, x in lines()]
        tile = jnp.concatenate(picked + picked[:2], axis=0)
        for dest in range(8):
            send_ref[dest, t] = tile
    copies[2].wait()


def own_kernel(step, *refs):
    if step == 0:
        stiff_ref, u_ref, got, *refs = refs
        old_ref = None
        own = lax.axis_index("gy")
        before = jnp.maximum(own - 1, 0)
        behind = jnp.minimum(own + 1, 7)
        ends = [jnp.where(own > 0, got[before, t], 0.0) for t in (2, 3)]
        ends += [jnp.where(own < 7, got[behind, t], 0.0) for t in (0, 1)]
    else:
        stiff_ref, u_ref, ends_ref, old_share, old_ref, *refs = refs
        ends = [ends_ref[t] for t in range(4)]
    if step < SUBSTEPS - 1:
        part_ref, share_ref, pad = refs
    else:
        part_ref, pad = refs
        share_ref = None
    stiff = stiff_ref[0]

    for c in range(3):
        for x in range(2):
            pad[c, x, 8 : 8 + CY, :] = u_ref[c, x]
            line = slice(2 * c + x, 2 * c + x + 1)
            pad[c, x, 6:7, :] = ends[0][line]
            pad[c, x, 7:8, :] = ends[1][line]
            pad[c, x, 8 + CY : 9 + CY, :] = ends[2][line]
            pad[c, x, 9 + CY : 10 + CY, :] = ends[3][line]

    for r in range(0, CY, CHUNK):
        rows = slice(r, r + CHUNK)
        for x in range(2):
            speed = [u_ref[d, x, rows, :] for d in range(3)]
            plus = [2.0 * courant[d] * jnp.maximum(speed[d], 0.0) for d in range(3)]
            minus = [2.0 * courant[d] * jnp.minimum(speed[d], 0.0) for d in range(3)]
            total = plus[0] - minus[0]
            for d in (1, 2):
                total = total + (plus[d] - minus[d])
            total = 0.75 * total
            for c in range(3):
                f = speed[c]
                adv = total * f
                y2, y1 = pad[c, x, 6 + r : 6 + r + CHUNK, :], pad[c, x, 7 + r : 7 + r + CHUNK, :]
                w1, w2 = pad[c, x, 9 + r : 9 + r + CHUNK, :], pad[c, x, 10 + r : 10 + r + CHUNK, :]
                adv = adv + plus[1] * (0.25 * y2 - y1) + minus[1] * (w1 - 0.25 * w2)
                z1, z2 = pltpu.roll(f, 1, 1), pltpu.roll(f, 2, 1)
                t1, t2 = pltpu.roll(f, LANES - 1, 1), pltpu.roll(f, LANES - 2, 1)
                adv = adv + plus[2] * (0.25 * z2 - z1) + minus[2] * (t1 - 0.25 * t2)
                forcing = f + (implicit_share[step] * stiff) * (w1 - 2.0 * f + y1) - new_weight[step] * adv
                if old_ref is not None:
                    old = old_share[c, x, rows, :] + old_ref[c, x, rows, :]
                    forcing = forcing - old_weight[step] * old
                part_ref[c, x, rows, :] = forcing
                if share_ref is not None:
                    share_ref[c, x, rows, :] = adv


def planes_kernel(step, *refs):
    stiff_ref, inverses, u_ref, far, near, part_ref, *refs = refs
    if step > 0:
        far_lf, old_vw, *refs = refs
    if step < SUBSTEPS - 1:
        g_ref, send_ref, vw_ref, adv_ref, rhs, inv_ref, sem = refs
    else:
        g_ref, send_ref, vw_ref, rhs, inv_ref, sem = refs
        adv_ref = None
    fetch = pltpu.make_async_copy(inverses.at[step], inv_ref, sem)
    fetch.start()
    own = lax.axis_index("gy")
    odd = lax.rem(lax.axis_index("gx"), 2) > 0
    stiff = stiff_ref[0]

    for r in range(0, CY, CHUNK):
        rows = slice(r, r + CHUNK)
        plus = [2.0 * courant[0] * jnp.maximum(u_ref[0, x, rows, :], 0.0) for x in range(2)]
        minus = [2.0 * courant[0] * jnp.minimum(u_ref[0, x, rows, :], 0.0) for x in range(2)]
        if step > 0:
            v, w = old_vw[0, rows, :], old_vw[1, rows, :]
        for c in range(3):
            away = [far[c, x, rows, :] for x in range(2)]
            if step > 0:
                for x in range(2):
                    line = 2 * c + x
                    away[x] = away[x] - v * far_lf[0, line : line + 1, :] - w * far_lf[1, line : line + 1, :]
            close = [near[c, x, rows, :] for x in range(2)]
            low = [jnp.where(odd, close[x], away[x]) for x in range(2)]
            high = [jnp.where(odd, away[x], close[x]) for x in range(2)]
            along = low + [u_ref[c, 0, rows, :], u_ref[c, 1, rows, :]] + high
            for x in range(2):
                b2, b1, a1, a2 = along[x], along[x + 1], along[x + 3], along[x + 4]
                adv = plus[x] * (0.25 * b2 - b1) + minus[x] * (a1 - 0.25 * a2)
                column = (2 * c + x) * LANES
                rhs[rows, column : column + LANES] = part_ref[c, x, rows, :] - new_weight[step] * adv
                if adv_ref is not None:
                    adv_ref[c, x, rows, :] = adv

    fetch.wait()
    inverse = inv_ref[...]
    first_flag = jnp.where(own > 0, 1.0, 0.0)
    last_flag = jnp.where(own < 7, 1.0, 0.0)
    coupling = -implicit_share[step] * stiff
    vw_ref[0] = jnp.broadcast_to(inverse[:, 0:1] * (coupling * first_flag), (CY, LANES))
    vw_ref[1] = jnp.broadcast_to(inverse[:, CY - 1 : CY] * (coupling * last_flag), (CY, LANES))
    for pair in range(3):
        solved = jnp.dot(
            inverse,
            rhs[:, pair * 256 : pair * 256 + 256],
            precision=lax.Precision.HIGHEST,
            preferred_element_type=jnp.float32,
        )
        g_ref[pair, 0] = solved[:, :LANES]
        g_ref[pair, 1] = solved[:, LANES:]
    for t, row in enumerate(ENDS):
        tile = jnp.concatenate(
            [g_ref[c, x, row : row + 1, :] for c in range(3) for x in range(2)]
            + [vw_ref[0, row : row + 1, :], vw_ref[1, row : row + 1, :]],
            axis=0,
        )
        for dest in range(8):
            send_ref[dest, t] = tile


def correct_kernel(step, got, g_ref, vw_ref, *refs):
    if step < SUBSTEPS - 1:
        u_ref, ends_ref, lf_ref, heads, tails = refs
    else:
        out_ref, heads, tails, u_ref, sems = refs
        ends_ref = None
    own = lax.axis_index("gy")
    shape = (8, LANES)

    def tip(block, t, which):
        return jnp.broadcast_to(got[block, t, 6 + which : 7 + which, :], shape)

    zero = jnp.zeros(shape, jnp.float32)
    for edge in (0, 1, 10, 11):
        heads[edge] = zero
        tails[edge] = zero
    prev_q, prev_last = zero, zero
    fronts, backs, front_qs, back_qs = [], [], [], []
    for block in range(8):
        head_v, tail_v, head_w, tail_w = tip(block, 0, 0), tip(block, 3, 0), tip(block, 0, 1), tip(block, 3, 1)
        pivot = 1.0 / (1.0 - head_v * prev_q)
        front = (got[block, 0] - head_v * prev_last) * pivot
        back = got[block, 3] - tail_v * prev_last + tail_v * prev_q * front
        front_q = head_w * pivot
        back_q = tail_w + tail_v * prev_q * front_q
        fronts.append(front)
        backs.append(back)
        front_qs.append(front_q)
        back_qs.append(back_q)
        prev_q, prev_last = back_q, back
    after = zero
    for block in range(7, -1, -1):
        head = fronts[block] - front_qs[block] * after
        heads[block + 2] = head
        tails[block + 2] = backs[block] - back_qs[block] * after
        after = head

    lower = tails[own + 1]
    upper = heads[own + 3]
    for c in range(3):
        for x in range(2):
            line = 2 * c + x
            low = lower[line : line + 1, :]
            high = upper[line : line + 1, :]
            u_ref[c, x] = g_ref[c, x] - vw_ref[0] * low - vw_ref[1] * high
        if ends_ref is None:
            pltpu.make_async_copy(u_ref.at[c], out_ref.at[c], sems.at[c]).start()
    if ends_ref is None:
        for c in range(3):
            pltpu.make_async_copy(u_ref.at[c], out_ref.at[c], sems.at[c]).wait()
    if ends_ref is not None:
        lf_ref[0] = lower
        lf_ref[1] = upper
        before = jnp.maximum(own - 1, 0)
        behind = jnp.minimum(own + 1, 7)
        row = got[before, 2]
        row = row - jnp.broadcast_to(got[before, 2, 6:7, :], shape) * tails[own]
        row = row - jnp.broadcast_to(got[before, 2, 7:8, :], shape) * heads[own + 2]
        ends_ref[0] = jnp.where(own > 0, row, zero)
        ends_ref[1] = lower
        ends_ref[2] = upper
        row = got[behind, 1]
        row = row - jnp.broadcast_to(got[behind, 1, 6:7, :], shape) * tails[own + 2]
        row = row - jnp.broadcast_to(got[behind, 1, 7:8, :], shape) * heads[own + 4]
        ends_ref[3] = jnp.where(own < 7, row, zero)


def f32(*shape):
    return pltpu.VMEM(shape, jnp.float32)


def call(kernel, arrays, outs, scratch, flops, scalars=(), large=(), out_hbm=False):
    return pl.pallas_call(
        kernel,
        out_shape=outs,
        in_specs=[SMEM] * len(scalars) + [HBM] * len(large) + [VMEM] * len(arrays),
        out_specs=[HBM if out_hbm else VMEM] * len(outs),
        scratch_shapes=scratch,
        cost_estimate=pl.CostEstimate(flops=flops, bytes_accessed=4 << 20, transcendentals=0),
        compiler_params=pltpu.CompilerParams(vmem_limit_bytes=16 << 20),
    )(
        *scalars,
        *[pltpu.with_memory_space_constraint(a, pltpu.HBM) for a in large],
        *[pltpu.with_memory_space_constraint(a, pltpu.VMEM) for a in arrays],
    )


def exchange(send):
    tiles = lax.all_to_all(send.reshape(8, 32, LANES), "gy", split_axis=0, concat_axis=0)
    return tiles.reshape(8, 4, 8, LANES)


def scratch(*shape):
    return pltpu.VMEM(shape, jnp.float32)


def body(velocity, stiffness, block_inverse):
    gx = lax.axis_size("gx")
    field = f32(3, 2, CY, LANES)
    tiles = f32(8, 4, 8, LANES)
    across = swaps(gx, 1, True)
    inside = swaps(gx, 0, True)
    for step in range(SUBSTEPS):
        last = step == SUBSTEPS - 1
        if step == 0:
            far = lax.ppermute(velocity, "gx", across)
            edge = [scratch(3, 2, 8, LANES)] * 2 + [pltpu.SemaphoreType.DMA((3,))]
            current, send = call(pack_kernel, [], [field, tiles], edge, 10**6, large=[velocity])
            got = exchange(send)
            near = lax.ppermute(current, "gx", inside)
            own_args = [current, got]
            more_args = []
        else:
            far_lf = lax.ppermute(lf, "gx", across)
            near = lax.ppermute(current, "gx", inside)
            own_args = [current, ends, share, adv]
            more_args = [far_lf, vw]
        pad = [scratch(3, 2, CY + 16, LANES)]
        own = functools.partial(own_kernel, step)
        kept = [] if last else [field]
        part, *shares = call(own, own_args, [field] + kept, pad, 10**8, [stiffness])
        outs = [field, tiles, f32(2, CY, LANES)] + [field] * (0 if last else 1)
        arrays = [current, far, near, part] + more_args
        planes = functools.partial(planes_kernel, step)
        rhs = [scratch(CY, 6 * LANES), scratch(CY, CY), pltpu.SemaphoreType.DMA]
        g, send, vw, *advs = call(planes, arrays, outs, rhs, 10**9, [stiffness], [block_inverse])
        got = exchange(send)
        if not last:
            share, adv = shares[0], advs[0]
            far = lax.ppermute(g, "gx", across)
        correct = functools.partial(correct_kernel, step)
        edge = [scratch(12, 8, LANES)] * 2
        if last:
            outs = [jax.ShapeDtypeStruct((3, 2, CY, LANES), jnp.float32)]
            edge = edge + [scratch(3, 2, CY, LANES), pltpu.SemaphoreType.DMA((3,))]
            return call(correct, [got, g, vw], outs, edge, 10**8, out_hbm=True)[0]
        outs = [field, f32(4, 8, LANES), f32(2, 8, LANES)]
        current, ends, lf = call(correct, [got, g, vw], outs, edge, 10**8)


def solution(mesh):
    return jax.shard_map(
        body,
        mesh=mesh,
        in_specs=(P(None, "gx", "gy", None), P("gy"), P(None, "gy", None)),
        out_specs=P(None, "gx", "gy", None),
        check_vma=False,
    )
```

profile of v0, /device:TPU:8, one launch (start us, length us, event | category | flops | bytes accessed | tf_op | source)
XLA Modules:
  0.0 99.0 jit_solution(10389527061264870286)
XLA Ops:
  0.0 12.6 %collective-permute-start = (f32[3,2,192,128]{3,2,1,0:T(8,128)}, f32[3,2,192,128]{3,2,1,0:T(8,128)S(1)}, u32[]{:S(2)}, u32[]{:S(2)}) collective-permute-start(f32[3,2,192,128]{3,2,1,0:T(8,128)} %velocity.1), channel_id=1, source_target_pairs={{8,16},{16,8},{24,32},{32,24},{40,48},{48,40},{56,64},{64,56},{72,... | collective-permute-start | bytes 1769480 | tf_op jit(solution)/shard_map/ppermute | solution.py:286
  12.6 1.8 %shard_map.37 = (f32[3,2,192,128]{3,2,1,0:T(8,128)S(1)}, f32[8,4,8,128]{3,2,1,0:T(8,128)}) custom-call(f32[3,2,192,128]{3,2,1,0:T(8,128)} %velocity.1), custom_call_target="tpu_custom_call" | custom-call | flops 1000000 | bytes 4194304 | tf_op jit(solution)/shard_map/pallas_call | solution.py:253
  14.4 1.9 %collective-permute-start.1 = (f32[3,2,192,128]{3,2,1,0:T(8,128)S(1)}, f32[3,2,192,128]{3,2,1,0:T(8,128)S(1)}, u32[]{:S(2)}, u32[]{:S(2)}) collective-permute-start(f32[3,2,192,128]{3,2,1,0:T(8,128)S(1)} %get-tuple-element.28.refs_1_.refs_2_), channel_id=1, source_target_pairs={{0,8},{8,0},{16,24},{24,16},{32,40},{40,32},{48,56},{56,48},{64,72... | collective-permute-start | bytes 1769480 | tf_op jit(solution)/shard_map/ppermute | solution.py:290
  16.3 7.6 %all-to-all-start = ((f32[8,32,128]{2,1,0:T(8,128)}), f32[8,32,128]{2,1,0:T(8,128)S(1)}, u32[]{:S(2)}, u32[]{:S(2)}) async-start(f32[8,32,128]{2,1,0:T(8,128)} %bitcast), calls=%async_computation | async-start | bytes 262144 | tf_op jit(solution)/shard_map/all_to_all | solution.py:269
  24.6 7.5 %all-to-all-done = f32[8,32,128]{2,1,0:T(8,128)S(1)} async-done(((f32[8,32,128]{2,1,0:T(8,128)}), f32[8,32,128]{2,1,0:T(8,128)S(1)}, u32[]{:S(2)}, u32[]{:S(2)}) %all-to-all-start) | async-done | bytes 131104 | tf_op jit(solution)/shard_map/all_to_all | solution.py:269
  32.1 0.7 shard_map.38
  32.8 0.0 collective-permute-done.refs_3_
  32.8 0.0 collective-permute-done.1.refs_4_
  32.8 0.0 copy-start
  32.8 0.8 copy-done
  33.6 0.0 copy-start.1
  33.6 1.1 %copy-done.1 = f32[3,2,192,128]{3,2,1,0:T(8,128)S(1)} copy-done((f32[3,2,192,128]{3,2,1,0:T(8,128)S(1)}, f32[3,2,192,128]{3,2,1,0:T(8,128)}, u32[]{:S(2)}) %copy-start.1) | copy-done | bytes 589848
  34.7 2.2 %shard_map.39 = (f32[3,2,192,128]{3,2,1,0:T(8,128)S(1)}, f32[8,4,8,128]{3,2,1,0:T(8,128)}, f32[2,192,128]{2,1,0:T(8,128)S(1)}, f32[3,2,192,128]{3,2,1,0:T(8,128)S(1)}) custom-call(f32[1]{0:T(128)S(6)} %copy.4.refs_0_, f32[3,192,192]{2,1,0:T(8,128)} %refs_1_.5, f32[3,2,192,128]{3,2,1,0:T(8,128)S(1)} %get-tuple-element.28.refs_1_.refs_2_, ...), custom_call_target="tpu_custom_call" | custom-call | flops 1000000000 | bytes 4194304 | tf_op jit(solution)/shard_map/pallas_call | solution.py:253
  36.9 4.8 %all-to-all-start.1 = ((f32[8,32,128]{2,1,0:T(8,128)}), f32[8,32,128]{2,1,0:T(8,128)S(1)}, u32[]{:S(2)}, u32[]{:S(2)}) async-start(f32[8,32,128]{2,1,0:T(8,128)} %bitcast.2), calls=%async_computation.1 | async-start | bytes 262144 | tf_op jit(solution)/shard_map/all_to_all | solution.py:269
  41.8 1.9 %collective-permute-start.2 = (f32[3,2,192,128]{3,2,1,0:T(8,128)S(1)}, f32[3,2,192,128]{3,2,1,0:T(8,128)S(1)}, u32[]{:S(2)}, u32[]{:S(2)}) collective-permute-start(f32[3,2,192,128]{3,2,1,0:T(8,128)S(1)} %get-tuple-element.32.g_ref), channel_id=1, source_target_pairs={{8,16},{16,8},{24,32},{32,24},{40,48},{48,40},{56,64},{64,56},{72,... | collective-permute-start | bytes 1769480 | tf_op jit(solution)/shard_map/ppermute | solution.py:310
  43.7 5.7 %all-to-all-done.1 = f32[8,32,128]{2,1,0:T(8,128)S(1)} async-done(((f32[8,32,128]{2,1,0:T(8,128)}), f32[8,32,128]{2,1,0:T(8,128)S(1)}, u32[]{:S(2)}, u32[]{:S(2)}) %all-to-all-start.1) | async-done | bytes 131104 | tf_op jit(solution)/shard_map/all_to_all | solution.py:269
  49.4 0.2 shard_map.40
  49.7 1.9 %collective-permute-start.3 = (f32[3,2,192,128]{3,2,1,0:T(8,128)S(1)}, f32[3,2,192,128]{3,2,1,0:T(8,128)S(1)}, u32[]{:S(2)}, u32[]{:S(2)}) collective-permute-start(f32[3,2,192,128]{3,2,1,0:T(8,128)S(1)} %get-tuple-element.34.refs_1_.refs_2_), channel_id=1, source_target_pairs={{0,8},{8,0},{16,24},{24,16},{32,40},{40,32},{48,56},{56,48},{64,72... | collective-permute-start | bytes 1769480 | tf_op jit(solution)/shard_map/ppermute | solution.py:295
  51.6 2.8 %collective-permute-start.4 = (f32[2,8,128]{2,1,0:T(8,128)S(1)}, f32[2,8,128]{2,1,0:T(8,128)S(1)}, u32[]{:S(2)}, u32[]{:S(2)}) collective-permute-start(f32[2,8,128]{2,1,0:T(8,128)S(1)} %get-tuple-element.39), channel_id=1, source_target_pairs={{8,16},{16,8},{24,32},{32,24},{40,48},{48,40},{56,64},{64,56},{72,... | collective-permute-start | bytes 24584 | tf_op jit(solution)/shard_map/ppermute | solution.py:294
  54.4 0.8 shard_map.41
  55.2 4.7 %collective-permute-done.4.refs_6_ = f32[2,8,128]{2,1,0:T(8,128)S(1)} collective-permute-done((f32[2,8,128]{2,1,0:T(8,128)S(1)}, f32[2,8,128]{2,1,0:T(8,128)S(1)}, u32[]{:S(2)}, u32[]{:S(2)}) %collective-permute-start.4) | collective-permute-done | bytes 8224 | tf_op jit(solution)/shard_map/ppermute | solution.py:294
  59.9 0.0 collective-permute-done.2.refs_3_
  59.9 0.0 collective-permute-done.3.refs_4_
  59.9 2.2 %shard_map.42 = (f32[3,2,192,128]{3,2,1,0:T(8,128)S(1)}, f32[8,4,8,128]{3,2,1,0:T(8,128)}, f32[2,192,128]{2,1,0:T(8,128)S(1)}, f32[3,2,192,128]{3,2,1,0:T(8,128)S(1)}) custom-call(f32[1]{0:T(128)S(6)} %copy.4.refs_0_, f32[3,192,192]{2,1,0:T(8,128)} %refs_1_.5, f32[3,2,192,128]{3,2,1,0:T(8,128)S(1)} %get-tuple-element.34.refs_1_.refs_2_, ...), custom_call_target="tpu_custom_call" | custom-call | flops 1000000000 | bytes 4194304 | tf_op jit(solution)/shard_map/pallas_call | solution.py:253
  62.1 4.7 %all-to-all-start.2 = ((f32[8,32,128]{2,1,0:T(8,128)}), f32[8,32,128]{2,1,0:T(8,128)S(1)}, u32[]{:S(2)}, u32[]{:S(2)}) async-start(f32[8,32,128]{2,1,0:T(8,128)} %bitcast.4), calls=%async_computation.2 | async-start | bytes 262144 | tf_op jit(solution)/shard_map/all_to_all | solution.py:269
  66.9 3.2 %collective-permute-start.5 = (f32[3,2,192,128]{3,2,1,0:T(8,128)S(1)}, f32[3,2,192,128]{3,2,1,0:T(8,128)S(1)}, u32[]{:S(2)}, u32[]{:S(2)}) collective-permute-start(f32[3,2,192,128]{3,2,1,0:T(8,128)S(1)} %get-tuple-element.41.g_ref), channel_id=1, source_target_pairs={{8,16},{16,8},{24,32},{32,24},{40,48},{48,40},{56,64},{64,56},{72,... | collective-permute-start | bytes 1769480 | tf_op jit(solution)/shard_map/ppermute | solution.py:310
  70.0 4.5 %all-to-all-done.2 = f32[8,32,128]{2,1,0:T(8,128)S(1)} async-done(((f32[8,32,128]{2,1,0:T(8,128)}), f32[8,32,128]{2,1,0:T(8,128)S(1)}, u32[]{:S(2)}, u32[]{:S(2)}) %all-to-all-start.2) | async-done | bytes 131104 | tf_op jit(solution)/shard_map/all_to_all | solution.py:269
  74.5 0.2 shard_map.43
  74.7 1.9 %collective-permute-start.6 = (f32[3,2,192,128]{3,2,1,0:T(8,128)S(1)}, f32[3,2,192,128]{3,2,1,0:T(8,128)S(1)}, u32[]{:S(2)}, u32[]{:S(2)}) collective-permute-start(f32[3,2,192,128]{3,2,1,0:T(8,128)S(1)} %get-tuple-element.43.refs_1_.refs_2_), channel_id=1, source_target_pairs={{0,8},{8,0},{16,24},{24,16},{32,40},{40,32},{48,56},{56,48},{64,72... | collective-permute-start | bytes 1769480 | tf_op jit(solution)/shard_map/ppermute | solution.py:295
  76.7 2.3 %collective-permute-start.7 = (f32[2,8,128]{2,1,0:T(8,128)S(1)}, f32[2,8,128]{2,1,0:T(8,128)S(1)}, u32[]{:S(2)}, u32[]{:S(2)}) collective-permute-start(f32[2,8,128]{2,1,0:T(8,128)S(1)} %get-tuple-element.47), channel_id=1, source_target_pairs={{8,16},{16,8},{24,32},{32,24},{40,48},{48,40},{56,64},{64,56},{72,... | collective-permute-start | bytes 24584 | tf_op jit(solution)/shard_map/ppermute | solution.py:294
  79.0 0.8 shard_map.44.refs_5_
  79.7 5.2 %collective-permute-done.7.refs_6_ = f32[2,8,128]{2,1,0:T(8,128)S(1)} collective-permute-done((f32[2,8,128]{2,1,0:T(8,128)S(1)}, f32[2,8,128]{2,1,0:T(8,128)S(1)}, u32[]{:S(2)}, u32[]{:S(2)}) %collective-permute-start.7) | collective-permute-done | bytes 8224 | tf_op jit(solution)/shard_map/ppermute | solution.py:294
  85.0 0.0 collective-permute-done.5.refs_3_
  85.0 0.0 collective-permute-done.6.refs_4_
  85.0 1.6 %shard_map.45 = (f32[3,2,192,128]{3,2,1,0:T(8,128)S(1)}, f32[8,4,8,128]{3,2,1,0:T(8,128)S(1)}, f32[2,192,128]{2,1,0:T(8,128)S(1)}) custom-call(f32[1]{0:T(128)S(6)} %copy.4.refs_0_, f32[3,192,192]{2,1,0:T(8,128)} %refs_1_.5, f32[3,2,192,128]{3,2,1,0:T(8,128)S(1)} %get-tuple-element.43.refs_1_.refs_2_, f32[3,2,192,128]{3,2,1,0:T(8,128)S(1)} %collective-permute-done.5.refs_3_, ...), custom_call_target="tpu_custom_call" | custom-call | flops 1000000000 | bytes 4194304 | tf_op jit(solution)/shard_map/pallas_call | solution.py:253
  86.6 11.4 %all_to_all.20 = f32[8,32,128]{2,1,0:T(8,128)S(1)} all-to-all(f32[8,32,128]{2,1,0:T(8,128)S(1)} %bitcast.12), channel_id=1, replica_groups=mesh['gx'=64,'gy'=8] {'gy'}, dimensions={0} | all-to-all | bytes 262144 | tf_op jit(solution)/shard_map/all_to_all | solution.py:269
  98.0 1.0 shard_map.46
Async XLA Ops:
  0.0 32.8 %collective-permute-start = (f32[3,2,192,128]{3,2,1,0:T(8,128)}, f32[3,2,192,128]{3,2,1,0:T(8,128)S(1)}, u32[]{:S(2)}, u32[]{:S(2)}) collective-permute-start(f32[3,2,192,128]{3,2,1,0:T(8,128)} %velocity.1), channel_id=1, source_target_pairs={{8,16},{16,8},{24,32},{32,24},{40,48},{48,40},{56,64},{64,56},{72,... | collective-permute-start | bytes 1769480 | tf_op jit(solution)/shard_map/ppermute | solution.py:286
  14.4 18.4 %collective-permute-start.1 = (f32[3,2,192,128]{3,2,1,0:T(8,128)S(1)}, f32[3,2,192,128]{3,2,1,0:T(8,128)S(1)}, u32[]{:S(2)}, u32[]{:S(2)}) collective-permute-start(f32[3,2,192,128]{3,2,1,0:T(8,128)S(1)} %get-tuple-element.28.refs_1_.refs_2_), channel_id=1, source_target_pairs={{0,8},{8,0},{16,24},{24,16},{32,40},{40,32},{48,56},{56,48},{64,72... | collective-permute-start | bytes 1769480 | tf_op jit(solution)/shard_map/ppermute | solution.py:290
  16.3 15.7 %all-to-all-start = ((f32[8,32,128]{2,1,0:T(8,128)}), f32[8,32,128]{2,1,0:T(8,128)S(1)}, u32[]{:S(2)}, u32[]{:S(2)}) async-start(f32[8,32,128]{2,1,0:T(8,128)} %bitcast), calls=%async_computation | async-start | bytes 262144 | tf_op jit(solution)/shard_map/all_to_all | solution.py:269
  32.8 0.8 copy-start
  33.6 1.1 %copy-start.1 = (f32[3,2,192,128]{3,2,1,0:T(8,128)S(1)}, f32[3,2,192,128]{3,2,1,0:T(8,128)}, u32[]{:S(2)}) copy-start(f32[3,2,192,128]{3,2,1,0:T(8,128)} %copy-done) | copy-start | bytes 1769476
  36.9 12.5 %all-to-all-start.1 = ((f32[8,32,128]{2,1,0:T(8,128)}), f32[8,32,128]{2,1,0:T(8,128)S(1)}, u32[]{:S(2)}, u32[]{:S(2)}) async-start(f32[8,32,128]{2,1,0:T(8,128)} %bitcast.2), calls=%async_computation.1 | async-start | bytes 262144 | tf_op jit(solution)/shard_map/all_to_all | solution.py:269
  41.8 18.1 %collective-permute-start.2 = (f32[3,2,192,128]{3,2,1,0:T(8,128)S(1)}, f32[3,2,192,128]{3,2,1,0:T(8,128)S(1)}, u32[]{:S(2)}, u32[]{:S(2)}) collective-permute-start(f32[3,2,192,128]{3,2,1,0:T(8,128)S(1)} %get-tuple-element.32.g_ref), channel_id=1, source_target_pairs={{8,16},{16,8},{24,32},{32,24},{40,48},{48,40},{56,64},{64,56},{72,... | collective-permute-start | bytes 1769480 | tf_op jit(solution)/shard_map/ppermute | solution.py:310
  49.7 10.2 %collective-permute-start.3 = (f32[3,2,192,128]{3,2,1,0:T(8,128)S(1)}, f32[3,2,192,128]{3,2,1,0:T(8,128)S(1)}, u32[]{:S(2)}, u32[]{:S(2)}) collective-permute-start(f32[3,2,192,128]{3,2,1,0:T(8,128)S(1)} %get-tuple-element.34.refs_1_.refs_2_), channel_id=1, source_target_pairs={{0,8},{8,0},{16,24},{24,16},{32,40},{40,32},{48,56},{56,48},{64,72... | collective-permute-start | bytes 1769480 | tf_op jit(solution)/shard_map/ppermute | solution.py:295
  51.6 8.3 %collective-permute-start.4 = (f32[2,8,128]{2,1,0:T(8,128)S(1)}, f32[2,8,128]{2,1,0:T(8,128)S(1)}, u32[]{:S(2)}, u32[]{:S(2)}) collective-permute-start(f32[2,8,128]{2,1,0:T(8,128)S(1)} %get-tuple-element.39), channel_id=1, source_target_pairs={{8,16},{16,8},{24,32},{32,24},{40,48},{48,40},{56,64},{64,56},{72,... | collective-permute-start | bytes 24584 | tf_op jit(solution)/shard_map/ppermute | solution.py:294
  62.1 12.4 %all-to-all-start.2 = ((f32[8,32,128]{2,1,0:T(8,128)}), f32[8,32,128]{2,1,0:T(8,128)S(1)}, u32[]{:S(2)}, u32[]{:S(2)}) async-start(f32[8,32,128]{2,1,0:T(8,128)} %bitcast.4), calls=%async_computation.2 | async-start | bytes 262144 | tf_op jit(solution)/shard_map/all_to_all | solution.py:269
  66.9 18.1 %collective-permute-start.5 = (f32[3,2,192,128]{3,2,1,0:T(8,128)S(1)}, f32[3,2,192,128]{3,2,1,0:T(8,128)S(1)}, u32[]{:S(2)}, u32[]{:S(2)}) collective-permute-start(f32[3,2,192,128]{3,2,1,0:T(8,128)S(1)} %get-tuple-element.41.g_ref), channel_id=1, source_target_pairs={{8,16},{16,8},{24,32},{32,24},{40,48},{48,40},{56,64},{64,56},{72,... | collective-permute-start | bytes 1769480 | tf_op jit(solution)/shard_map/ppermute | solution.py:310
  74.7 10.2 %collective-permute-start.6 = (f32[3,2,192,128]{3,2,1,0:T(8,128)S(1)}, f32[3,2,192,128]{3,2,1,0:T(8,128)S(1)}, u32[]{:S(2)}, u32[]{:S(2)}) collective-permute-start(f32[3,2,192,128]{3,2,1,0:T(8,128)S(1)} %get-tuple-element.43.refs_1_.refs_2_), channel_id=1, source_target_pairs={{0,8},{8,0},{16,24},{24,16},{32,40},{40,32},{48,56},{56,48},{64,72... | collective-permute-start | bytes 1769480 | tf_op jit(solution)/shard_map/ppermute | solution.py:295
  76.7 8.3 %collective-permute-start.7 = (f32[2,8,128]{2,1,0:T(8,128)S(1)}, f32[2,8,128]{2,1,0:T(8,128)S(1)}, u32[]{:S(2)}, u32[]{:S(2)}) collective-permute-start(f32[2,8,128]{2,1,0:T(8,128)S(1)} %get-tuple-element.47), channel_id=1, source_target_pairs={{8,16},{16,8},{24,32},{32,24},{40,48},{48,40},{56,64},{64,56},{72,... | collective-permute-start | bytes 24584 | tf_op jit(solution)/shard_map/ppermute | solution.py:294
where the time goes:
time: 99.8 us; the launch traced here: 99 us
  starting transfers between devices  45.7 us (46%)
  waiting for transfers between devices  27.6 us (28%)
  Pallas kernels  11.6 us (12%)
  blocking collectives  11.4 us (11%)
  local copies, waits for them, and re-layouts  1.87 us (2%)
    all_to_all x3, waiting for transfers between devices, exchange(): lax.all_to_all(send.reshape(8, 32, LANES), 'gy', split_axis=0, concat_axi...  17.7 us
    all_to_all x3, starting transfers between devices, exchange(): lax.all_to_all(send.reshape(8, 32, LANES), 'gy', split_axis=0, concat_axi...  17.1 us
    ppermute x1, starting transfers between devices, body(): far = lax.ppermute(velocity, 'gx', across)  12.6 us
    pallas_call x10, Pallas kernels, call(): pl.pallas_call(kernel, out_shape=outs, in_specs=[SMEM] * len(scalars) + [...  11.6 us
    all_to_all x1, blocking collectives, exchange(): lax.all_to_all(send.reshape(8, 32, LANES), 'gy', split_axis=0, concat_axi...  11.4 us
    ppermute x2, waiting for transfers between devices, body(): far_lf = lax.ppermute(lf, 'gx', across)  9.88 us
    ppermute x3, starting transfers between devices, body(): near = lax.ppermute(current, 'gx', inside)  5.76 us
    ppermute x2, starting transfers between devices, body(): far_lf = lax.ppermute(lf, 'gx', across)  5.12 us
  transfers between devices with their start and end apart: 11, of which 5 were waited for; matrix products, arithmetic and copies ran while one was open for 0% of the time, Pallas kernels for 5%

commit v1 on v0

--- a/solution.py
+++ b/solution.py
@@ -39,36 +39,24 @@
     return [(c, x) for c in range(3) for x in range(2)]
 
 
-def pack_kernel(velocity, u_ref, send_ref, top, bottom, sems):
+def pack_kernel(velocity, u_ref, rows_ref, sems):
     copies = [
-        pltpu.make_async_copy(velocity.at[:, :, pl.ds(0, 8), :], top, sems.at[0]),
-        pltpu.make_async_copy(velocity.at[:, :, pl.ds(CY - 8, 8), :], bottom, sems.at[1]),
+        pltpu.make_async_copy(velocity.at[:, :, pl.ds(0, 8), :], rows_ref.at[:, :, pl.ds(0, 8), :], sems.at[0]),
+        pltpu.make_async_copy(velocity.at[:, :, pl.ds(CY - 8, 8), :], rows_ref.at[:, :, pl.ds(8, 8), :], sems.at[1]),
         pltpu.make_async_copy(velocity, u_ref, sems.at[2]),
     ]
     for copy in copies:
         copy.start()
-    copies[0].wait()
-    copies[1].wait()
-    for t, (source, row) in enumerate(((top, 0), (top, 1), (bottom, 6), (bottom, 7))):
-        picked = [source[c, x, row : row + 1, :] for c, x in lines()]
-        tile = jnp.concatenate(picked + picked[:2], axis=0)
-        for dest in range(8):
-            send_ref[dest, t] = tile
-    copies[2].wait()
+    for copy in copies:
+        copy.wait()
 
 
 def own_kernel(step, *refs):
     if step == 0:
-        stiff_ref, u_ref, got, *refs = refs
-        old_ref = None
-        own = lax.axis_index("gy")
-        before = jnp.maximum(own - 1, 0)
-        behind = jnp.minimum(own + 1, 7)
-        ends = [jnp.where(own > 0, got[before, t], 0.0) for t in (2, 3)]
-        ends += [jnp.where(own < 7, got[behind, t], 0.0) for t in (0, 1)]
+        stiff_ref, u_ref, *refs = refs
+        ends_ref = old_ref = None
     else:
         stiff_ref, u_ref, ends_ref, old_share, old_ref, *refs = refs
-        ends = [ends_ref[t] for t in range(4)]
     if step < SUBSTEPS - 1:
         part_ref, share_ref, pad = refs
     else:
@@ -79,11 +67,15 @@
     for c in range(3):
         for x in range(2):
             pad[c, x, 8 : 8 + CY, :] = u_ref[c, x]
-            line = slice(2 * c + x, 2 * c + x + 1)
-            pad[c, x, 6:7, :] = ends[0][line]
-            pad[c, x, 7:8, :] = ends[1][line]
-            pad[c, x, 8 + CY : 9 + CY, :] = ends[2][line]
-            pad[c, x, 9 + CY : 10 + CY, :] = ends[3][line]
+            if step == 0:
+                pad[c, x, 0:8, :] = jnp.zeros((8, LANES), jnp.float32)
+                pad[c, x, 8 + CY : 16 + CY, :] = jnp.zeros((8, LANES), jnp.float32)
+            else:
+                line = 2 * c + x
+                pad[c, x, 6:7, :] = ends_ref[0, line : line + 1, :]
+                pad[c, x, 7:8, :] = ends_ref[1, line : line + 1, :]
+                pad[c, x, 8 + CY : 9 + CY, :] = ends_ref[2, line : line + 1, :]
+                pad[c, x, 9 + CY : 10 + CY, :] = ends_ref[3, line : line + 1, :]
 
     for r in range(0, CY, CHUNK):
         rows = slice(r, r + CHUNK)
@@ -117,6 +109,8 @@
     stiff_ref, inverses, u_ref, far, near, part_ref, *refs = refs
     if step > 0:
         far_lf, old_vw, *refs = refs
+    else:
+        pair_y, other_y, *refs = refs
     if step < SUBSTEPS - 1:
         g_ref, send_ref, vw_ref, adv_ref, rhs, inv_ref, sem = refs
     else:
@@ -152,6 +146,30 @@
                 if adv_ref is not None:
                     adv_ref[c, x, rows, :] = adv
 
+    if step == 0:
+        odd_y = lax.rem(own, 2) > 0
+        for c, x in lines():
+            low = jnp.where(odd_y, pair_y[c, x, 8:16, :], other_y[c, x, 8:16, :])
+            high = jnp.where(odd_y, other_y[c, x, 0:8, :], pair_y[c, x, 0:8, :])
+            y2, y1, w1, w2 = low[6:7], low[7:8], high[0:1], high[1:2]
+            for row, viscous, up, down in (
+                (0, y1, 0.25 * y2 - y1, None),
+                (1, None, 0.25 * y1, None),
+                (CY - 2, None, None, -0.25 * w1),
+                (CY - 1, w1, None, w1 - 0.25 * w2),
+            ):
+                speed = u_ref[1, x, row : row + 1, :]
+                if up is not None:
+                    adv = 2.0 * courant[1] * jnp.maximum(speed, 0.0) * up
+                else:
+                    adv = 2.0 * courant[1] * jnp.minimum(speed, 0.0) * down
+                adv_ref[c, x, row : row + 1, :] = adv_ref[c, x, row : row + 1, :] + adv
+                change = -new_weight[step] * adv
+                if viscous is not None:
+                    change = change + (implicit_share[step] * stiff) * viscous
+                column = slice((2 * c + x) * LANES, (2 * c + x + 1) * LANES)
+                rhs[row : row + 1, column] = rhs[row : row + 1, column] + change
+
     fetch.wait()
     inverse = inv_ref[...]
     first_flag = jnp.where(own > 0, 1.0, 0.0)
@@ -174,33 +192,42 @@
             + [vw_ref[0, row : row + 1, :], vw_ref[1, row : row + 1, :]],
             axis=0,
         )
-        for dest in range(8):
+        for dest in range(send_ref.shape[0]):
             send_ref[dest, t] = tile
 
 
 def correct_kernel(step, got, g_ref, vw_ref, *refs):
     if step < SUBSTEPS - 1:
-        u_ref, ends_ref, lf_ref, heads, tails = refs
+        u_ref, ends_ref, lf_ref, heads, tails, far_heads, far_tails = refs
+        first = jnp.where(lax.rem(lax.axis_index("gx"), 2) > 0, 0, 8)
+        sets = ((first, heads, tails), (8 - first, far_heads, far_tails))
     else:
         out_ref, heads, tails, u_ref, sems = refs
         ends_ref = None
+        first = 0
+        sets = ((first, heads, tails),)
     own = lax.axis_index("gy")
     shape = (8, LANES)
+    zero = jnp.zeros(shape, jnp.float32)
 
     def tip(block, t, which):
-        return jnp.broadcast_to(got[block, t, 6 + which : 7 + which, :], shape)
-
-    zero = jnp.zeros(shape, jnp.float32)
-    for edge in (0, 1, 10, 11):
-        heads[edge] = zero
-        tails[edge] = zero
-    prev_q, prev_last = zero, zero
+        return jnp.broadcast_to(got[first + block, t, 6 + which : 7 + which, :], shape)
+
+    for _, head_ref, tail_ref in sets:
+        for edge in (0, 1, 10, 11):
+            head_ref[edge] = zero
+            tail_ref[edge] = zero
+    prev_q = zero
+    prev_last = [zero for _ in sets]
     fronts, backs, front_qs, back_qs = [], [], [], []
     for block in range(8):
         head_v, tail_v, head_w, tail_w = tip(block, 0, 0), tip(block, 3, 0), tip(block, 0, 1), tip(block, 3, 1)
         pivot = 1.0 / (1.0 - head_v * prev_q)
-        front = (got[block, 0] - head_v * prev_last) * pivot
-        back = got[block, 3] - tail_v * prev_last + tail_v * prev_q * front
+        front = [(got[base + block, 0] - head_v * last) * pivot for (base, _, _), last in zip(sets, prev_last)]
+        back = [
+            got[base + block, 3] - tail_v * last + tail_v * prev_q * new
+            for (base, _, _), last, new in zip(sets, prev_last, front)
+        ]
         front_q = head_w * pivot
         back_q = tail_w + tail_v * prev_q * front_q
         fronts.append(front)
@@ -208,12 +235,12 @@
         front_qs.append(front_q)
         back_qs.append(back_q)
         prev_q, prev_last = back_q, back
-    after = zero
+    after = [zero for _ in sets]
     for block in range(7, -1, -1):
-        head = fronts[block] - front_qs[block] * after
-        heads[block + 2] = head
-        tails[block + 2] = backs[block] - back_qs[block] * after
-        after = head
+        for n, (_, head_ref, tail_ref) in enumerate(sets):
+            head_ref[block + 2] = fronts[block][n] - front_qs[block] * after[n]
+            tail_ref[block + 2] = backs[block][n] - back_qs[block] * after[n]
+        after = [fronts[block][n] - front_qs[block] * after[n] for n in range(len(sets))]
 
     lower = tails[own + 1]
     upper = heads[own + 3]
@@ -229,10 +256,10 @@
         for c in range(3):
             pltpu.make_async_copy(u_ref.at[c], out_ref.at[c], sems.at[c]).wait()
     if ends_ref is not None:
-        lf_ref[0] = lower
-        lf_ref[1] = upper
-        before = jnp.maximum(own - 1, 0)
-        behind = jnp.minimum(own + 1, 7)
+        lf_ref[0] = far_tails[own + 1]
+        lf_ref[1] = far_heads[own + 3]
+        before = first + jnp.maximum(own - 1, 0)
+        behind = first + jnp.minimum(own + 1, 7)
         row = got[before, 2]
         row = row - jnp.broadcast_to(got[before, 2, 6:7, :], shape) * tails[own]
         row = row - jnp.broadcast_to(got[before, 2, 7:8, :], shape) * heads[own + 2]
@@ -265,9 +292,15 @@
     )
 
 
-def exchange(send):
-    tiles = lax.all_to_all(send.reshape(8, 32, LANES), "gy", split_axis=0, concat_axis=0)
-    return tiles.reshape(8, 4, 8, LANES)
+def exchange(send, gx, gy):
+    count = send.shape[0]
+    send = send.reshape(count, 32, LANES)
+    if count == gy:
+        tiles = lax.all_to_all(send, "gy", split_axis=0, concat_axis=0)
+    else:
+        groups = [[((a + side) % gx) * gy + k for side in (0, 1) for k in range(gy)] for a in range(1, gx, 2)]
+        tiles = lax.all_to_all(send, ("gx", "gy"), split_axis=0, concat_axis=0, axis_index_groups=groups)
+    return tiles.reshape(count, 4, 8, LANES)
 
 
 def scratch(*shape):
@@ -276,35 +309,34 @@
 
 def body(velocity, stiffness, block_inverse):
     gx = lax.axis_size("gx")
+    gy = lax.axis_size("gy")
     field = f32(3, 2, CY, LANES)
-    tiles = f32(8, 4, 8, LANES)
     across = swaps(gx, 1, True)
     inside = swaps(gx, 0, True)
     for step in range(SUBSTEPS):
         last = step == SUBSTEPS - 1
         if step == 0:
             far = lax.ppermute(velocity, "gx", across)
-            edge = [scratch(3, 2, 8, LANES)] * 2 + [pltpu.SemaphoreType.DMA((3,))]
-            current, send = call(pack_kernel, [], [field, tiles], edge, 10**6, large=[velocity])
-            got = exchange(send)
-            near = lax.ppermute(current, "gx", inside)
-            own_args = [current, got]
-            more_args = []
+            outs = [field, f32(3, 2, 16, LANES)]
+            current, rows = call(pack_kernel, [], outs, [pltpu.SemaphoreType.DMA((3,))], 10**6, large=[velocity])
+            pair_y = lax.ppermute(rows, "gy", swaps(gy, 0, False))
+            other_y = lax.ppermute(rows, "gy", swaps(gy, 1, False))
+            own_args = [current]
+            more_args = [pair_y, other_y]
         else:
-            far_lf = lax.ppermute(lf, "gx", across)
-            near = lax.ppermute(current, "gx", inside)
             own_args = [current, ends, share, adv]
             more_args = [far_lf, vw]
+        near = lax.ppermute(current, "gx", inside)
         pad = [scratch(3, 2, CY + 16, LANES)]
         own = functools.partial(own_kernel, step)
-        kept = [] if last else [field]
-        part, *shares = call(own, own_args, [field] + kept, pad, 10**8, [stiffness])
+        part, *shares = call(own, own_args, [field] * (1 if last else 2), pad, 10**8, [stiffness])
+        tiles = f32(8 if last else 16, 4, 8, LANES)
         outs = [field, tiles, f32(2, CY, LANES)] + [field] * (0 if last else 1)
         arrays = [current, far, near, part] + more_args
         planes = functools.partial(planes_kernel, step)
         rhs = [scratch(CY, 6 * LANES), scratch(CY, CY), pltpu.SemaphoreType.DMA]
         g, send, vw, *advs = call(planes, arrays, outs, rhs, 10**9, [stiffness], [block_inverse])
-        got = exchange(send)
+        got = exchange(send, gx, gy)
         if not last:
             share, adv = shares[0], advs[0]
             far = lax.ppermute(g, "gx", across)
@@ -315,7 +347,7 @@
             edge = edge + [scratch(3, 2, CY, LANES), pltpu.SemaphoreType.DMA((3,))]
             return call(correct, [got, g, vw], outs, edge, 10**8, out_hbm=True)[0]
         outs = [field, f32(4, 8, LANES), f32(2, 8, LANES)]
-        current, ends, lf = call(correct, [got, g, vw], outs, edge, 10**8)
+        current, ends, far_lf = call(correct, [got, g, vw], outs, edge * 2, 10**8)
 
 
 def solution(mesh):

time: 99.8 us -> 98.3 us (0.985)
  waiting for transfers between devices: 27.6 us -> 21.5 us
  starting transfers between devices: 45.7 us -> 49.8 us
  blocking collectives: 11.4 us -> 14.6 us
  local copies, waits for them, and re-layouts: 1.87 us -> 0 us
    ppermute x2, waiting for transfers between devices: 9.88 us -> 2.69 us  [the longest x1 2.69 us: body(): pair_y = lax.ppermute(rows, 'gy', swaps(gy, 0, False))]
    ppermute x2, waiting for transfers between devices: 0.01 us -> 5.67 us  [body(): far = lax.ppermute(g, 'gx', across)]
    all_to_all x3 -> x2, waiting for transfers between devices: 17.7 us -> 13.1 us  [exchange(): lax.all_to_all(send, ('gx', 'gy'), split_axis=0, concat_axis=0, axis_inde...]
    all_to_all x3 -> x2, starting transfers between devices: 17.1 us -> 21.7 us  [exchange(): lax.all_to_all(send, ('gx', 'gy'), split_axis=0, concat_axis=0, axis_inde...]
    all_to_all x1, blocking collectives: 11.4 us -> 14.6 us  [exchange(): tiles = lax.all_to_all(send, 'gy', split_axis=0, concat_axis=0)]
    unnamed x4 -> x0, local copies, waits for them, and re-layouts: 1.87 us -> none
  transfers between devices with their start and end apart: 11 -> 10, of which waited for: 5 -> 5; matrix products, arithmetic and copies ran while one was open for 0% -> 0% of each run, Pallas kernels for 5% -> 4%
where the time goes in v1:
time: 98.3 us; the launch traced here: 97.7 us
  starting transfers between devices  49.8 us (51%)
  waiting for transfers between devices  21.5 us (22%)
  blocking collectives  14.6 us (15%)
  Pallas kernels  11 us (11%)
    all_to_all x2, starting transfers between devices, exchange(): lax.all_to_all(send, ('gx', 'gy'), split_axis=0, concat_axis=0, axis_inde...  21.7 us
    all_to_all x1, blocking collectives, exchange(): tiles = lax.all_to_all(send, 'gy', split_axis=0, concat_axis=0)  14.6 us
    all_to_all x2, waiting for transfers between devices, exchange(): lax.all_to_all(send, ('gx', 'gy'), split_axis=0, concat_axis=0, axis_inde...  13.1 us
    ppermute x1, starting transfers between devices, body(): far = lax.ppermute(velocity, 'gx', across)  12.6 us
    pallas_call x10, Pallas kernels, call(): pl.pallas_call(kernel, out_shape=outs, in_specs=[SMEM] * len(scalars) + [...  11 us
    ppermute x3, starting transfers between devices, body(): near = lax.ppermute(current, 'gx', inside)  5.76 us
    ppermute x2, waiting for transfers between devices, body(): far = lax.ppermute(g, 'gx', across)  5.67 us
    ppermute x2, starting transfers between devices, body(): far = lax.ppermute(g, 'gx', across)  4.35 us
  transfers between devices with their start and end apart: 10, of which 5 were waited for; matrix products, arithmetic and copies ran while one was open for 0% of the time, Pallas kernels for 4%

profile of v1, /device:TPU:8, one launch (start us, length us, event | category | flops | bytes accessed | tf_op | source)
XLA Modules:
  0.0 97.7 jit_solution(2706776648352970896)
XLA Ops:
  0.0 12.6 %collective-permute-start = (f32[3,2,192,128]{3,2,1,0:T(8,128)}, f32[3,2,192,128]{3,2,1,0:T(8,128)S(1)}, u32[]{:S(2)}, u32[]{:S(2)}) collective-permute-start(f32[3,2,192,128]{3,2,1,0:T(8,128)} %velocity.1), channel_id=1, source_target_pairs={{8,16},{16,8},{24,32},{32,24},{40,48},{48,40},{56,64},{64,56},{72,... | collective-permute-start | bytes 1769480 | tf_op jit(solution)/shard_map/ppermute | solution.py:319
  12.6 1.2 %shard_map.37 = (f32[3,2,192,128]{3,2,1,0:T(8,128)S(1)}, f32[3,2,16,128]{3,2,1,0:T(8,128)S(1)}) custom-call(f32[3,2,192,128]{3,2,1,0:T(8,128)} %velocity.1), custom_call_target="tpu_custom_call" | custom-call | flops 1000000 | bytes 4194304 | tf_op jit(solution)/shard_map/pallas_call | solution.py:280
  13.8 1.9 %collective-permute-start.1 = (f32[3,2,192,128]{3,2,1,0:T(8,128)S(1)}, f32[3,2,192,128]{3,2,1,0:T(8,128)S(1)}, u32[]{:S(2)}, u32[]{:S(2)}) collective-permute-start(f32[3,2,192,128]{3,2,1,0:T(8,128)S(1)} %get-tuple-element.28.refs_1_.refs_2_), channel_id=1, source_target_pairs={{0,8},{8,0},{16,24},{24,16},{32,40},{40,32},{48,56},{56,48},{64,72... | collective-permute-start | bytes 1769480 | tf_op jit(solution)/shard_map/ppermute | solution.py:329
  15.7 3.5 %collective-permute-start.3 = (f32[3,2,16,128]{3,2,1,0:T(8,128)S(1)}, f32[3,2,16,128]{3,2,1,0:T(8,128)S(1)}, u32[]{:S(2)}, u32[]{:S(2)}) collective-permute-start(f32[3,2,16,128]{3,2,1,0:T(8,128)S(1)} %get-tuple-element.30), channel_id=1, source_target_pairs={{1,2},{2,1},{3,4},{4,3},{5,6},{6,5},{9,10},{10,9},{11,12},{12,11},... | collective-permute-start | bytes 147464 | tf_op jit(solution)/shard_map/ppermute | solution.py:323
  19.2 1.9 %collective-permute-start.2 = (f32[3,2,16,128]{3,2,1,0:T(8,128)S(1)}, f32[3,2,16,128]{3,2,1,0:T(8,128)S(1)}, u32[]{:S(2)}, u32[]{:S(2)}) collective-permute-start(f32[3,2,16,128]{3,2,1,0:T(8,128)S(1)} %get-tuple-element.30), channel_id=1, source_target_pairs={{0,1},{1,0},{2,3},{3,2},{4,5},{5,4},{6,7},{7,6},{8,9},{9,8},{10,11... | collective-permute-start | bytes 147464 | tf_op jit(solution)/shard_map/ppermute | solution.py:322
  21.8 0.7 shard_map.38
  22.5 0.0 collective-permute-done.3.refs_7_
  22.5 2.7 %collective-permute-done.2.refs_6_ = f32[3,2,16,128]{3,2,1,0:T(8,128)S(1)} collective-permute-done((f32[3,2,16,128]{3,2,1,0:T(8,128)S(1)}, f32[3,2,16,128]{3,2,1,0:T(8,128)S(1)}, u32[]{:S(2)}, u32[]{:S(2)}) %collective-permute-start.2) | collective-permute-done | bytes 49184 | tf_op jit(solution)/shard_map/ppermute | solution.py:322
  25.2 0.0 collective-permute-done.refs_3_
  25.2 0.0 collective-permute-done.1.refs_4_
  25.2 2.3 %shard_map.39 = (f32[3,2,192,128]{3,2,1,0:T(8,128)S(1)}, f32[16,4,8,128]{3,2,1,0:T(8,128)}, f32[2,192,128]{2,1,0:T(8,128)S(1)}, f32[3,2,192,128]{3,2,1,0:T(8,128)S(1)}) custom-call(f32[1]{0:T(128)S(6)} %copy.4.refs_0_, f32[3,192,192]{2,1,0:T(8,128)} %refs_1_.5, f32[3,2,192,128]{3,2,1,0:T(8,128)S(1)} %get-tuple-element.28.refs_1_.refs_2_, ...), custom_call_target="tpu_custom_call" | custom-call | flops 1000000000 | bytes 4194304 | tf_op jit(solution)/shard_map/pallas_call | solution.py:280
  27.5 10.5 %all-to-all-start = ((f32[16,32,128]{2,1,0:T(8,128)}), f32[16,32,128]{2,1,0:T(8,128)S(1)}, u32[]{:S(2)}, u32[]{:S(2)}) async-start(f32[16,32,128]{2,1,0:T(8,128)} %bitcast), calls=%async_computation | async-start | bytes 524288 | tf_op jit(solution)/shard_map/all_to_all | solution.py:302
  38.0 2.2 %collective-permute-start.4 = (f32[3,2,192,128]{3,2,1,0:T(8,128)S(1)}, f32[3,2,192,128]{3,2,1,0:T(8,128)S(1)}, u32[]{:S(2)}, u32[]{:S(2)}) collective-permute-start(f32[3,2,192,128]{3,2,1,0:T(8,128)S(1)} %get-tuple-element.32.g_ref), channel_id=1, source_target_pairs={{8,16},{16,8},{24,32},{32,24},{40,48},{48,40},{56,64},{64,56},{72,... | collective-permute-start | bytes 1769480 | tf_op jit(solution)/shard_map/ppermute | solution.py:342
  40.2 6.5 %all-to-all-done = f32[16,32,128]{2,1,0:T(8,128)S(1)} async-done(((f32[16,32,128]{2,1,0:T(8,128)}), f32[16,32,128]{2,1,0:T(8,128)S(1)}, u32[]{:S(2)}, u32[]{:S(2)}) %all-to-all-start) | async-done | bytes 262176 | tf_op jit(solution)/shard_map/all_to_all | solution.py:302
  46.7 0.2 shard_map.40
  46.9 1.9 %collective-permute-start.5 = (f32[3,2,192,128]{3,2,1,0:T(8,128)S(1)}, f32[3,2,192,128]{3,2,1,0:T(8,128)S(1)}, u32[]{:S(2)}, u32[]{:S(2)}) collective-permute-start(f32[3,2,192,128]{3,2,1,0:T(8,128)S(1)} %get-tuple-element.34.refs_1_.refs_2_), channel_id=1, source_target_pairs={{0,8},{8,0},{16,24},{24,16},{32,40},{40,32},{48,56},{56,48},{64,72... | collective-permute-start | bytes 1769480 | tf_op jit(solution)/shard_map/ppermute | solution.py:329
  48.9 0.8 shard_map.41
  49.7 2.8 %collective-permute-done.4.refs_3_ = f32[3,2,192,128]{3,2,1,0:T(8,128)S(1)} collective-permute-done((f32[3,2,192,128]{3,2,1,0:T(8,128)S(1)}, f32[3,2,192,128]{3,2,1,0:T(8,128)S(1)}, u32[]{:S(2)}, u32[]{:S(2)}) %collective-permute-start.4) | collective-permute-done | bytes 589856 | tf_op jit(solution)/shard_map/ppermute | solution.py:342
  52.5 0.0 collective-permute-done.5.refs_4_
  52.5 2.3 %shard_map.42 = (f32[3,2,192,128]{3,2,1,0:T(8,128)S(1)}, f32[16,4,8,128]{3,2,1,0:T(8,128)}, f32[2,192,128]{2,1,0:T(8,128)S(1)}, f32[3,2,192,128]{3,2,1,0:T(8,128)S(1)}) custom-call(f32[1]{0:T(128)S(6)} %copy.4.refs_0_, f32[3,192,192]{2,1,0:T(8,128)} %refs_1_.5, f32[3,2,192,128]{3,2,1,0:T(8,128)S(1)} %get-tuple-element.34.refs_1_.refs_2_, ...), custom_call_target="tpu_custom_call" | custom-call | flops 1000000000 | bytes 4194304 | tf_op jit(solution)/shard_map/pallas_call | solution.py:280
  54.8 11.2 %all-to-all-start.1 = ((f32[16,32,128]{2,1,0:T(8,128)}), f32[16,32,128]{2,1,0:T(8,128)S(1)}, u32[]{:S(2)}, u32[]{:S(2)}) async-start(f32[16,32,128]{2,1,0:T(8,128)} %bitcast.2), calls=%async_computation.1 | async-start | bytes 524288 | tf_op jit(solution)/shard_map/all_to_all | solution.py:302
  66.0 2.2 %collective-permute-start.6 = (f32[3,2,192,128]{3,2,1,0:T(8,128)S(1)}, f32[3,2,192,128]{3,2,1,0:T(8,128)S(1)}, u32[]{:S(2)}, u32[]{:S(2)}) collective-permute-start(f32[3,2,192,128]{3,2,1,0:T(8,128)S(1)} %get-tuple-element.41.g_ref), channel_id=1, source_target_pairs={{8,16},{16,8},{24,32},{32,24},{40,48},{48,40},{56,64},{64,56},{72,... | collective-permute-start | bytes 1769480 | tf_op jit(solution)/shard_map/ppermute | solution.py:342
  68.2 6.5 %all-to-all-done.1 = f32[16,32,128]{2,1,0:T(8,128)S(1)} async-done(((f32[16,32,128]{2,1,0:T(8,128)}), f32[16,32,128]{2,1,0:T(8,128)S(1)}, u32[]{:S(2)}, u32[]{:S(2)}) %all-to-all-start.1) | async-done | bytes 262176 | tf_op jit(solution)/shard_map/all_to_all | solution.py:302
  74.7 0.2 shard_map.43
  74.9 1.9 %collective-permute-start.7 = (f32[3,2,192,128]{3,2,1,0:T(8,128)S(1)}, f32[3,2,192,128]{3,2,1,0:T(8,128)S(1)}, u32[]{:S(2)}, u32[]{:S(2)}) collective-permute-start(f32[3,2,192,128]{3,2,1,0:T(8,128)S(1)} %get-tuple-element.43.refs_1_.refs_2_), channel_id=1, source_target_pairs={{0,8},{8,0},{16,24},{24,16},{32,40},{40,32},{48,56},{56,48},{64,72... | collective-permute-start | bytes 1769480 | tf_op jit(solution)/shard_map/ppermute | solution.py:329
  76.9 0.8 shard_map.44.refs_5_
  77.6 2.8 %collective-permute-done.6.refs_3_ = f32[3,2,192,128]{3,2,1,0:T(8,128)S(1)} collective-permute-done((f32[3,2,192,128]{3,2,1,0:T(8,128)S(1)}, f32[3,2,192,128]{3,2,1,0:T(8,128)S(1)}, u32[]{:S(2)}, u32[]{:S(2)}) %collective-permute-start.6) | collective-permute-done | bytes 589856 | tf_op jit(solution)/shard_map/ppermute | solution.py:342
  80.5 0.0 collective-permute-done.7.refs_4_
  80.5 1.6 %shard_map.45 = (f32[3,2,192,128]{3,2,1,0:T(8,128)S(1)}, f32[8,4,8,128]{3,2,1,0:T(8,128)S(1)}, f32[2,192,128]{2,1,0:T(8,128)S(1)}) custom-call(f32[1]{0:T(128)S(6)} %copy.4.refs_0_, f32[3,192,192]{2,1,0:T(8,128)} %refs_1_.5, f32[3,2,192,128]{3,2,1,0:T(8,128)S(1)} %get-tuple-element.43.refs_1_.refs_2_, f32[3,2,192,128]{3,2,1,0:T(8,128)S(1)} %collective-permute-done.6.refs_3_, ...), custom_call_target="tpu_custom_call" | custom-call | flops 1000000000 | bytes 4194304 | tf_op jit(solution)/shard_map/pallas_call | solution.py:280
  82.1 14.6 %all_to_all.15 = f32[8,32,128]{2,1,0:T(8,128)S(1)} all-to-all(f32[8,32,128]{2,1,0:T(8,128)S(1)} %bitcast.9), channel_id=1, replica_groups=mesh['gx'=64,'gy'=8] {'gy'}, dimensions={0} | all-to-all | bytes 262144 | tf_op jit(solution)/shard_map/all_to_all | solution.py:299
  96.7 1.0 %shard_map.46 = f32[3,2,192,128]{3,2,1,0:T(8,128)} custom-call(f32[8,4,8,128]{3,2,1,0:T(8,128)S(1)} %bitcast.8, f32[3,2,192,128]{3,2,1,0:T(8,128)S(1)} %get-tuple-element.49.g_ref, f32[2,192,128]{2,1,0:T(8,128)S(1)} %get-tuple-element.50.vw_ref), custom_call_target="tpu_custom_call" | custom-call | flops 100000000 | bytes 4194304 | tf_op jit(solution)/shard_map/pallas_call | solution.py:280
Async XLA Ops:
  0.0 25.2 %collective-permute-start = (f32[3,2,192,128]{3,2,1,0:T(8,128)}, f32[3,2,192,128]{3,2,1,0:T(8,128)S(1)}, u32[]{:S(2)}, u32[]{:S(2)}) collective-permute-start(f32[3,2,192,128]{3,2,1,0:T(8,128)} %velocity.1), channel_id=1, source_target_pairs={{8,16},{16,8},{24,32},{32,24},{40,48},{48,40},{56,64},{64,56},{72,... | collective-permute-start | bytes 1769480 | tf_op jit(solution)/shard_map/ppermute | solution.py:319
  13.8 11.4 %collective-permute-start.1 = (f32[3,2,192,128]{3,2,1,0:T(8,128)S(1)}, f32[3,2,192,128]{3,2,1,0:T(8,128)S(1)}, u32[]{:S(2)}, u32[]{:S(2)}) collective-permute-start(f32[3,2,192,128]{3,2,1,0:T(8,128)S(1)} %get-tuple-element.28.refs_1_.refs_2_), channel_id=1, source_target_pairs={{0,8},{8,0},{16,24},{24,16},{32,40},{40,32},{48,56},{56,48},{64,72... | collective-permute-start | bytes 1769480 | tf_op jit(solution)/shard_map/ppermute | solution.py:329
  15.7 6.8 %collective-permute-start.3 = (f32[3,2,16,128]{3,2,1,0:T(8,128)S(1)}, f32[3,2,16,128]{3,2,1,0:T(8,128)S(1)}, u32[]{:S(2)}, u32[]{:S(2)}) collective-permute-start(f32[3,2,16,128]{3,2,1,0:T(8,128)S(1)} %get-tuple-element.30), channel_id=1, source_target_pairs={{1,2},{2,1},{3,4},{4,3},{5,6},{6,5},{9,10},{10,9},{11,12},{12,11},... | collective-permute-start | bytes 147464 | tf_op jit(solution)/shard_map/ppermute | solution.py:323
  19.2 6.0 %collective-permute-start.2 = (f32[3,2,16,128]{3,2,1,0:T(8,128)S(1)}, f32[3,2,16,128]{3,2,1,0:T(8,128)S(1)}, u32[]{:S(2)}, u32[]{:S(2)}) collective-permute-start(f32[3,2,16,128]{3,2,1,0:T(8,128)S(1)} %get-tuple-element.30), channel_id=1, source_target_pairs={{0,1},{1,0},{2,3},{3,2},{4,5},{5,4},{6,7},{7,6},{8,9},{9,8},{10,11... | collective-permute-start | bytes 147464 | tf_op jit(solution)/shard_map/ppermute | solution.py:322
  27.5 19.2 %all-to-all-start = ((f32[16,32,128]{2,1,0:T(8,128)}), f32[16,32,128]{2,1,0:T(8,128)S(1)}, u32[]{:S(2)}, u32[]{:S(2)}) async-start(f32[16,32,128]{2,1,0:T(8,128)} %bitcast), calls=%async_computation | async-start | bytes 524288 | tf_op jit(solution)/shard_map/all_to_all | solution.py:302
  38.0 14.5 %collective-permute-start.4 = (f32[3,2,192,128]{3,2,1,0:T(8,128)S(1)}, f32[3,2,192,128]{3,2,1,0:T(8,128)S(1)}, u32[]{:S(2)}, u32[]{:S(2)}) collective-permute-start(f32[3,2,192,128]{3,2,1,0:T(8,128)S(1)} %get-tuple-element.32.g_ref), channel_id=1, source_target_pairs={{8,16},{16,8},{24,32},{32,24},{40,48},{48,40},{56,64},{64,56},{72,... | collective-permute-start | bytes 1769480 | tf_op jit(solution)/shard_map/ppermute | solution.py:342
  46.9 5.6 %collective-permute-start.5 = (f32[3,2,192,128]{3,2,1,0:T(8,128)S(1)}, f32[3,2,192,128]{3,2,1,0:T(8,128)S(1)}, u32[]{:S(2)}, u32[]{:S(2)}) collective-permute-start(f32[3,2,192,128]{3,2,1,0:T(8,128)S(1)} %get-tuple-element.34.refs_1_.refs_2_), channel_id=1, source_target_pairs={{0,8},{8,0},{16,24},{24,16},{32,40},{40,32},{48,56},{56,48},{64,72... | collective-permute-start | bytes 1769480 | tf_op jit(solution)/shard_map/ppermute | solution.py:329
  54.8 19.9 %all-to-all-start.1 = ((f32[16,32,128]{2,1,0:T(8,128)}), f32[16,32,128]{2,1,0:T(8,128)S(1)}, u32[]{:S(2)}, u32[]{:S(2)}) async-start(f32[16,32,128]{2,1,0:T(8,128)} %bitcast.2), calls=%async_computation.1 | async-start | bytes 524288 | tf_op jit(solution)/shard_map/all_to_all | solution.py:302
  66.0 14.5 %collective-permute-start.6 = (f32[3,2,192,128]{3,2,1,0:T(8,128)S(1)}, f32[3,2,192,128]{3,2,1,0:T(8,128)S(1)}, u32[]{:S(2)}, u32[]{:S(2)}) collective-permute-start(f32[3,2,192,128]{3,2,1,0:T(8,128)S(1)} %get-tuple-element.41.g_ref), channel_id=1, source_target_pairs={{8,16},{16,8},{24,32},{32,24},{40,48},{48,40},{56,64},{64,56},{72,... | collective-permute-start | bytes 1769480 | tf_op jit(solution)/shard_map/ppermute | solution.py:342
  74.9 5.6 %collective-permute-start.7 = (f32[3,2,192,128]{3,2,1,0:T(8,128)S(1)}, f32[3,2,192,128]{3,2,1,0:T(8,128)S(1)}, u32[]{:S(2)}, u32[]{:S(2)}) collective-permute-start(f32[3,2,192,128]{3,2,1,0:T(8,128)S(1)} %get-tuple-element.43.refs_1_.refs_2_), channel_id=1, source_target_pairs={{0,8},{8,0},{16,24},{24,16},{32,40},{40,32},{48,56},{56,48},{64,72... | collective-permute-start | bytes 1769480 | tf_op jit(solution)/shard_map/ppermute | solution.py:329

commit v2 on v1

--- a/solution.py
+++ b/solution.py
@@ -198,36 +198,27 @@
 
 def correct_kernel(step, got, g_ref, vw_ref, *refs):
     if step < SUBSTEPS - 1:
-        u_ref, ends_ref, lf_ref, heads, tails, far_heads, far_tails = refs
-        first = jnp.where(lax.rem(lax.axis_index("gx"), 2) > 0, 0, 8)
-        sets = ((first, heads, tails), (8 - first, far_heads, far_tails))
+        u_ref, ends_ref, lf_ref, heads, tails = refs
     else:
         out_ref, heads, tails, u_ref, sems = refs
         ends_ref = None
-        first = 0
-        sets = ((first, heads, tails),)
     own = lax.axis_index("gy")
     shape = (8, LANES)
     zero = jnp.zeros(shape, jnp.float32)
 
     def tip(block, t, which):
-        return jnp.broadcast_to(got[first + block, t, 6 + which : 7 + which, :], shape)
-
-    for _, head_ref, tail_ref in sets:
-        for edge in (0, 1, 10, 11):
-            head_ref[edge] = zero
-            tail_ref[edge] = zero
-    prev_q = zero
-    prev_last = [zero for _ in sets]
+        return jnp.broadcast_to(got[block, t, 6 + which : 7 + which, :], shape)
+
+    for edge in (0, 1, 10, 11):
+        heads[edge] = zero
+        tails[edge] = zero
+    prev_q, prev_last = zero, zero
     fronts, backs, front_qs, back_qs = [], [], [], []
     for block in range(8):
         head_v, tail_v, head_w, tail_w = tip(block, 0, 0), tip(block, 3, 0), tip(block, 0, 1), tip(block, 3, 1)
         pivot = 1.0 / (1.0 - head_v * prev_q)
-        front = [(got[base + block, 0] - head_v * last) * pivot for (base, _, _), last in zip(sets, prev_last)]
-        back = [
-            got[base + block, 3] - tail_v * last + tail_v * prev_q * new
-            for (base, _, _), last, new in zip(sets, prev_last, front)
-        ]
+        front = (got[block, 0] - head_v * prev_last) * pivot
+        back = got[block, 3] - tail_v * prev_last + tail_v * prev_q * front
         front_q = head_w * pivot
         back_q = tail_w + tail_v * prev_q * front_q
         fronts.append(front)
@@ -235,12 +226,12 @@
         front_qs.append(front_q)
         back_qs.append(back_q)
         prev_q, prev_last = back_q, back
-    after = [zero for _ in sets]
+    after = zero
     for block in range(7, -1, -1):
-        for n, (_, head_ref, tail_ref) in enumerate(sets):
-            head_ref[block + 2] = fronts[block][n] - front_qs[block] * after[n]
-            tail_ref[block + 2] = backs[block][n] - back_qs[block] * after[n]
-        after = [fronts[block][n] - front_qs[block] * after[n] for n in range(len(sets))]
+        head = fronts[block] - front_qs[block] * after
+        heads[block + 2] = head
+        tails[block + 2] = backs[block] - back_qs[block] * after
+        after = head
 
     lower = tails[own + 1]
     upper = heads[own + 3]
@@ -256,10 +247,10 @@
         for c in range(3):
             pltpu.make_async_copy(u_ref.at[c], out_ref.at[c], sems.at[c]).wait()
     if ends_ref is not None:
-        lf_ref[0] = far_tails[own + 1]
-        lf_ref[1] = far_heads[own + 3]
-        before = first + jnp.maximum(own - 1, 0)
-        behind = first + jnp.minimum(own + 1, 7)
+        lf_ref[0] = lower
+        lf_ref[1] = upper
+        before = jnp.maximum(own - 1, 0)
+        behind = jnp.minimum(own + 1, 7)
         row = got[before, 2]
         row = row - jnp.broadcast_to(got[before, 2, 6:7, :], shape) * tails[own]
         row = row - jnp.broadcast_to(got[before, 2, 7:8, :], shape) * heads[own + 2]
@@ -292,15 +283,9 @@
     )
 
 
-def exchange(send, gx, gy):
-    count = send.shape[0]
-    send = send.reshape(count, 32, LANES)
-    if count == gy:
-        tiles = lax.all_to_all(send, "gy", split_axis=0, concat_axis=0)
-    else:
-        groups = [[((a + side) % gx) * gy + k for side in (0, 1) for k in range(gy)] for a in range(1, gx, 2)]
-        tiles = lax.all_to_all(send, ("gx", "gy"), split_axis=0, concat_axis=0, axis_index_groups=groups)
-    return tiles.reshape(count, 4, 8, LANES)
+def exchange(send):
+    tiles = lax.all_to_all(send.reshape(8, 32, LANES), "gy", split_axis=0, concat_axis=0)
+    return tiles.reshape(8, 4, 8, LANES)
 
 
 def scratch(*shape):
@@ -324,19 +309,20 @@
             own_args = [current]
             more_args = [pair_y, other_y]
         else:
+            far_lf = lax.ppermute(lf, "gx", across)
             own_args = [current, ends, share, adv]
             more_args = [far_lf, vw]
         near = lax.ppermute(current, "gx", inside)
         pad = [scratch(3, 2, CY + 16, LANES)]
         own = functools.partial(own_kernel, step)
         part, *shares = call(own, own_args, [field] * (1 if last else 2), pad, 10**8, [stiffness])
-        tiles = f32(8 if last else 16, 4, 8, LANES)
+        tiles = f32(8, 4, 8, LANES)
         outs = [field, tiles, f32(2, CY, LANES)] + [field] * (0 if last else 1)
         arrays = [current, far, near, part] + more_args
         planes = functools.partial(planes_kernel, step)
         rhs = [scratch(CY, 6 * LANES), scratch(CY, CY), pltpu.SemaphoreType.DMA]
         g, send, vw, *advs = call(planes, arrays, outs, rhs, 10**9, [stiffness], [block_inverse])
-        got = exchange(send, gx, gy)
+        got = exchange(send)
         if not last:
             share, adv = shares[0], advs[0]
             far = lax.ppermute(g, "gx", across)
@@ -347,7 +333,7 @@
             edge = edge + [scratch(3, 2, CY, LANES), pltpu.SemaphoreType.DMA((3,))]
             return call(correct, [got, g, vw], outs, edge, 10**8, out_hbm=True)[0]
         outs = [field, f32(4, 8, LANES), f32(2, 8, LANES)]
-        current, ends, far_lf = call(correct, [got, g, vw], outs, edge * 2, 10**8)
+        current, ends, lf = call(correct, [got, g, vw], outs, edge, 10**8)
 
 
 def solution(mesh):

time: 98.3 us -> 91.8 us (0.934)
  blocking collectives: 14.6 us -> 11.4 us
  starting transfers between devices: 49.8 us -> 47.5 us
  waiting for transfers between devices: 21.5 us -> 20.4 us
    all_to_all x2, starting transfers between devices: 21.7 us -> 11.3 us  [exchange(): lax.all_to_all(send.reshape(8, 32, LANES), 'gy', split_axis=0, concat_axi...]
    ppermute x0 -> x2, waiting for transfers between devices: none -> 8.56 us  [body(): far_lf = lax.ppermute(lf, 'gx', across)]
    ppermute x0 -> x2, starting transfers between devices: none -> 6.44 us  [body(): far_lf = lax.ppermute(lf, 'gx', across)]
    ppermute x2, waiting for transfers between devices: 5.67 us -> 0.01 us  [body(): far = lax.ppermute(g, 'gx', across)]
    all_to_all x2, waiting for transfers between devices: 13.1 us -> 9.18 us  [exchange(): lax.all_to_all(send.reshape(8, 32, LANES), 'gy', split_axis=0, concat_axi...]
    all_to_all x1, blocking collectives: 14.6 us -> 11.4 us  [exchange(): lax.all_to_all(send.reshape(8, 32, LANES), 'gy', split_axis=0, concat_axi...]
    ppermute x2, starting transfers between devices: 4.35 us -> 6.07 us  [body(): far = lax.ppermute(g, 'gx', across)]
  transfers between devices with their start and end apart: 10 -> 12, of which waited for: 5 -> 5; matrix products, arithmetic and copies ran while one was open for 0% -> 0% of each run, Pallas kernels for 4% -> 4%
where the time goes in v2:
time: 91.8 us; the launch traced here: 91.1 us
  starting transfers between devices  47.5 us (52%)
  waiting for transfers between devices  20.4 us (22%)
  blocking collectives  11.4 us (12%)
  Pallas kernels  10.9 us (12%)
    ppermute x1, starting transfers between devices, body(): far = lax.ppermute(velocity, 'gx', across)  12.6 us
    all_to_all x1, blocking collectives, exchange(): lax.all_to_all(send.reshape(8, 32, LANES), 'gy', split_axis=0, concat_axi...  11.4 us
    all_to_all x2, starting transfers between devices, exchange(): lax.all_to_all(send.reshape(8, 32, LANES), 'gy', split_axis=0, concat_axi...  11.3 us
    pallas_call x10, Pallas kernels, call(): pl.pallas_call(kernel, out_shape=outs, in_specs=[SMEM] * len(scalars) + [...  10.9 us
    all_to_all x2, waiting for transfers between devices, exchange(): lax.all_to_all(send.reshape(8, 32, LANES), 'gy', split_axis=0, concat_axi...  9.18 us
    ppermute x2, waiting for transfers between devices, body(): far_lf = lax.ppermute(lf, 'gx', across)  8.56 us
    ppermute x2, starting transfers between devices, body(): far_lf = lax.ppermute(lf, 'gx', across)  6.44 us
    ppermute x2, starting transfers between devices, body(): far = lax.ppermute(g, 'gx', across)  6.07 us
  transfers between devices with their start and end apart: 12, of which 5 were waited for; matrix products, arithmetic and copies ran while one was open for 0% of the time, Pallas kernels for 4%

profile of v2, /device:TPU:8, one launch (start us, length us, event | category | flops | bytes accessed | tf_op | source)
XLA Modules:
  0.0 91.1 jit_solution(15136088228504840021)
XLA Ops:
  0.0 12.6 %collective-permute-start = (f32[3,2,192,128]{3,2,1,0:T(8,128)}, f32[3,2,192,128]{3,2,1,0:T(8,128)S(1)}, u32[]{:S(2)}, u32[]{:S(2)}) collective-permute-start(f32[3,2,192,128]{3,2,1,0:T(8,128)} %velocity.1), channel_id=1, source_target_pairs={{8,16},{16,8},{24,32},{32,24},{40,48},{48,40},{56,64},{64,56},{72,... | collective-permute-start | bytes 1769480 | tf_op jit(solution)/shard_map/ppermute | solution.py:304
  12.6 1.2 %shard_map.37 = (f32[3,2,192,128]{3,2,1,0:T(8,128)S(1)}, f32[3,2,16,128]{3,2,1,0:T(8,128)S(1)}) custom-call(f32[3,2,192,128]{3,2,1,0:T(8,128)} %velocity.1), custom_call_target="tpu_custom_call" | custom-call | flops 1000000 | bytes 4194304 | tf_op jit(solution)/shard_map/pallas_call | solution.py:271
  13.8 1.9 %collective-permute-start.1 = (f32[3,2,192,128]{3,2,1,0:T(8,128)S(1)}, f32[3,2,192,128]{3,2,1,0:T(8,128)S(1)}, u32[]{:S(2)}, u32[]{:S(2)}) collective-permute-start(f32[3,2,192,128]{3,2,1,0:T(8,128)S(1)} %get-tuple-element.28.refs_1_.refs_2_), channel_id=1, source_target_pairs={{0,8},{8,0},{16,24},{24,16},{32,40},{40,32},{48,56},{56,48},{64,72... | collective-permute-start | bytes 1769480 | tf_op jit(solution)/shard_map/ppermute | solution.py:315
  15.7 3.5 %collective-permute-start.3 = (f32[3,2,16,128]{3,2,1,0:T(8,128)S(1)}, f32[3,2,16,128]{3,2,1,0:T(8,128)S(1)}, u32[]{:S(2)}, u32[]{:S(2)}) collective-permute-start(f32[3,2,16,128]{3,2,1,0:T(8,128)S(1)} %get-tuple-element.30), channel_id=1, source_target_pairs={{1,2},{2,1},{3,4},{4,3},{5,6},{6,5},{9,10},{10,9},{11,12},{12,11},... | collective-permute-start | bytes 147464 | tf_op jit(solution)/shard_map/ppermute | solution.py:308
  19.2 1.9 %collective-permute-start.2 = (f32[3,2,16,128]{3,2,1,0:T(8,128)S(1)}, f32[3,2,16,128]{3,2,1,0:T(8,128)S(1)}, u32[]{:S(2)}, u32[]{:S(2)}) collective-permute-start(f32[3,2,16,128]{3,2,1,0:T(8,128)S(1)} %get-tuple-element.30), channel_id=1, source_target_pairs={{0,1},{1,0},{2,3},{3,2},{4,5},{5,4},{6,7},{7,6},{8,9},{9,8},{10,11... | collective-permute-start | bytes 147464 | tf_op jit(solution)/shard_map/ppermute | solution.py:307
  21.8 0.7 shard_map.38
  22.5 0.0 collective-permute-done.3.refs_7_
  22.5 2.7 %collective-permute-done.2.refs_6_ = f32[3,2,16,128]{3,2,1,0:T(8,128)S(1)} collective-permute-done((f32[3,2,16,128]{3,2,1,0:T(8,128)S(1)}, f32[3,2,16,128]{3,2,1,0:T(8,128)S(1)}, u32[]{:S(2)}, u32[]{:S(2)}) %collective-permute-start.2) | collective-permute-done | bytes 49184 | tf_op jit(solution)/shard_map/ppermute | solution.py:307
  25.2 0.0 collective-permute-done.refs_3_
  25.2 0.0 collective-permute-done.1.refs_4_
  25.2 2.2 %shard_map.39 = (f32[3,2,192,128]{3,2,1,0:T(8,128)S(1)}, f32[8,4,8,128]{3,2,1,0:T(8,128)}, f32[2,192,128]{2,1,0:T(8,128)S(1)}, f32[3,2,192,128]{3,2,1,0:T(8,128)S(1)}) custom-call(f32[1]{0:T(128)S(6)} %copy.4.refs_0_, f32[3,192,192]{2,1,0:T(8,128)} %refs_1_.5, f32[3,2,192,128]{3,2,1,0:T(8,128)S(1)} %get-tuple-element.28.refs_1_.refs_2_, ...), custom_call_target="tpu_custom_call" | custom-call | flops 1000000000 | bytes 4194304 | tf_op jit(solution)/shard_map/pallas_call | solution.py:271
  27.4 6.5 %all-to-all-start = ((f32[8,32,128]{2,1,0:T(8,128)}), f32[8,32,128]{2,1,0:T(8,128)S(1)}, u32[]{:S(2)}, u32[]{:S(2)}) async-start(f32[8,32,128]{2,1,0:T(8,128)} %bitcast), calls=%async_computation | async-start | bytes 262144 | tf_op jit(solution)/shard_map/all_to_all | solution.py:287
  34.0 2.6 %collective-permute-start.4 = (f32[3,2,192,128]{3,2,1,0:T(8,128)S(1)}, f32[3,2,192,128]{3,2,1,0:T(8,128)S(1)}, u32[]{:S(2)}, u32[]{:S(2)}) collective-permute-start(f32[3,2,192,128]{3,2,1,0:T(8,128)S(1)} %get-tuple-element.32.g_ref), channel_id=1, source_target_pairs={{8,16},{16,8},{24,32},{32,24},{40,48},{48,40},{56,64},{64,56},{72,... | collective-permute-start | bytes 1769480 | tf_op jit(solution)/shard_map/ppermute | solution.py:328
  36.5 5.0 %all-to-all-done = f32[8,32,128]{2,1,0:T(8,128)S(1)} async-done(((f32[8,32,128]{2,1,0:T(8,128)}), f32[8,32,128]{2,1,0:T(8,128)S(1)}, u32[]{:S(2)}, u32[]{:S(2)}) %all-to-all-start) | async-done | bytes 131104 | tf_op jit(solution)/shard_map/all_to_all | solution.py:287
  41.6 0.2 shard_map.40
  41.8 1.9 %collective-permute-start.5 = (f32[3,2,192,128]{3,2,1,0:T(8,128)S(1)}, f32[3,2,192,128]{3,2,1,0:T(8,128)S(1)}, u32[]{:S(2)}, u32[]{:S(2)}) collective-permute-start(f32[3,2,192,128]{3,2,1,0:T(8,128)S(1)} %get-tuple-element.34.refs_1_.refs_2_), channel_id=1, source_target_pairs={{0,8},{8,0},{16,24},{24,16},{32,40},{40,32},{48,56},{56,48},{64,72... | collective-permute-start | bytes 1769480 | tf_op jit(solution)/shard_map/ppermute | solution.py:315
  43.7 3.8 %collective-permute-start.6 = (f32[2,8,128]{2,1,0:T(8,128)S(1)}, f32[2,8,128]{2,1,0:T(8,128)S(1)}, u32[]{:S(2)}, u32[]{:S(2)}) collective-permute-start(f32[2,8,128]{2,1,0:T(8,128)S(1)} %get-tuple-element.39), channel_id=1, source_target_pairs={{8,16},{16,8},{24,32},{32,24},{40,48},{48,40},{56,64},{64,56},{72,... | collective-permute-start | bytes 24584 | tf_op jit(solution)/shard_map/ppermute | solution.py:312
  47.5 0.8 shard_map.41
  48.3 3.7 %collective-permute-done.6.refs_6_ = f32[2,8,128]{2,1,0:T(8,128)S(1)} collective-permute-done((f32[2,8,128]{2,1,0:T(8,128)S(1)}, f32[2,8,128]{2,1,0:T(8,128)S(1)}, u32[]{:S(2)}, u32[]{:S(2)}) %collective-permute-start.6) | collective-permute-done | bytes 8224 | tf_op jit(solution)/shard_map/ppermute | solution.py:312
  52.0 0.0 collective-permute-done.4.refs_3_
  52.0 0.0 collective-permute-done.5.refs_4_
  52.0 2.2 %shard_map.42 = (f32[3,2,192,128]{3,2,1,0:T(8,128)S(1)}, f32[8,4,8,128]{3,2,1,0:T(8,128)}, f32[2,192,128]{2,1,0:T(8,128)S(1)}, f32[3,2,192,128]{3,2,1,0:T(8,128)S(1)}) custom-call(f32[1]{0:T(128)S(6)} %copy.4.refs_0_, f32[3,192,192]{2,1,0:T(8,128)} %refs_1_.5, f32[3,2,192,128]{3,2,1,0:T(8,128)S(1)} %get-tuple-element.34.refs_1_.refs_2_, ...), custom_call_target="tpu_custom_call" | custom-call | flops 1000000000 | bytes 4194304 | tf_op jit(solution)/shard_map/pallas_call | solution.py:271
  54.3 4.7 %all-to-all-start.1 = ((f32[8,32,128]{2,1,0:T(8,128)}), f32[8,32,128]{2,1,0:T(8,128)S(1)}, u32[]{:S(2)}, u32[]{:S(2)}) async-start(f32[8,32,128]{2,1,0:T(8,128)} %bitcast.2), calls=%async_computation.1 | async-start | bytes 262144 | tf_op jit(solution)/shard_map/all_to_all | solution.py:287
  59.0 3.5 %collective-permute-start.7 = (f32[3,2,192,128]{3,2,1,0:T(8,128)S(1)}, f32[3,2,192,128]{3,2,1,0:T(8,128)S(1)}, u32[]{:S(2)}, u32[]{:S(2)}) collective-permute-start(f32[3,2,192,128]{3,2,1,0:T(8,128)S(1)} %get-tuple-element.41.g_ref), channel_id=1, source_target_pairs={{8,16},{16,8},{24,32},{32,24},{40,48},{48,40},{56,64},{64,56},{72,... | collective-permute-start | bytes 1769480 | tf_op jit(solution)/shard_map/ppermute | solution.py:328
  62.5 4.1 %all-to-all-done.1 = f32[8,32,128]{2,1,0:T(8,128)S(1)} async-done(((f32[8,32,128]{2,1,0:T(8,128)}), f32[8,32,128]{2,1,0:T(8,128)S(1)}, u32[]{:S(2)}, u32[]{:S(2)}) %all-to-all-start.1) | async-done | bytes 131104 | tf_op jit(solution)/shard_map/all_to_all | solution.py:287
  66.7 0.2 shard_map.43
  66.9 1.9 %collective-permute-start.8 = (f32[3,2,192,128]{3,2,1,0:T(8,128)S(1)}, f32[3,2,192,128]{3,2,1,0:T(8,128)S(1)}, u32[]{:S(2)}, u32[]{:S(2)}) collective-permute-start(f32[3,2,192,128]{3,2,1,0:T(8,128)S(1)} %get-tuple-element.43.refs_1_.refs_2_), channel_id=1, source_target_pairs={{0,8},{8,0},{16,24},{24,16},{32,40},{40,32},{48,56},{56,48},{64,72... | collective-permute-start | bytes 1769480 | tf_op jit(solution)/shard_map/ppermute | solution.py:315
  68.8 2.6 %collective-permute-start.9 = (f32[2,8,128]{2,1,0:T(8,128)S(1)}, f32[2,8,128]{2,1,0:T(8,128)S(1)}, u32[]{:S(2)}, u32[]{:S(2)}) collective-permute-start(f32[2,8,128]{2,1,0:T(8,128)S(1)} %get-tuple-element.47), channel_id=1, source_target_pairs={{8,16},{16,8},{24,32},{32,24},{40,48},{48,40},{56,64},{64,56},{72,... | collective-permute-start | bytes 24584 | tf_op jit(solution)/shard_map/ppermute | solution.py:312
  71.5 0.8 shard_map.44.refs_5_
  72.3 4.9 %collective-permute-done.9.refs_6_ = f32[2,8,128]{2,1,0:T(8,128)S(1)} collective-permute-done((f32[2,8,128]{2,1,0:T(8,128)S(1)}, f32[2,8,128]{2,1,0:T(8,128)S(1)}, u32[]{:S(2)}, u32[]{:S(2)}) %collective-permute-start.9) | collective-permute-done | bytes 8224 | tf_op jit(solution)/shard_map/ppermute | solution.py:312
  77.1 0.0 collective-permute-done.7.refs_3_
  77.1 0.0 collective-permute-done.8.refs_4_
  77.1 1.6 %shard_map.45 = (f32[3,2,192,128]{3,2,1,0:T(8,128)S(1)}, f32[8,4,8,128]{3,2,1,0:T(8,128)S(1)}, f32[2,192,128]{2,1,0:T(8,128)S(1)}) custom-call(f32[1]{0:T(128)S(6)} %copy.4.refs_0_, f32[3,192,192]{2,1,0:T(8,128)} %refs_1_.5, f32[3,2,192,128]{3,2,1,0:T(8,128)S(1)} %get-tuple-element.43.refs_1_.refs_2_, f32[3,2,192,128]{3,2,1,0:T(8,128)S(1)} %collective-permute-done.7.refs_3_, ...), custom_call_target="tpu_custom_call" | custom-call | flops 1000000000 | bytes 4194304 | tf_op jit(solution)/shard_map/pallas_call | solution.py:271
  78.7 11.4 %all_to_all.15 = f32[8,32,128]{2,1,0:T(8,128)S(1)} all-to-all(f32[8,32,128]{2,1,0:T(8,128)S(1)} %bitcast.9), channel_id=1, replica_groups=mesh['gx'=64,'gy'=8] {'gy'}, dimensions={0} | all-to-all | bytes 262144 | tf_op jit(solution)/shard_map/all_to_all | solution.py:287
  90.2 1.0 %shard_map.46 = f32[3,2,192,128]{3,2,1,0:T(8,128)} custom-call(f32[8,4,8,128]{3,2,1,0:T(8,128)S(1)} %bitcast.8, f32[3,2,192,128]{3,2,1,0:T(8,128)S(1)} %get-tuple-element.49.g_ref, f32[2,192,128]{2,1,0:T(8,128)S(1)} %get-tuple-element.50.vw_ref), custom_call_target="tpu_custom_call" | custom-call | flops 100000000 | bytes 4194304 | tf_op jit(solution)/shard_map/pallas_call | solution.py:271
Async XLA Ops:
  0.0 25.2 %collective-permute-start = (f32[3,2,192,128]{3,2,1,0:T(8,128)}, f32[3,2,192,128]{3,2,1,0:T(8,128)S(1)}, u32[]{:S(2)}, u32[]{:S(2)}) collective-permute-start(f32[3,2,192,128]{3,2,1,0:T(8,128)} %velocity.1), channel_id=1, source_target_pairs={{8,16},{16,8},{24,32},{32,24},{40,48},{48,40},{56,64},{64,56},{72,... | collective-permute-start | bytes 1769480 | tf_op jit(solution)/shard_map/ppermute | solution.py:304
  13.8 11.4 %collective-permute-start.1 = (f32[3,2,192,128]{3,2,1,0:T(8,128)S(1)}, f32[3,2,192,128]{3,2,1,0:T(8,128)S(1)}, u32[]{:S(2)}, u32[]{:S(2)}) collective-permute-start(f32[3,2,192,128]{3,2,1,0:T(8,128)S(1)} %get-tuple-element.28.refs_1_.refs_2_), channel_id=1, source_target_pairs={{0,8},{8,0},{16,24},{24,16},{32,40},{40,32},{48,56},{56,48},{64,72... | collective-permute-start | bytes 1769480 | tf_op jit(solution)/shard_map/ppermute | solution.py:315
  15.7 6.8 %collective-permute-start.3 = (f32[3,2,16,128]{3,2,1,0:T(8,128)S(1)}, f32[3,2,16,128]{3,2,1,0:T(8,128)S(1)}, u32[]{:S(2)}, u32[]{:S(2)}) collective-permute-start(f32[3,2,16,128]{3,2,1,0:T(8,128)S(1)} %get-tuple-element.30), channel_id=1, source_target_pairs={{1,2},{2,1},{3,4},{4,3},{5,6},{6,5},{9,10},{10,9},{11,12},{12,11},... | collective-permute-start | bytes 147464 | tf_op jit(solution)/shard_map/ppermute | solution.py:308
  19.2 6.0 %collective-permute-start.2 = (f32[3,2,16,128]{3,2,1,0:T(8,128)S(1)}, f32[3,2,16,128]{3,2,1,0:T(8,128)S(1)}, u32[]{:S(2)}, u32[]{:S(2)}) collective-permute-start(f32[3,2,16,128]{3,2,1,0:T(8,128)S(1)} %get-tuple-element.30), channel_id=1, source_target_pairs={{0,1},{1,0},{2,3},{3,2},{4,5},{5,4},{6,7},{7,6},{8,9},{9,8},{10,11... | collective-permute-start | bytes 147464 | tf_op jit(solution)/shard_map/ppermute | solution.py:307
  27.4 14.2 %all-to-all-start = ((f32[8,32,128]{2,1,0:T(8,128)}), f32[8,32,128]{2,1,0:T(8,128)S(1)}, u32[]{:S(2)}, u32[]{:S(2)}) async-start(f32[8,32,128]{2,1,0:T(8,128)} %bitcast), calls=%async_computation | async-start | bytes 262144 | tf_op jit(solution)/shard_map/all_to_all | solution.py:287
  34.0 18.1 %collective-permute-start.4 = (f32[3,2,192,128]{3,2,1,0:T(8,128)S(1)}, f32[3,2,192,128]{3,2,1,0:T(8,128)S(1)}, u32[]{:S(2)}, u32[]{:S(2)}) collective-permute-start(f32[3,2,192,128]{3,2,1,0:T(8,128)S(1)} %get-tuple-element.32.g_ref), channel_id=1, source_target_pairs={{8,16},{16,8},{24,32},{32,24},{40,48},{48,40},{56,64},{64,56},{72,... | collective-permute-start | bytes 1769480 | tf_op jit(solution)/shard_map/ppermute | solution.py:328
  41.8 10.2 %collective-permute-start.5 = (f32[3,2,192,128]{3,2,1,0:T(8,128)S(1)}, f32[3,2,192,128]{3,2,1,0:T(8,128)S(1)}, u32[]{:S(2)}, u32[]{:S(2)}) collective-permute-start(f32[3,2,192,128]{3,2,1,0:T(8,128)S(1)} %get-tuple-element.34.refs_1_.refs_2_), channel_id=1, source_target_pairs={{0,8},{8,0},{16,24},{24,16},{32,40},{40,32},{48,56},{56,48},{64,72... | collective-permute-start | bytes 1769480 | tf_op jit(solution)/shard_map/ppermute | solution.py:315
  43.7 8.3 %collective-permute-start.6 = (f32[2,8,128]{2,1,0:T(8,128)S(1)}, f32[2,8,128]{2,1,0:T(8,128)S(1)}, u32[]{:S(2)}, u32[]{:S(2)}) collective-permute-start(f32[2,8,128]{2,1,0:T(8,128)S(1)} %get-tuple-element.39), channel_id=1, source_target_pairs={{8,16},{16,8},{24,32},{32,24},{40,48},{48,40},{56,64},{64,56},{72,... | collective-permute-start | bytes 24584 | tf_op jit(solution)/shard_map/ppermute | solution.py:312
  54.3 12.4 %all-to-all-start.1 = ((f32[8,32,128]{2,1,0:T(8,128)}), f32[8,32,128]{2,1,0:T(8,128)S(1)}, u32[]{:S(2)}, u32[]{:S(2)}) async-start(f32[8,32,128]{2,1,0:T(8,128)} %bitcast.2), calls=%async_computation.1 | async-start | bytes 262144 | tf_op jit(solution)/shard_map/all_to_all | solution.py:287
  59.0 18.1 %collective-permute-start.7 = (f32[3,2,192,128]{3,2,1,0:T(8,128)S(1)}, f32[3,2,192,128]{3,2,1,0:T(8,128)S(1)}, u32[]{:S(2)}, u32[]{:S(2)}) collective-permute-start(f32[3,2,192,128]{3,2,1,0:T(8,128)S(1)} %get-tuple-element.41.g_ref), channel_id=1, source_target_pairs={{8,16},{16,8},{24,32},{32,24},{40,48},{48,40},{56,64},{64,56},{72,... | collective-permute-start | bytes 1769480 | tf_op jit(solution)/shard_map/ppermute | solution.py:328
  66.9 10.2 %collective-permute-start.8 = (f32[3,2,192,128]{3,2,1,0:T(8,128)S(1)}, f32[3,2,192,128]{3,2,1,0:T(8,128)S(1)}, u32[]{:S(2)}, u32[]{:S(2)}) collective-permute-start(f32[3,2,192,128]{3,2,1,0:T(8,128)S(1)} %get-tuple-element.43.refs_1_.refs_2_), channel_id=1, source_target_pairs={{0,8},{8,0},{16,24},{24,16},{32,40},{40,32},{48,56},{56,48},{64,72... | collective-permute-start | bytes 1769480 | tf_op jit(solution)/shard_map/ppermute | solution.py:315
  68.8 8.3 %collective-permute-start.9 = (f32[2,8,128]{2,1,0:T(8,128)S(1)}, f32[2,8,128]{2,1,0:T(8,128)S(1)}, u32[]{:S(2)}, u32[]{:S(2)}) collective-permute-start(f32[2,8,128]{2,1,0:T(8,128)S(1)} %get-tuple-element.47), channel_id=1, source_target_pairs={{8,16},{16,8},{24,32},{32,24},{40,48},{48,40},{56,64},{64,56},{72,... | collective-permute-start | bytes 24584 | tf_op jit(solution)/shard_map/ppermute | solution.py:312

commit v3 on v1

--- a/solution.py
+++ b/solution.py
@@ -108,7 +108,7 @@
 def planes_kernel(step, *refs):
     stiff_ref, inverses, u_ref, far, near, part_ref, *refs = refs
     if step > 0:
-        far_lf, old_vw, *refs = refs
+        far_lf, near_lf, old_vw, *refs = refs
     else:
         pair_y, other_y, *refs = refs
     if step < SUBSTEPS - 1:
@@ -130,11 +130,12 @@
             v, w = old_vw[0, rows, :], old_vw[1, rows, :]
         for c in range(3):
             away = [far[c, x, rows, :] for x in range(2)]
+            close = [near[c, x, rows, :] for x in range(2)]
             if step > 0:
                 for x in range(2):
                     line = 2 * c + x
                     away[x] = away[x] - v * far_lf[0, line : line + 1, :] - w * far_lf[1, line : line + 1, :]
-            close = [near[c, x, rows, :] for x in range(2)]
+                    close[x] = close[x] - v * near_lf[0, line : line + 1, :] - w * near_lf[1, line : line + 1, :]
             low = [jnp.where(odd, close[x], away[x]) for x in range(2)]
             high = [jnp.where(odd, away[x], close[x]) for x in range(2)]
             along = low + [u_ref[c, 0, rows, :], u_ref[c, 1, rows, :]] + high
@@ -198,9 +199,9 @@
 
 def correct_kernel(step, got, g_ref, vw_ref, *refs):
     if step < SUBSTEPS - 1:
-        u_ref, ends_ref, lf_ref, heads, tails, far_heads, far_tails = refs
-        first = jnp.where(lax.rem(lax.axis_index("gx"), 2) > 0, 0, 8)
-        sets = ((first, heads, tails), (8 - first, far_heads, far_tails))
+        u_ref, ends_ref, lf_ref, near_lf, heads, tails, near_heads, near_tails = refs
+        first = jnp.where(lax.rem(lax.axis_index("gx"), 2) > 0, 8, 0)
+        sets = ((first, heads, tails), (8 - first, near_heads, near_tails))
     else:
         out_ref, heads, tails, u_ref, sems = refs
         ends_ref = None
@@ -256,8 +257,10 @@
         for c in range(3):
             pltpu.make_async_copy(u_ref.at[c], out_ref.at[c], sems.at[c]).wait()
     if ends_ref is not None:
-        lf_ref[0] = far_tails[own + 1]
-        lf_ref[1] = far_heads[own + 3]
+        lf_ref[0] = lower
+        lf_ref[1] = upper
+        near_lf[0] = near_tails[own + 1]
+        near_lf[1] = near_heads[own + 3]
         before = first + jnp.maximum(own - 1, 0)
         behind = first + jnp.minimum(own + 1, 7)
         row = got[before, 2]
@@ -298,7 +301,7 @@
     if count == gy:
         tiles = lax.all_to_all(send, "gy", split_axis=0, concat_axis=0)
     else:
-        groups = [[((a + side) % gx) * gy + k for side in (0, 1) for k in range(gy)] for a in range(1, gx, 2)]
+        groups = [[a * gy + k for k in range(2 * gy)] for a in range(0, gx, 2)]
         tiles = lax.all_to_all(send, ("gx", "gy"), split_axis=0, concat_axis=0, axis_index_groups=groups)
     return tiles.reshape(count, 4, 8, LANES)
 
@@ -321,12 +324,13 @@
             current, rows = call(pack_kernel, [], outs, [pltpu.SemaphoreType.DMA((3,))], 10**6, large=[velocity])
             pair_y = lax.ppermute(rows, "gy", swaps(gy, 0, False))
             other_y = lax.ppermute(rows, "gy", swaps(gy, 1, False))
+            near = lax.ppermute(current, "gx", inside)
             own_args = [current]
             more_args = [pair_y, other_y]
         else:
+            far_lf = lax.ppermute(lf, "gx", across)
             own_args = [current, ends, share, adv]
-            more_args = [far_lf, vw]
-        near = lax.ppermute(current, "gx", inside)
+            more_args = [far_lf, near_lf, vw]
         pad = [scratch(3, 2, CY + 16, LANES)]
         own = functools.partial(own_kernel, step)
         part, *shares = call(own, own_args, [field] * (1 if last else 2), pad, 10**8, [stiffness])
@@ -340,14 +344,15 @@
         if not last:
             share, adv = shares[0], advs[0]
             far = lax.ppermute(g, "gx", across)
+            near = lax.ppermute(g, "gx", inside)
         correct = functools.partial(correct_kernel, step)
         edge = [scratch(12, 8, LANES)] * 2
         if last:
             outs = [jax.ShapeDtypeStruct((3, 2, CY, LANES), jnp.float32)]
             edge = edge + [scratch(3, 2, CY, LANES), pltpu.SemaphoreType.DMA((3,))]
             return call(correct, [got, g, vw], outs, edge, 10**8, out_hbm=True)[0]
-        outs = [field, f32(4, 8, LANES), f32(2, 8, LANES)]
-        current, ends, far_lf = call(correct, [got, g, vw], outs, edge * 2, 10**8)
+        outs = [field, f32(4, 8, LANES), f32(2, 8, LANES), f32(2, 8, LANES)]
+        current, ends, lf, near_lf = call(correct, [got, g, vw], outs, edge * 2, 10**8)
 
 
 def solution(mesh):

time: 98.3 us -> 104 us (1.058)
  blocking collectives: 14.6 us -> 44.2 us
  starting transfers between devices: 49.8 us -> 36.9 us
  waiting for transfers between devices: 21.5 us -> 11.7 us
  Pallas kernels: 11 us -> 9.5 us
    all_to_all x0 -> x2, blocking collectives: none -> 33.1 us  [exchange(): lax.all_to_all(send, ('gx', 'gy'), split_axis=0, concat_axis=0, axis_inde...]
    all_to_all x2 -> x0, starting transfers between devices: 21.7 us -> none  [exchange(): lax.all_to_all(send, ('gx', 'gy'), split_axis=0, concat_axis=0, axis_inde...]
    all_to_all x2 -> x0, waiting for transfers between devices: 13.1 us -> none  [exchange(): lax.all_to_all(send, ('gx', 'gy'), split_axis=0, concat_axis=0, axis_inde...]
    ppermute x0 -> x4, starting transfers between devices: none -> 9.97 us  [the longest x2 6.13 us: body(): far_lf = lax.ppermute(lf, 'gx', across)]
    ppermute x0 -> x4, waiting for transfers between devices: none -> 9 us  [the longest x2 9 us: body(): far_lf = lax.ppermute(lf, 'gx', across)]
    ppermute x2, waiting for transfers between devices: 5.67 us -> 0.01 us  [body(): far = lax.ppermute(g, 'gx', across)]
    ppermute x3 -> x1, starting transfers between devices: 5.76 us -> 1.92 us  [body(): near = lax.ppermute(current, 'gx', inside)]
    all_to_all x1, blocking collectives: 14.6 us -> 11.1 us  [exchange(): tiles = lax.all_to_all(send, 'gy', split_axis=0, concat_axis=0)]
  transfers between devices with their start and end apart: 10 -> 10, of which waited for: 5 -> 3; matrix products, arithmetic and copies ran while one was open for 0% -> 0% of each run, Pallas kernels for 4% -> 4%
where the time goes in v3:
time: 104 us; the launch traced here: 103 us
  blocking collectives  44.2 us (42%)
  starting transfers between devices  36.9 us (35%)
  waiting for transfers between devices  11.7 us (11%)
  Pallas kernels  9.5 us (9%)
    all_to_all x2, blocking collectives, exchange(): lax.all_to_all(send, ('gx', 'gy'), split_axis=0, concat_axis=0, axis_inde...  33.1 us
    ppermute x1, starting transfers between devices, body(): far = lax.ppermute(velocity, 'gx', across)  12.6 us
    all_to_all x1, blocking collectives, exchange(): tiles = lax.all_to_all(send, 'gy', split_axis=0, concat_axis=0)  11.1 us
    pallas_call x10, Pallas kernels, call(): pl.pallas_call(kernel, out_shape=outs, in_specs=[SMEM] * len(scalars) + [...  9.5 us
    ppermute x2, waiting for transfers between devices, body(): far_lf = lax.ppermute(lf, 'gx', across)  9 us
    ppermute x2, starting transfers between devices, body(): far = lax.ppermute(g, 'gx', across)  7.01 us
    ppermute x2, starting transfers between devices, body(): far_lf = lax.ppermute(lf, 'gx', across)  6.13 us
    ppermute x2, starting transfers between devices, body(): near = lax.ppermute(g, 'gx', inside)  3.84 us
  transfers between devices with their start and end apart: 10, of which 3 were waited for; matrix products, arithmetic and copies ran while one was open for 0% of the time, Pallas kernels for 4%

profile of v3, /device:TPU:8, one launch (start us, length us, event | category | flops | bytes accessed | tf_op | source)
XLA Modules:
  0.0 103.1 jit_solution(9370195992112674315)
XLA Ops:
  0.0 12.6 %collective-permute-start = (f32[3,2,192,128]{3,2,1,0:T(8,128)}, f32[3,2,192,128]{3,2,1,0:T(8,128)S(1)}, u32[]{:S(2)}, u32[]{:S(2)}) collective-permute-start(f32[3,2,192,128]{3,2,1,0:T(8,128)} %velocity.1), channel_id=1, source_target_pairs={{8,16},{16,8},{24,32},{32,24},{40,48},{48,40},{56,64},{64,56},{72,... | collective-permute-start | bytes 1769480 | tf_op jit(solution)/shard_map/ppermute | solution.py:322
  12.6 1.2 %shard_map.37 = (f32[3,2,192,128]{3,2,1,0:T(8,128)S(1)}, f32[3,2,16,128]{3,2,1,0:T(8,128)S(1)}) custom-call(f32[3,2,192,128]{3,2,1,0:T(8,128)} %velocity.1), custom_call_target="tpu_custom_call" | custom-call | flops 1000000 | bytes 4194304 | tf_op jit(solution)/shard_map/pallas_call | solution.py:283
  13.8 1.9 %collective-permute-start.1 = (f32[3,2,192,128]{3,2,1,0:T(8,128)S(1)}, f32[3,2,192,128]{3,2,1,0:T(8,128)S(1)}, u32[]{:S(2)}, u32[]{:S(2)}) collective-permute-start(f32[3,2,192,128]{3,2,1,0:T(8,128)S(1)} %get-tuple-element.30.refs_1_.refs_2_), channel_id=1, source_target_pairs={{0,8},{8,0},{16,24},{24,16},{32,40},{40,32},{48,56},{56,48},{64,72... | collective-permute-start | bytes 1769480 | tf_op jit(solution)/shard_map/ppermute | solution.py:327
  15.7 3.5 %collective-permute-start.3 = (f32[3,2,16,128]{3,2,1,0:T(8,128)S(1)}, f32[3,2,16,128]{3,2,1,0:T(8,128)S(1)}, u32[]{:S(2)}, u32[]{:S(2)}) collective-permute-start(f32[3,2,16,128]{3,2,1,0:T(8,128)S(1)} %get-tuple-element.32), channel_id=1, source_target_pairs={{1,2},{2,1},{3,4},{4,3},{5,6},{6,5},{9,10},{10,9},{11,12},{12,11},... | collective-permute-start | bytes 147464 | tf_op jit(solution)/shard_map/ppermute | solution.py:326
  19.2 1.9 %collective-permute-start.2 = (f32[3,2,16,128]{3,2,1,0:T(8,128)S(1)}, f32[3,2,16,128]{3,2,1,0:T(8,128)S(1)}, u32[]{:S(2)}, u32[]{:S(2)}) collective-permute-start(f32[3,2,16,128]{3,2,1,0:T(8,128)S(1)} %get-tuple-element.32), channel_id=1, source_target_pairs={{0,1},{1,0},{2,3},{3,2},{4,5},{5,4},{6,7},{7,6},{8,9},{9,8},{10,11... | collective-permute-start | bytes 147464 | tf_op jit(solution)/shard_map/ppermute | solution.py:325
  21.8 0.7 shard_map.38
  22.5 0.0 collective-permute-done.3.refs_7_
  22.5 2.7 %collective-permute-done.2.refs_6_ = f32[3,2,16,128]{3,2,1,0:T(8,128)S(1)} collective-permute-done((f32[3,2,16,128]{3,2,1,0:T(8,128)S(1)}, f32[3,2,16,128]{3,2,1,0:T(8,128)S(1)}, u32[]{:S(2)}, u32[]{:S(2)}) %collective-permute-start.2) | collective-permute-done | bytes 49184 | tf_op jit(solution)/shard_map/ppermute | solution.py:325
  25.2 0.0 collective-permute-done.refs_3_
  25.2 0.0 collective-permute-done.1.refs_4_
  25.2 1.6 %shard_map.39 = (f32[3,2,192,128]{3,2,1,0:T(8,128)S(1)}, f32[16,4,8,128]{3,2,1,0:T(8,128)S(1)}, f32[2,192,128]{2,1,0:T(8,128)S(1)}, f32[3,2,192,128]{3,2,1,0:T(8,128)S(1)}) custom-call(f32[1]{0:T(128)S(6)} %copy.4.refs_0_, f32[3,192,192]{2,1,0:T(8,128)} %refs_1_.5, f32[3,2,192,128]{3,2,1,0:T(8,128)S(1)} %get-tuple-element.30.refs_1_.refs_2_, ...), custom_call_target="tpu_custom_call" | custom-call | flops 1000000000 | bytes 4194304 | tf_op jit(solution)/shard_map/pallas_call | solution.py:283
  26.8 1.9 %collective-permute-start.5 = (f32[3,2,192,128]{3,2,1,0:T(8,128)S(1)}, f32[3,2,192,128]{3,2,1,0:T(8,128)S(1)}, u32[]{:S(2)}, u32[]{:S(2)}) collective-permute-start(f32[3,2,192,128]{3,2,1,0:T(8,128)S(1)} %get-tuple-element.34.g_ref), channel_id=1, source_target_pairs={{0,8},{8,0},{16,24},{24,16},{32,40},{40,32},{48,56},{56,48},{64,72... | collective-permute-start | bytes 1769480 | tf_op jit(solution)/shard_map/ppermute | solution.py:347
  28.7 2.8 %collective-permute-start.4 = (f32[3,2,192,128]{3,2,1,0:T(8,128)S(1)}, f32[3,2,192,128]{3,2,1,0:T(8,128)S(1)}, u32[]{:S(2)}, u32[]{:S(2)}) collective-permute-start(f32[3,2,192,128]{3,2,1,0:T(8,128)S(1)} %get-tuple-element.34.g_ref), channel_id=1, source_target_pairs={{8,16},{16,8},{24,32},{32,24},{40,48},{48,40},{56,64},{64,56},{72,... | collective-permute-start | bytes 1769480 | tf_op jit(solution)/shard_map/ppermute | solution.py:346
  31.6 17.6 %all_to_all.15 = f32[16,32,128]{2,1,0:T(8,128)S(1)} all-to-all(f32[16,32,128]{2,1,0:T(8,128)S(1)} %bitcast.10), channel_id=1, replica_groups={{0,1,2,3,4,5,6,7,8,9,10,11,12,13,14,15},{16,17,18,19,20,21,22,23,24,25,..., dimensions={0} | all-to-all | bytes 524288 | tf_op jit(solution)/shard_map/all_to_all | solution.py:305
  49.1 0.2 shard_map.40
  49.3 4.2 %collective-permute-start.6 = (f32[2,8,128]{2,1,0:T(8,128)S(1)}, f32[2,8,128]{2,1,0:T(8,128)S(1)}, u32[]{:S(2)}, u32[]{:S(2)}) collective-permute-start(f32[2,8,128]{2,1,0:T(8,128)S(1)} %get-tuple-element.41), channel_id=1, source_target_pairs={{8,16},{16,8},{24,32},{32,24},{40,48},{48,40},{56,64},{64,56},{72,... | collective-permute-start | bytes 24584 | tf_op jit(solution)/shard_map/ppermute | solution.py:331
  53.5 0.7 shard_map.41
  54.2 3.4 %collective-permute-done.6.refs_6_ = f32[2,8,128]{2,1,0:T(8,128)S(1)} collective-permute-done((f32[2,8,128]{2,1,0:T(8,128)S(1)}, f32[2,8,128]{2,1,0:T(8,128)S(1)}, u32[]{:S(2)}, u32[]{:S(2)}) %collective-permute-start.6) | collective-permute-done | bytes 8224 | tf_op jit(solution)/shard_map/ppermute | solution.py:331
  57.6 0.0 collective-permute-done.5.refs_4_
  57.6 0.0 collective-permute-done.4.refs_3_
  57.6 1.6 %shard_map.42 = (f32[3,2,192,128]{3,2,1,0:T(8,128)S(1)}, f32[16,4,8,128]{3,2,1,0:T(8,128)S(1)}, f32[2,192,128]{2,1,0:T(8,128)S(1)}, f32[3,2,192,128]{3,2,1,0:T(8,128)S(1)}) custom-call(f32[1]{0:T(128)S(6)} %copy.4.refs_0_, f32[3,192,192]{2,1,0:T(8,128)} %refs_1_.5, f32[3,2,192,128]{3,2,1,0:T(8,128)S(1)} %get-tuple-element.36.refs_1_.refs_2_, ...), custom_call_target="tpu_custom_call" | custom-call | flops 1000000000 | bytes 4194304 | tf_op jit(solution)/shard_map/pallas_call | solution.py:283
  59.2 1.9 %collective-permute-start.8 = (f32[3,2,192,128]{3,2,1,0:T(8,128)S(1)}, f32[3,2,192,128]{3,2,1,0:T(8,128)S(1)}, u32[]{:S(2)}, u32[]{:S(2)}) collective-permute-start(f32[3,2,192,128]{3,2,1,0:T(8,128)S(1)} %get-tuple-element.44.g_ref), channel_id=1, source_target_pairs={{0,8},{8,0},{16,24},{24,16},{32,40},{40,32},{48,56},{56,48},{64,72... | collective-permute-start | bytes 1769480 | tf_op jit(solution)/shard_map/ppermute | solution.py:347
  61.2 4.2 %collective-permute-start.7 = (f32[3,2,192,128]{3,2,1,0:T(8,128)S(1)}, f32[3,2,192,128]{3,2,1,0:T(8,128)S(1)}, u32[]{:S(2)}, u32[]{:S(2)}) collective-permute-start(f32[3,2,192,128]{3,2,1,0:T(8,128)S(1)} %get-tuple-element.44.g_ref), channel_id=1, source_target_pairs={{8,16},{16,8},{24,32},{32,24},{40,48},{48,40},{56,64},{64,56},{72,... | collective-permute-start | bytes 1769480 | tf_op jit(solution)/shard_map/ppermute | solution.py:346
  65.3 15.5 %all_to_all.16 = f32[16,32,128]{2,1,0:T(8,128)S(1)} all-to-all(f32[16,32,128]{2,1,0:T(8,128)S(1)} %bitcast.9), channel_id=1, replica_groups={{0,1,2,3,4,5,6,7,8,9,10,11,12,13,14,15},{16,17,18,19,20,21,22,23,24,25,..., dimensions={0} | all-to-all | bytes 524288 | tf_op jit(solution)/shard_map/all_to_all | solution.py:305
  80.9 0.2 shard_map.43
  81.1 2.0 %collective-permute-start.9 = (f32[2,8,128]{2,1,0:T(8,128)S(1)}, f32[2,8,128]{2,1,0:T(8,128)S(1)}, u32[]{:S(2)}, u32[]{:S(2)}) collective-permute-start(f32[2,8,128]{2,1,0:T(8,128)S(1)} %get-tuple-element.50), channel_id=1, source_target_pairs={{8,16},{16,8},{24,32},{32,24},{40,48},{48,40},{56,64},{64,56},{72,... | collective-permute-start | bytes 24584 | tf_op jit(solution)/shard_map/ppermute | solution.py:331
  83.1 0.7 shard_map.44.refs_5_
  83.8 5.6 %collective-permute-done.9.refs_6_ = f32[2,8,128]{2,1,0:T(8,128)S(1)} collective-permute-done((f32[2,8,128]{2,1,0:T(8,128)S(1)}, f32[2,8,128]{2,1,0:T(8,128)S(1)}, u32[]{:S(2)}, u32[]{:S(2)}) %collective-permute-start.9) | collective-permute-done | bytes 8224 | tf_op jit(solution)/shard_map/ppermute | solution.py:331
  89.4 0.0 collective-permute-done.8.refs_4_
  89.4 0.0 collective-permute-done.7.refs_3_
  89.4 1.6 %shard_map.45 = (f32[3,2,192,128]{3,2,1,0:T(8,128)S(1)}, f32[8,4,8,128]{3,2,1,0:T(8,128)S(1)}, f32[2,192,128]{2,1,0:T(8,128)S(1)}) custom-call(f32[1]{0:T(128)S(6)} %copy.4.refs_0_, f32[3,192,192]{2,1,0:T(8,128)} %refs_1_.5, f32[3,2,192,128]{3,2,1,0:T(8,128)S(1)} %get-tuple-element.46.refs_1_.refs_2_, f32[3,2,192,128]{3,2,1,0:T(8,128)S(1)} %collective-permute-done.7.refs_3_, ...), custom_call_target="tpu_custom_call" | custom-call | flops 1000000000 | bytes 4194304 | tf_op jit(solution)/shard_map/pallas_call | solution.py:283
  91.0 11.1 %all_to_all.17 = f32[8,32,128]{2,1,0:T(8,128)S(1)} all-to-all(f32[8,32,128]{2,1,0:T(8,128)S(1)} %bitcast.11), channel_id=1, replica_groups=mesh['gx'=64,'gy'=8] {'gy'}, dimensions={0} | all-to-all | bytes 262144 | tf_op jit(solution)/shard_map/all_to_all | solution.py:302
  102.1 1.0 shard_map.46
Async XLA Ops:
  0.0 25.2 %collective-permute-start = (f32[3,2,192,128]{3,2,1,0:T(8,128)}, f32[3,2,192,128]{3,2,1,0:T(8,128)S(1)}, u32[]{:S(2)}, u32[]{:S(2)}) collective-permute-start(f32[3,2,192,128]{3,2,1,0:T(8,128)} %velocity.1), channel_id=1, source_target_pairs={{8,16},{16,8},{24,32},{32,24},{40,48},{48,40},{56,64},{64,56},{72,... | collective-permute-start | bytes 1769480 | tf_op jit(solution)/shard_map/ppermute | solution.py:322
  13.8 11.4 %collective-permute-start.1 = (f32[3,2,192,128]{3,2,1,0:T(8,128)S(1)}, f32[3,2,192,128]{3,2,1,0:T(8,128)S(1)}, u32[]{:S(2)}, u32[]{:S(2)}) collective-permute-start(f32[3,2,192,128]{3,2,1,0:T(8,128)S(1)} %get-tuple-element.30.refs_1_.refs_2_), channel_id=1, source_target_pairs={{0,8},{8,0},{16,24},{24,16},{32,40},{40,32},{48,56},{56,48},{64,72... | collective-permute-start | bytes 1769480 | tf_op jit(solution)/shard_map/ppermute | solution.py:327
  15.7 6.8 %collective-permute-start.3 = (f32[3,2,16,128]{3,2,1,0:T(8,128)S(1)}, f32[3,2,16,128]{3,2,1,0:T(8,128)S(1)}, u32[]{:S(2)}, u32[]{:S(2)}) collective-permute-start(f32[3,2,16,128]{3,2,1,0:T(8,128)S(1)} %get-tuple-element.32), channel_id=1, source_target_pairs={{1,2},{2,1},{3,4},{4,3},{5,6},{6,5},{9,10},{10,9},{11,12},{12,11},... | collective-permute-start | bytes 147464 | tf_op jit(solution)/shard_map/ppermute | solution.py:326
  19.2 6.0 %collective-permute-start.2 = (f32[3,2,16,128]{3,2,1,0:T(8,128)S(1)}, f32[3,2,16,128]{3,2,1,0:T(8,128)S(1)}, u32[]{:S(2)}, u32[]{:S(2)}) collective-permute-start(f32[3,2,16,128]{3,2,1,0:T(8,128)S(1)} %get-tuple-element.32), channel_id=1, source_target_pairs={{0,1},{1,0},{2,3},{3,2},{4,5},{5,4},{6,7},{7,6},{8,9},{9,8},{10,11... | collective-permute-start | bytes 147464 | tf_op jit(solution)/shard_map/ppermute | solution.py:325
  26.8 30.9 %collective-permute-start.5 = (f32[3,2,192,128]{3,2,1,0:T(8,128)S(1)}, f32[3,2,192,128]{3,2,1,0:T(8,128)S(1)}, u32[]{:S(2)}, u32[]{:S(2)}) collective-permute-start(f32[3,2,192,128]{3,2,1,0:T(8,128)S(1)} %get-tuple-element.34.g_ref), channel_id=1, source_target_pairs={{0,8},{8,0},{16,24},{24,16},{32,40},{40,32},{48,56},{56,48},{64,72... | collective-permute-start | bytes 1769480 | tf_op jit(solution)/shard_map/ppermute | solution.py:347
  28.7 28.9 %collective-permute-start.4 = (f32[3,2,192,128]{3,2,1,0:T(8,128)S(1)}, f32[3,2,192,128]{3,2,1,0:T(8,128)S(1)}, u32[]{:S(2)}, u32[]{:S(2)}) collective-permute-start(f32[3,2,192,128]{3,2,1,0:T(8,128)S(1)} %get-tuple-element.34.g_ref), channel_id=1, source_target_pairs={{8,16},{16,8},{24,32},{32,24},{40,48},{48,40},{56,64},{64,56},{72,... | collective-permute-start | bytes 1769480 | tf_op jit(solution)/shard_map/ppermute | solution.py:346
  49.3 8.3 %collective-permute-start.6 = (f32[2,8,128]{2,1,0:T(8,128)S(1)}, f32[2,8,128]{2,1,0:T(8,128)S(1)}, u32[]{:S(2)}, u32[]{:S(2)}) collective-permute-start(f32[2,8,128]{2,1,0:T(8,128)S(1)} %get-tuple-element.41), channel_id=1, source_target_pairs={{8,16},{16,8},{24,32},{32,24},{40,48},{48,40},{56,64},{64,56},{72,... | collective-permute-start | bytes 24584 | tf_op jit(solution)/shard_map/ppermute | solution.py:331
  59.2 30.2 %collective-permute-start.8 = (f32[3,2,192,128]{3,2,1,0:T(8,128)S(1)}, f32[3,2,192,128]{3,2,1,0:T(8,128)S(1)}, u32[]{:S(2)}, u32[]{:S(2)}) collective-permute-start(f32[3,2,192,128]{3,2,1,0:T(8,128)S(1)} %get-tuple-element.44.g_ref), channel_id=1, source_target_pairs={{0,8},{8,0},{16,24},{24,16},{32,40},{40,32},{48,56},{56,48},{64,72... | collective-permute-start | bytes 1769480 | tf_op jit(solution)/shard_map/ppermute | solution.py:347
  61.2 28.3 %collective-permute-start.7 = (f32[3,2,192,128]{3,2,1,0:T(8,128)S(1)}, f32[3,2,192,128]{3,2,1,0:T(8,128)S(1)}, u32[]{:S(2)}, u32[]{:S(2)}) collective-permute-start(f32[3,2,192,128]{3,2,1,0:T(8,128)S(1)} %get-tuple-element.44.g_ref), channel_id=1, source_target_pairs={{8,16},{16,8},{24,32},{32,24},{40,48},{48,40},{56,64},{64,56},{72,... | collective-permute-start | bytes 1769480 | tf_op jit(solution)/shard_map/ppermute | solution.py:346
  81.1 8.3 %collective-permute-start.9 = (f32[2,8,128]{2,1,0:T(8,128)S(1)}, f32[2,8,128]{2,1,0:T(8,128)S(1)}, u32[]{:S(2)}, u32[]{:S(2)}) collective-permute-start(f32[2,8,128]{2,1,0:T(8,128)S(1)} %get-tuple-element.50), channel_id=1, source_target_pairs={{8,16},{16,8},{24,32},{32,24},{40,48},{48,40},{56,64},{64,56},{72,... | collective-permute-start | bytes 24584 | tf_op jit(solution)/shard_map/ppermute | solution.py:331

commit v4 on v2

--- a/solution.py
+++ b/solution.py
@@ -17,7 +17,6 @@
 CY = 192
 LANES = 128
 CHUNK = 32
-ENDS = (0, 1, CY - 2, CY - 1)
 
 VMEM = pl.BlockSpec(memory_space=pltpu.VMEM)
 HBM = pl.BlockSpec(memory_space=pltpu.HBM)
@@ -53,15 +52,17 @@
 
 def own_kernel(step, *refs):
     if step == 0:
-        stiff_ref, u_ref, *refs = refs
+        stiff_ref, inverses, u_ref, *refs = refs
         ends_ref = old_ref = None
     else:
-        stiff_ref, u_ref, ends_ref, old_share, old_ref, *refs = refs
+        stiff_ref, inverses, u_ref, ends_ref, old_share, old_ref, *refs = refs
     if step < SUBSTEPS - 1:
-        part_ref, share_ref, pad = refs
-    else:
-        part_ref, pad = refs
+        part_ref, inv_ref, share_ref, pad, sem = refs
+    else:
+        part_ref, inv_ref, pad, sem = refs
         share_ref = None
+    fetch = pltpu.make_async_copy(inverses.at[step], inv_ref, sem)
+    fetch.start()
     stiff = stiff_ref[0]
 
     for c in range(3):
@@ -103,21 +104,20 @@
                 part_ref[c, x, rows, :] = forcing
                 if share_ref is not None:
                     share_ref[c, x, rows, :] = adv
+    fetch.wait()
 
 
 def planes_kernel(step, *refs):
-    stiff_ref, inverses, u_ref, far, near, part_ref, *refs = refs
+    stiff_ref, u_ref, far, near, part_ref, inv_ref, *refs = refs
     if step > 0:
         far_lf, old_vw, *refs = refs
     else:
         pair_y, other_y, *refs = refs
     if step < SUBSTEPS - 1:
-        g_ref, send_ref, vw_ref, adv_ref, rhs, inv_ref, sem = refs
-    else:
-        g_ref, send_ref, vw_ref, rhs, inv_ref, sem = refs
+        g_ref, vw_ref, adv_ref, send_ref, rhs, packed, sems = refs
+    else:
+        g_ref, vw_ref, send_ref, rhs = refs
         adv_ref = None
-    fetch = pltpu.make_async_copy(inverses.at[step], inv_ref, sem)
-    fetch.start()
     own = lax.axis_index("gy")
     odd = lax.rem(lax.axis_index("gx"), 2) > 0
     stiff = stiff_ref[0]
@@ -170,30 +170,50 @@
                 column = slice((2 * c + x) * LANES, (2 * c + x + 1) * LANES)
                 rhs[row : row + 1, column] = rhs[row : row + 1, column] + change
 
-    fetch.wait()
     inverse = inv_ref[...]
     first_flag = jnp.where(own > 0, 1.0, 0.0)
     last_flag = jnp.where(own < 7, 1.0, 0.0)
     coupling = -implicit_share[step] * stiff
     vw_ref[0] = jnp.broadcast_to(inverse[:, 0:1] * (coupling * first_flag), (CY, LANES))
     vw_ref[1] = jnp.broadcast_to(inverse[:, CY - 1 : CY] * (coupling * last_flag), (CY, LANES))
-    for pair in range(3):
-        solved = jnp.dot(
-            inverse,
+
+    def product(some, pair):
+        return jnp.dot(
+            some,
             rhs[:, pair * 256 : pair * 256 + 256],
             precision=lax.Precision.HIGHEST,
             preferred_element_type=jnp.float32,
         )
+
+    outer = jnp.concatenate([inverse[0:8], inverse[CY - 8 : CY]], axis=0)
+    found = [product(outer, pair) for pair in range(3)]
+
+    def tile(row):
+        at = row if row < 8 else row - CY + 16
+        picked = [found[c][at : at + 1, x * LANES : (x + 1) * LANES] for c, x in lines()]
+        return jnp.concatenate(picked + [vw_ref[0, row : row + 1, :], vw_ref[1, row : row + 1, :]], axis=0)
+
+    if adv_ref is None:
+        for t, row in enumerate((0, CY - 1)):
+            for dest in range(8):
+                send_ref[dest, t] = tile(row)
+    else:
+        for way, beside in enumerate((1, CY - 2)):
+            for t, row in enumerate((0, CY - 1, beside)):
+                packed[way, t] = tile(row)
+        copies = [
+            pltpu.make_async_copy(packed.at[jnp.where(own < dest, 1, 0)], send_ref.at[dest], sems.at[dest])
+            for dest in range(8)
+        ]
+        for copy in copies:
+            copy.start()
+    for pair in range(3):
+        solved = product(inverse, pair)
         g_ref[pair, 0] = solved[:, :LANES]
         g_ref[pair, 1] = solved[:, LANES:]
-    for t, row in enumerate(ENDS):
-        tile = jnp.concatenate(
-            [g_ref[c, x, row : row + 1, :] for c in range(3) for x in range(2)]
-            + [vw_ref[0, row : row + 1, :], vw_ref[1, row : row + 1, :]],
-            axis=0,
-        )
-        for dest in range(send_ref.shape[0]):
-            send_ref[dest, t] = tile
+    if adv_ref is not None:
+        for copy in copies:
+            copy.wait()
 
 
 def correct_kernel(step, got, g_ref, vw_ref, *refs):
@@ -215,10 +235,10 @@
     prev_q, prev_last = zero, zero
     fronts, backs, front_qs, back_qs = [], [], [], []
     for block in range(8):
-        head_v, tail_v, head_w, tail_w = tip(block, 0, 0), tip(block, 3, 0), tip(block, 0, 1), tip(block, 3, 1)
+        head_v, tail_v, head_w, tail_w = tip(block, 0, 0), tip(block, 1, 0), tip(block, 0, 1), tip(block, 1, 1)
         pivot = 1.0 / (1.0 - head_v * prev_q)
         front = (got[block, 0] - head_v * prev_last) * pivot
-        back = got[block, 3] - tail_v * prev_last + tail_v * prev_q * front
+        back = got[block, 1] - tail_v * prev_last + tail_v * prev_q * front
         front_q = head_w * pivot
         back_q = tail_w + tail_v * prev_q * front_q
         fronts.append(front)
@@ -257,9 +277,9 @@
         ends_ref[0] = jnp.where(own > 0, row, zero)
         ends_ref[1] = lower
         ends_ref[2] = upper
-        row = got[behind, 1]
-        row = row - jnp.broadcast_to(got[behind, 1, 6:7, :], shape) * tails[own + 2]
-        row = row - jnp.broadcast_to(got[behind, 1, 7:8, :], shape) * heads[own + 4]
+        row = got[behind, 2]
+        row = row - jnp.broadcast_to(got[behind, 2, 6:7, :], shape) * tails[own + 2]
+        row = row - jnp.broadcast_to(got[behind, 2, 7:8, :], shape) * heads[own + 4]
         ends_ref[3] = jnp.where(own < 7, row, zero)
 
 
@@ -267,12 +287,12 @@
     return pltpu.VMEM(shape, jnp.float32)
 
 
-def call(kernel, arrays, outs, scratch, flops, scalars=(), large=(), out_hbm=False):
+def call(kernel, arrays, outs, scratch, flops, scalars=(), large=(), hbm_outs=0):
     return pl.pallas_call(
         kernel,
         out_shape=outs,
         in_specs=[SMEM] * len(scalars) + [HBM] * len(large) + [VMEM] * len(arrays),
-        out_specs=[HBM if out_hbm else VMEM] * len(outs),
+        out_specs=[VMEM] * (len(outs) - hbm_outs) + [HBM] * hbm_outs,
         scratch_shapes=scratch,
         cost_estimate=pl.CostEstimate(flops=flops, bytes_accessed=4 << 20, transcendentals=0),
         compiler_params=pltpu.CompilerParams(vmem_limit_bytes=16 << 20),
@@ -284,8 +304,8 @@
 
 
 def exchange(send):
-    tiles = lax.all_to_all(send.reshape(8, 32, LANES), "gy", split_axis=0, concat_axis=0)
-    return tiles.reshape(8, 4, 8, LANES)
+    flat = send.reshape(8, send.shape[1] * 8, LANES)
+    return lax.all_to_all(flat, "gy", split_axis=0, concat_axis=0).reshape(send.shape)
 
 
 def scratch(*shape):
@@ -313,15 +333,20 @@
             own_args = [current, ends, share, adv]
             more_args = [far_lf, vw]
         near = lax.ppermute(current, "gx", inside)
-        pad = [scratch(3, 2, CY + 16, LANES)]
+        pad = [scratch(3, 2, CY + 16, LANES), pltpu.SemaphoreType.DMA]
         own = functools.partial(own_kernel, step)
-        part, *shares = call(own, own_args, [field] * (1 if last else 2), pad, 10**8, [stiffness])
-        tiles = f32(8, 4, 8, LANES)
-        outs = [field, tiles, f32(2, CY, LANES)] + [field] * (0 if last else 1)
-        arrays = [current, far, near, part] + more_args
+        outs = [field, f32(CY, CY)] + [field] * (0 if last else 1)
+        part, inverse, *shares = call(own, own_args, outs, pad, 10**8, [stiffness], [block_inverse])
+        arrays = [current, far, near, part, inverse] + more_args
         planes = functools.partial(planes_kernel, step)
-        rhs = [scratch(CY, 6 * LANES), scratch(CY, CY), pltpu.SemaphoreType.DMA]
-        g, send, vw, *advs = call(planes, arrays, outs, rhs, 10**9, [stiffness], [block_inverse])
+        edge = [scratch(CY, 6 * LANES)]
+        if last:
+            outs = [field, f32(2, CY, LANES), f32(8, 2, 8, LANES)]
+        else:
+            outs = [field, f32(2, CY, LANES), field, jax.ShapeDtypeStruct((8, 3, 8, LANES), jnp.float32)]
+            edge += [scratch(2, 3, 8, LANES), pltpu.SemaphoreType.DMA((8,))]
+        results = call(planes, arrays, outs, edge, 10**9, [stiffness], hbm_outs=0 if last else 1)
+        g, vw, *advs, send = results
         got = exchange(send)
         if not last:
             share, adv = shares[0], advs[0]
@@ -331,7 +356,7 @@
         if last:
             outs = [jax.ShapeDtypeStruct((3, 2, CY, LANES), jnp.float32)]
             edge = edge + [scratch(3, 2, CY, LANES), pltpu.SemaphoreType.DMA((3,))]
-            return call(correct, [got, g, vw], outs, edge, 10**8, out_hbm=True)[0]
+            return call(correct, [got, g, vw], outs, edge, 10**8, hbm_outs=1)[0]
         outs = [field, f32(4, 8, LANES), f32(2, 8, LANES)]
         current, ends, lf = call(correct, [got, g, vw], outs, edge, 10**8)
 

time: 91.8 us -> 89 us (0.969)
  transfers between devices with their start and end apart: 12 -> 12, of which waited for: 5 -> 5; matrix products, arithmetic and copies ran while one was open for 0% -> 0% of each run, Pallas kernels for 4% -> 5%
where the time goes in v4:
time: 89 us; the launch traced here: 88.4 us
  starting transfers between devices  47.1 us (53%)
  waiting for transfers between devices  19.6 us (22%)
  blocking collectives  10.8 us (12%)
  Pallas kernels  10.1 us (11%)
    ppermute x1, starting transfers between devices, body(): far = lax.ppermute(velocity, 'gx', across)  12.6 us
    all_to_all x2, starting transfers between devices, exchange(): lax.all_to_all(flat, 'gy', split_axis=0, concat_axis=0).reshape(send.shape)  11.3 us
    all_to_all x1, blocking collectives, exchange(): lax.all_to_all(flat, 'gy', split_axis=0, concat_axis=0).reshape(send.shape)  10.8 us
    pallas_call x10, Pallas kernels, call(): pl.pallas_call(kernel, out_shape=outs, in_specs=[SMEM] * len(scalars) + [...  10.1 us
    ppermute x2, waiting for transfers between devices, body(): far_lf = lax.ppermute(lf, 'gx', across)  8.7 us
    all_to_all x2, waiting for transfers between devices, exchange(): lax.all_to_all(flat, 'gy', split_axis=0, concat_axis=0).reshape(send.shape)  8.46 us
    ppermute x2, starting transfers between devices, body(): far = lax.ppermute(g, 'gx', across)  6.1 us
    ppermute x2, starting transfers between devices, body(): far_lf = lax.ppermute(lf, 'gx', across)  5.94 us
  transfers between devices with their start and end apart: 12, of which 5 were waited for; matrix products, arithmetic and copies ran while one was open for 0% of the time, Pallas kernels for 5%

profile of v4, /device:TPU:8, one launch (start us, length us, event | category | flops | bytes accessed | tf_op | source)
XLA Modules:
  0.0 88.4 jit_solution(13803568012248667735)
XLA Ops:
  0.0 12.6 %collective-permute-start = (f32[3,2,192,128]{3,2,1,0:T(8,128)}, f32[3,2,192,128]{3,2,1,0:T(8,128)S(1)}, u32[]{:S(2)}, u32[]{:S(2)}) collective-permute-start(f32[3,2,192,128]{3,2,1,0:T(8,128)} %velocity.1), channel_id=1, source_target_pairs={{8,16},{16,8},{24,32},{32,24},{40,48},{48,40},{56,64},{64,56},{72,... | collective-permute-start | bytes 1769480 | tf_op jit(solution)/shard_map/ppermute | solution.py:324
  12.6 1.2 %shard_map.37 = (f32[3,2,192,128]{3,2,1,0:T(8,128)S(1)}, f32[3,2,16,128]{3,2,1,0:T(8,128)S(1)}) custom-call(f32[3,2,192,128]{3,2,1,0:T(8,128)} %velocity.1), custom_call_target="tpu_custom_call" | custom-call | flops 1000000 | bytes 4194304 | tf_op jit(solution)/shard_map/pallas_call | solution.py:291
  13.8 1.9 %collective-permute-start.1 = (f32[3,2,192,128]{3,2,1,0:T(8,128)S(1)}, f32[3,2,192,128]{3,2,1,0:T(8,128)S(1)}, u32[]{:S(2)}, u32[]{:S(2)}) collective-permute-start(f32[3,2,192,128]{3,2,1,0:T(8,128)S(1)} %get-tuple-element.32.refs_2_.refs_1_), channel_id=1, source_target_pairs={{0,8},{8,0},{16,24},{24,16},{32,40},{40,32},{48,56},{56,48},{64,72... | collective-permute-start | bytes 1769480 | tf_op jit(solution)/shard_map/ppermute | solution.py:335
  15.7 3.5 %collective-permute-start.3 = (f32[3,2,16,128]{3,2,1,0:T(8,128)S(1)}, f32[3,2,16,128]{3,2,1,0:T(8,128)S(1)}, u32[]{:S(2)}, u32[]{:S(2)}) collective-permute-start(f32[3,2,16,128]{3,2,1,0:T(8,128)S(1)} %get-tuple-element.35), channel_id=1, source_target_pairs={{1,2},{2,1},{3,4},{4,3},{5,6},{6,5},{9,10},{10,9},{11,12},{12,11},... | collective-permute-start | bytes 147464 | tf_op jit(solution)/shard_map/ppermute | solution.py:328
  19.2 1.9 %collective-permute-start.2 = (f32[3,2,16,128]{3,2,1,0:T(8,128)S(1)}, f32[3,2,16,128]{3,2,1,0:T(8,128)S(1)}, u32[]{:S(2)}, u32[]{:S(2)}) collective-permute-start(f32[3,2,16,128]{3,2,1,0:T(8,128)S(1)} %get-tuple-element.35), channel_id=1, source_target_pairs={{0,1},{1,0},{2,3},{3,2},{4,5},{5,4},{6,7},{7,6},{8,9},{9,8},{10,11... | collective-permute-start | bytes 147464 | tf_op jit(solution)/shard_map/ppermute | solution.py:327
  21.8 1.0 %shard_map.38 = (f32[3,2,192,128]{3,2,1,0:T(8,128)S(1)}, f32[192,192]{1,0:T(8,128)S(1)}, f32[3,2,192,128]{3,2,1,0:T(8,128)S(1)}) custom-call(f32[1]{0:T(128)S(6)} %copy.4.refs_0_, f32[3,192,192]{2,1,0:T(8,128)} %refs_1_.5, f32[3,2,192,128]{3,2,1,0:T(8,128)S(1)} %get-tuple-element.32.refs_2_.refs_1_), custom_call_target="tpu_custom_call" | custom-call | flops 100000000 | bytes 4194304 | tf_op jit(solution)/shard_map/pallas_call | solution.py:291
  22.7 0.0 collective-permute-done.3.refs_7_
  22.7 2.4 %collective-permute-done.2.refs_6_ = f32[3,2,16,128]{3,2,1,0:T(8,128)S(1)} collective-permute-done((f32[3,2,16,128]{3,2,1,0:T(8,128)S(1)}, f32[3,2,16,128]{3,2,1,0:T(8,128)S(1)}, u32[]{:S(2)}, u32[]{:S(2)}) %collective-permute-start.2) | collective-permute-done | bytes 49184 | tf_op jit(solution)/shard_map/ppermute | solution.py:327
  25.2 0.0 collective-permute-done.refs_2_
  25.2 0.0 collective-permute-done.1.refs_3_
  25.2 1.7 %shard_map.39 = (f32[3,2,192,128]{3,2,1,0:T(8,128)S(1)}, f32[2,192,128]{2,1,0:T(8,128)S(1)}, f32[3,2,192,128]{3,2,1,0:T(8,128)S(1)}, f32[8,3,8,128]{3,2,1,0:T(8,128)}) custom-call(f32[1]{0:T(128)S(6)} %copy.4.refs_0_, f32[3,2,192,128]{3,2,1,0:T(8,128)S(1)} %get-tuple-element.32.refs_2_.refs_1_, f32[3,2,192,128]{3,2,1,0:T(8,128)S(1)} %collective-permute-done.refs_2_, ...), custom_call_target="tpu_custom_call" | custom-call | flops 1000000000 | bytes 4194304 | tf_op jit(solution)/shard_map/pallas_call | solution.py:291
  26.9 6.5 %all-to-all-start = ((f32[8,24,128]{2,1,0:T(8,128)}), f32[8,24,128]{2,1,0:T(8,128)S(1)}, u32[]{:S(2)}, u32[]{:S(2)}) async-start(f32[8,24,128]{2,1,0:T(8,128)} %bitcast), calls=%async_computation | async-start | bytes 196608 | tf_op jit(solution)/shard_map/all_to_all | solution.py:308
  33.5 2.6 %collective-permute-start.4 = (f32[3,2,192,128]{3,2,1,0:T(8,128)S(1)}, f32[3,2,192,128]{3,2,1,0:T(8,128)S(1)}, u32[]{:S(2)}, u32[]{:S(2)}) collective-permute-start(f32[3,2,192,128]{3,2,1,0:T(8,128)S(1)} %get-tuple-element.37.g_ref), channel_id=1, source_target_pairs={{8,16},{16,8},{24,32},{32,24},{40,48},{48,40},{56,64},{64,56},{72,... | collective-permute-start | bytes 1769480 | tf_op jit(solution)/shard_map/ppermute | solution.py:353
  36.1 4.7 %all-to-all-done = f32[8,24,128]{2,1,0:T(8,128)S(1)} async-done(((f32[8,24,128]{2,1,0:T(8,128)}), f32[8,24,128]{2,1,0:T(8,128)S(1)}, u32[]{:S(2)}, u32[]{:S(2)}) %all-to-all-start) | async-done | bytes 98336 | tf_op jit(solution)/shard_map/all_to_all | solution.py:308
  40.7 0.2 shard_map.40
  41.0 1.9 %collective-permute-start.5 = (f32[3,2,192,128]{3,2,1,0:T(8,128)S(1)}, f32[3,2,192,128]{3,2,1,0:T(8,128)S(1)}, u32[]{:S(2)}, u32[]{:S(2)}) collective-permute-start(f32[3,2,192,128]{3,2,1,0:T(8,128)S(1)} %get-tuple-element.39.refs_2_.refs_1_), channel_id=1, source_target_pairs={{0,8},{8,0},{16,24},{24,16},{32,40},{40,32},{48,56},{56,48},{64,72... | collective-permute-start | bytes 1769480 | tf_op jit(solution)/shard_map/ppermute | solution.py:335
  42.9 3.3 %collective-permute-start.6 = (f32[2,8,128]{2,1,0:T(8,128)S(1)}, f32[2,8,128]{2,1,0:T(8,128)S(1)}, u32[]{:S(2)}, u32[]{:S(2)}) collective-permute-start(f32[2,8,128]{2,1,0:T(8,128)S(1)} %get-tuple-element.45), channel_id=1, source_target_pairs={{8,16},{16,8},{24,32},{32,24},{40,48},{48,40},{56,64},{64,56},{72,... | collective-permute-start | bytes 24584 | tf_op jit(solution)/shard_map/ppermute | solution.py:332
  46.2 1.0 %shard_map.41 = (f32[3,2,192,128]{3,2,1,0:T(8,128)S(1)}, f32[192,192]{1,0:T(8,128)S(1)}, f32[3,2,192,128]{3,2,1,0:T(8,128)S(1)}) custom-call(f32[1]{0:T(128)S(6)} %copy.4.refs_0_, f32[3,192,192]{2,1,0:T(8,128)} %refs_1_.5, f32[3,2,192,128]{3,2,1,0:T(8,128)S(1)} %get-tuple-element.39.refs_2_.refs_1_, f32[4,8,128]{2,1,0:T(8,128)S(1)} %get-tuple-element.40.refs_3_, ...), custom_call_target="tpu_custom_call" | custom-call | flops 100000000 | bytes 4194304 | tf_op jit(solution)/shard_map/pallas_call | solution.py:291
  47.2 4.0 %collective-permute-done.6.refs_6_ = f32[2,8,128]{2,1,0:T(8,128)S(1)} collective-permute-done((f32[2,8,128]{2,1,0:T(8,128)S(1)}, f32[2,8,128]{2,1,0:T(8,128)S(1)}, u32[]{:S(2)}, u32[]{:S(2)}) %collective-permute-start.6) | collective-permute-done | bytes 8224 | tf_op jit(solution)/shard_map/ppermute | solution.py:332
  51.2 0.0 collective-permute-done.4.refs_2_
  51.2 0.0 collective-permute-done.5.refs_3_
  51.2 1.7 %shard_map.42 = (f32[3,2,192,128]{3,2,1,0:T(8,128)S(1)}, f32[2,192,128]{2,1,0:T(8,128)S(1)}, f32[3,2,192,128]{3,2,1,0:T(8,128)S(1)}, f32[8,3,8,128]{3,2,1,0:T(8,128)}) custom-call(f32[1]{0:T(128)S(6)} %copy.4.refs_0_, f32[3,2,192,128]{3,2,1,0:T(8,128)S(1)} %get-tuple-element.39.refs_2_.refs_1_, f32[3,2,192,128]{3,2,1,0:T(8,128)S(1)} %collective-permute-done.4.refs_2_, ...), custom_call_target="tpu_custom_call" | custom-call | flops 1000000000 | bytes 4194304 | tf_op jit(solution)/shard_map/pallas_call | solution.py:291
  53.0 4.7 %all-to-all-start.1 = ((f32[8,24,128]{2,1,0:T(8,128)}), f32[8,24,128]{2,1,0:T(8,128)S(1)}, u32[]{:S(2)}, u32[]{:S(2)}) async-start(f32[8,24,128]{2,1,0:T(8,128)} %bitcast.2), calls=%async_computation.1 | async-start | bytes 196608 | tf_op jit(solution)/shard_map/all_to_all | solution.py:308
  57.7 3.5 %collective-permute-start.7 = (f32[3,2,192,128]{3,2,1,0:T(8,128)S(1)}, f32[3,2,192,128]{3,2,1,0:T(8,128)S(1)}, u32[]{:S(2)}, u32[]{:S(2)}) collective-permute-start(f32[3,2,192,128]{3,2,1,0:T(8,128)S(1)} %get-tuple-element.47.g_ref), channel_id=1, source_target_pairs={{8,16},{16,8},{24,32},{32,24},{40,48},{48,40},{56,64},{64,56},{72,... | collective-permute-start | bytes 1769480 | tf_op jit(solution)/shard_map/ppermute | solution.py:353
  61.2 3.8 %all-to-all-done.1 = f32[8,24,128]{2,1,0:T(8,128)S(1)} async-done(((f32[8,24,128]{2,1,0:T(8,128)}), f32[8,24,128]{2,1,0:T(8,128)S(1)}, u32[]{:S(2)}, u32[]{:S(2)}) %all-to-all-start.1) | async-done | bytes 98336 | tf_op jit(solution)/shard_map/all_to_all | solution.py:308
  65.0 0.2 shard_map.43
  65.2 1.9 %collective-permute-start.8 = (f32[3,2,192,128]{3,2,1,0:T(8,128)S(1)}, f32[3,2,192,128]{3,2,1,0:T(8,128)S(1)}, u32[]{:S(2)}, u32[]{:S(2)}) collective-permute-start(f32[3,2,192,128]{3,2,1,0:T(8,128)S(1)} %get-tuple-element.49.refs_2_.refs_1_), channel_id=1, source_target_pairs={{0,8},{8,0},{16,24},{24,16},{32,40},{40,32},{48,56},{56,48},{64,72... | collective-permute-start | bytes 1769480 | tf_op jit(solution)/shard_map/ppermute | solution.py:335
  67.1 2.6 %collective-permute-start.9 = (f32[2,8,128]{2,1,0:T(8,128)S(1)}, f32[2,8,128]{2,1,0:T(8,128)S(1)}, u32[]{:S(2)}, u32[]{:S(2)}) collective-permute-start(f32[2,8,128]{2,1,0:T(8,128)S(1)} %get-tuple-element.55), channel_id=1, source_target_pairs={{8,16},{16,8},{24,32},{32,24},{40,48},{48,40},{56,64},{64,56},{72,... | collective-permute-start | bytes 24584 | tf_op jit(solution)/shard_map/ppermute | solution.py:332
  69.8 0.9 %shard_map.44 = (f32[3,2,192,128]{3,2,1,0:T(8,128)S(1)}, f32[192,192]{1,0:T(8,128)S(1)}) custom-call(f32[1]{0:T(128)S(6)} %copy.4.refs_0_, f32[3,192,192]{2,1,0:T(8,128)} %refs_1_.5, f32[3,2,192,128]{3,2,1,0:T(8,128)S(1)} %get-tuple-element.49.refs_2_.refs_1_, f32[4,8,128]{2,1,0:T(8,128)S(1)} %get-tuple-element.50.refs_3_, ...), custom_call_target="tpu_custom_call" | custom-call | flops 100000000 | bytes 4194304 | tf_op jit(solution)/shard_map/pallas_call | solution.py:291
  70.7 4.7 %collective-permute-done.9.refs_6_ = f32[2,8,128]{2,1,0:T(8,128)S(1)} collective-permute-done((f32[2,8,128]{2,1,0:T(8,128)S(1)}, f32[2,8,128]{2,1,0:T(8,128)S(1)}, u32[]{:S(2)}, u32[]{:S(2)}) %collective-permute-start.9) | collective-permute-done | bytes 8224 | tf_op jit(solution)/shard_map/ppermute | solution.py:332
  75.4 0.0 collective-permute-done.7.refs_2_
  75.4 0.0 collective-permute-done.8.refs_3_
  75.4 1.1 %shard_map.45 = (f32[3,2,192,128]{3,2,1,0:T(8,128)S(1)}, f32[2,192,128]{2,1,0:T(8,128)S(1)}, f32[8,2,8,128]{3,2,1,0:T(8,128)S(1)}) custom-call(f32[1]{0:T(128)S(6)} %copy.4.refs_0_, f32[3,2,192,128]{3,2,1,0:T(8,128)S(1)} %get-tuple-element.49.refs_2_.refs_1_, f32[3,2,192,128]{3,2,1,0:T(8,128)S(1)} %collective-permute-done.7.refs_2_, ...), custom_call_target="tpu_custom_call" | custom-call | flops 1000000000 | bytes 4194304 | tf_op jit(solution)/shard_map/pallas_call | solution.py:291
  76.6 10.8 %all_to_all.15 = f32[8,16,128]{2,1,0:T(8,128)S(1)} all-to-all(f32[8,16,128]{2,1,0:T(8,128)S(1)} %bitcast.9), channel_id=1, replica_groups=mesh['gx'=64,'gy'=8] {'gy'}, dimensions={0} | all-to-all | bytes 131072 | tf_op jit(solution)/shard_map/all_to_all | solution.py:308
  87.4 1.0 %shard_map.46 = f32[3,2,192,128]{3,2,1,0:T(8,128)} custom-call(f32[8,2,8,128]{3,2,1,0:T(8,128)S(1)} %bitcast.8, f32[3,2,192,128]{3,2,1,0:T(8,128)S(1)} %get-tuple-element.57.g_ref, f32[2,192,128]{2,1,0:T(8,128)S(1)} %get-tuple-element.58.vw_ref), custom_call_target="tpu_custom_call" | custom-call | flops 100000000 | bytes 4194304 | tf_op jit(solution)/shard_map/pallas_call | solution.py:291
Async XLA Ops:
  0.0 25.2 %collective-permute-start = (f32[3,2,192,128]{3,2,1,0:T(8,128)}, f32[3,2,192,128]{3,2,1,0:T(8,128)S(1)}, u32[]{:S(2)}, u32[]{:S(2)}) collective-permute-start(f32[3,2,192,128]{3,2,1,0:T(8,128)} %velocity.1), channel_id=1, source_target_pairs={{8,16},{16,8},{24,32},{32,24},{40,48},{48,40},{56,64},{64,56},{72,... | collective-permute-start | bytes 1769480 | tf_op jit(solution)/shard_map/ppermute | solution.py:324
  13.8 11.4 %collective-permute-start.1 = (f32[3,2,192,128]{3,2,1,0:T(8,128)S(1)}, f32[3,2,192,128]{3,2,1,0:T(8,128)S(1)}, u32[]{:S(2)}, u32[]{:S(2)}) collective-permute-start(f32[3,2,192,128]{3,2,1,0:T(8,128)S(1)} %get-tuple-element.32.refs_2_.refs_1_), channel_id=1, source_target_pairs={{0,8},{8,0},{16,24},{24,16},{32,40},{40,32},{48,56},{56,48},{64,72... | collective-permute-start | bytes 1769480 | tf_op jit(solution)/shard_map/ppermute | solution.py:335
  15.7 7.0 %collective-permute-start.3 = (f32[3,2,16,128]{3,2,1,0:T(8,128)S(1)}, f32[3,2,16,128]{3,2,1,0:T(8,128)S(1)}, u32[]{:S(2)}, u32[]{:S(2)}) collective-permute-start(f32[3,2,16,128]{3,2,1,0:T(8,128)S(1)} %get-tuple-element.35), channel_id=1, source_target_pairs={{1,2},{2,1},{3,4},{4,3},{5,6},{6,5},{9,10},{10,9},{11,12},{12,11},... | collective-permute-start | bytes 147464 | tf_op jit(solution)/shard_map/ppermute | solution.py:328
  19.2 6.0 %collective-permute-start.2 = (f32[3,2,16,128]{3,2,1,0:T(8,128)S(1)}, f32[3,2,16,128]{3,2,1,0:T(8,128)S(1)}, u32[]{:S(2)}, u32[]{:S(2)}) collective-permute-start(f32[3,2,16,128]{3,2,1,0:T(8,128)S(1)} %get-tuple-element.35), channel_id=1, source_target_pairs={{0,1},{1,0},{2,3},{3,2},{4,5},{5,4},{6,7},{7,6},{8,9},{9,8},{10,11... | collective-permute-start | bytes 147464 | tf_op jit(solution)/shard_map/ppermute | solution.py:327
  26.9 13.8 %all-to-all-start = ((f32[8,24,128]{2,1,0:T(8,128)}), f32[8,24,128]{2,1,0:T(8,128)S(1)}, u32[]{:S(2)}, u32[]{:S(2)}) async-start(f32[8,24,128]{2,1,0:T(8,128)} %bitcast), calls=%async_computation | async-start | bytes 196608 | tf_op jit(solution)/shard_map/all_to_all | solution.py:308
  33.5 17.7 %collective-permute-start.4 = (f32[3,2,192,128]{3,2,1,0:T(8,128)S(1)}, f32[3,2,192,128]{3,2,1,0:T(8,128)S(1)}, u32[]{:S(2)}, u32[]{:S(2)}) collective-permute-start(f32[3,2,192,128]{3,2,1,0:T(8,128)S(1)} %get-tuple-element.37.g_ref), channel_id=1, source_target_pairs={{8,16},{16,8},{24,32},{32,24},{40,48},{48,40},{56,64},{64,56},{72,... | collective-permute-start | bytes 1769480 | tf_op jit(solution)/shard_map/ppermute | solution.py:353
  41.0 10.2 %collective-permute-start.5 = (f32[3,2,192,128]{3,2,1,0:T(8,128)S(1)}, f32[3,2,192,128]{3,2,1,0:T(8,128)S(1)}, u32[]{:S(2)}, u32[]{:S(2)}) collective-permute-start(f32[3,2,192,128]{3,2,1,0:T(8,128)S(1)} %get-tuple-element.39.refs_2_.refs_1_), channel_id=1, source_target_pairs={{0,8},{8,0},{16,24},{24,16},{32,40},{40,32},{48,56},{56,48},{64,72... | collective-permute-start | bytes 1769480 | tf_op jit(solution)/shard_map/ppermute | solution.py:335
  42.9 8.3 %collective-permute-start.6 = (f32[2,8,128]{2,1,0:T(8,128)S(1)}, f32[2,8,128]{2,1,0:T(8,128)S(1)}, u32[]{:S(2)}, u32[]{:S(2)}) collective-permute-start(f32[2,8,128]{2,1,0:T(8,128)S(1)} %get-tuple-element.45), channel_id=1, source_target_pairs={{8,16},{16,8},{24,32},{32,24},{40,48},{48,40},{56,64},{64,56},{72,... | collective-permute-start | bytes 24584 | tf_op jit(solution)/shard_map/ppermute | solution.py:332
  53.0 12.0 %all-to-all-start.1 = ((f32[8,24,128]{2,1,0:T(8,128)}), f32[8,24,128]{2,1,0:T(8,128)S(1)}, u32[]{:S(2)}, u32[]{:S(2)}) async-start(f32[8,24,128]{2,1,0:T(8,128)} %bitcast.2), calls=%async_computation.1 | async-start | bytes 196608 | tf_op jit(solution)/shard_map/all_to_all | solution.py:308
  57.7 17.7 %collective-permute-start.7 = (f32[3,2,192,128]{3,2,1,0:T(8,128)S(1)}, f32[3,2,192,128]{3,2,1,0:T(8,128)S(1)}, u32[]{:S(2)}, u32[]{:S(2)}) collective-permute-start(f32[3,2,192,128]{3,2,1,0:T(8,128)S(1)} %get-tuple-element.47.g_ref), channel_id=1, source_target_pairs={{8,16},{16,8},{24,32},{32,24},{40,48},{48,40},{56,64},{64,56},{72,... | collective-permute-start | bytes 1769480 | tf_op jit(solution)/shard_map/ppermute | solution.py:353
  65.2 10.2 %collective-permute-start.8 = (f32[3,2,192,128]{3,2,1,0:T(8,128)S(1)}, f32[3,2,192,128]{3,2,1,0:T(8,128)S(1)}, u32[]{:S(2)}, u32[]{:S(2)}) collective-permute-start(f32[3,2,192,128]{3,2,1,0:T(8,128)S(1)} %get-tuple-element.49.refs_2_.refs_1_), channel_id=1, source_target_pairs={{0,8},{8,0},{16,24},{24,16},{32,40},{40,32},{48,56},{56,48},{64,72... | collective-permute-start | bytes 1769480 | tf_op jit(solution)/shard_map/ppermute | solution.py:335
  67.1 8.3 %collective-permute-start.9 = (f32[2,8,128]{2,1,0:T(8,128)S(1)}, f32[2,8,128]{2,1,0:T(8,128)S(1)}, u32[]{:S(2)}, u32[]{:S(2)}) collective-permute-start(f32[2,8,128]{2,1,0:T(8,128)S(1)} %get-tuple-element.55), channel_id=1, source_target_pairs={{8,16},{16,8},{24,32},{32,24},{40,48},{48,40},{56,64},{64,56},{72,... | collective-permute-start | bytes 24584 | tf_op jit(solution)/shard_map/ppermute | solution.py:332

commit v5 on v4

--- a/solution.py
+++ b/solution.py
@@ -55,7 +55,7 @@
         stiff_ref, inverses, u_ref, *refs = refs
         ends_ref = old_ref = None
     else:
-        stiff_ref, inverses, u_ref, ends_ref, old_share, old_ref, *refs = refs
+        stiff_ref, inverses, u_ref, ends_ref, old_share, old_ref, _, *refs = refs
     if step < SUBSTEPS - 1:
         part_ref, inv_ref, share_ref, pad, sem = refs
     else:
@@ -120,6 +120,7 @@
         adv_ref = None
     own = lax.axis_index("gy")
     odd = lax.rem(lax.axis_index("gx"), 2) > 0
+    partner = jnp.where(odd, 1, 0)
     stiff = stiff_ref[0]
 
     for r in range(0, CY, CHUNK):
@@ -128,12 +129,13 @@
         minus = [2.0 * courant[0] * jnp.minimum(u_ref[0, x, rows, :], 0.0) for x in range(2)]
         if step > 0:
             v, w = old_vw[0, rows, :], old_vw[1, rows, :]
+            low_far, high_far = far_lf[partner, 0], far_lf[partner, 1]
         for c in range(3):
             away = [far[c, x, rows, :] for x in range(2)]
             if step > 0:
                 for x in range(2):
                     line = 2 * c + x
-                    away[x] = away[x] - v * far_lf[0, line : line + 1, :] - w * far_lf[1, line : line + 1, :]
+                    away[x] = away[x] - v * low_far[line : line + 1, :] - w * high_far[line : line + 1, :]
             close = [near[c, x, rows, :] for x in range(2)]
             low = [jnp.where(odd, close[x], away[x]) for x in range(2)]
             high = [jnp.where(odd, away[x], close[x]) for x in range(2)]
@@ -185,35 +187,46 @@
             preferred_element_type=jnp.float32,
         )
 
-    outer = jnp.concatenate([inverse[0:8], inverse[CY - 8 : CY]], axis=0)
-    found = [product(outer, pair) for pair in range(3)]
-
-    def tile(row):
-        at = row if row < 8 else row - CY + 16
-        picked = [found[c][at : at + 1, x * LANES : (x + 1) * LANES] for c, x in lines()]
+    def tile(row, pick):
+        picked = [pick(c, x, row) for c, x in lines()]
         return jnp.concatenate(picked + [vw_ref[0, row : row + 1, :], vw_ref[1, row : row + 1, :]], axis=0)
 
-    if adv_ref is None:
-        for t, row in enumerate((0, CY - 1)):
-            for dest in range(8):
-                send_ref[dest, t] = tile(row)
-    else:
+    if adv_ref is not None:
+        outer = jnp.concatenate([inverse[0:8], inverse[CY - 8 : CY]], axis=0)
+        found = [product(outer, pair) for pair in range(3)]
+
+        def outermost(c, x, row):
+            at = row if row < 8 else row - CY + 16
+            return found[c][at : at + 1, x * LANES : (x + 1) * LANES]
+
         for way, beside in enumerate((1, CY - 2)):
             for t, row in enumerate((0, CY - 1, beside)):
-                packed[way, t] = tile(row)
+                packed[way, t] = tile(row, outermost)
         copies = [
             pltpu.make_async_copy(packed.at[jnp.where(own < dest, 1, 0)], send_ref.at[dest], sems.at[dest])
             for dest in range(8)
         ]
         for copy in copies:
             copy.start()
-    for pair in range(3):
-        solved = product(inverse, pair)
-        g_ref[pair, 0] = solved[:, :LANES]
-        g_ref[pair, 1] = solved[:, LANES:]
-    if adv_ref is not None:
+
+        @pl.when(own >= 0)
+        def _():
+            for pair in range(3):
+                solved = product(inv_ref[...], pair)
+                g_ref[pair, 0] = solved[:, :LANES]
+                g_ref[pair, 1] = solved[:, LANES:]
+
         for copy in copies:
             copy.wait()
+    else:
+        for pair in range(3):
+            solved = product(inverse, pair)
+            g_ref[pair, 0] = solved[:, :LANES]
+            g_ref[pair, 1] = solved[:, LANES:]
+        for t, row in enumerate((0, CY - 1)):
+            ends = tile(row, lambda c, x, row: g_ref[c, x, row : row + 1, :])
+            for dest in range(8):
+                send_ref[dest, t] = ends
 
 
 def correct_kernel(step, got, g_ref, vw_ref, *refs):
@@ -267,8 +280,9 @@
         for c in range(3):
             pltpu.make_async_copy(u_ref.at[c], out_ref.at[c], sems.at[c]).wait()
     if ends_ref is not None:
-        lf_ref[0] = lower
-        lf_ref[1] = upper
+        for side in range(2):
+            lf_ref[side, 0] = lower
+            lf_ref[side, 1] = upper
         before = jnp.maximum(own - 1, 0)
         behind = jnp.minimum(own + 1, 7)
         row = got[before, 2]
@@ -329,8 +343,11 @@
             own_args = [current]
             more_args = [pair_y, other_y]
         else:
-            far_lf = lax.ppermute(lf, "gx", across)
-            own_args = [current, ends, share, adv]
+            pairs = [[a, (a + 1) % gx] for a in range(1, gx, 2)]
+            far_lf = lax.all_to_all(
+                lf.reshape(2, 16, LANES), "gx", split_axis=0, concat_axis=0, axis_index_groups=pairs
+            ).reshape(2, 2, 8, LANES)
+            own_args = [current, ends, share, adv, far_lf]
             more_args = [far_lf, vw]
         near = lax.ppermute(current, "gx", inside)
         pad = [scratch(3, 2, CY + 16, LANES), pltpu.SemaphoreType.DMA]
@@ -357,7 +374,7 @@
             outs = [jax.ShapeDtypeStruct((3, 2, CY, LANES), jnp.float32)]
             edge = edge + [scratch(3, 2, CY, LANES), pltpu.SemaphoreType.DMA((3,))]
             return call(correct, [got, g, vw], outs, edge, 10**8, hbm_outs=1)[0]
-        outs = [field, f32(4, 8, LANES), f32(2, 8, LANES)]
+        outs = [field, f32(4, 8, LANES), f32(2, 2, 8, LANES)]
         current, ends, lf = call(correct, [got, g, vw], outs, edge, 10**8)
 
 

time: 89 us -> 91.4 us (1.027)
  blocking collectives: 10.8 us -> 28.7 us
  waiting for transfers between devices: 19.6 us -> 7.79 us
  starting transfers between devices: 47.1 us -> 44.2 us
    all_to_all x0 -> x2, blocking collectives: none -> 15.5 us  [body(): lax.all_to_all(lf.reshape(2, 16, LANES), 'gx', split_axis=0, concat_axis=...]
    ppermute x2 -> x0, waiting for transfers between devices: 8.7 us -> none  [body(): far_lf = lax.ppermute(lf, 'gx', across)]
    ppermute x2 -> x0, starting transfers between devices: 5.94 us -> none  [body(): far_lf = lax.ppermute(lf, 'gx', across)]
    all_to_all x2, waiting for transfers between devices: 8.46 us -> 5.33 us  [exchange(): lax.all_to_all(flat, 'gy', split_axis=0, concat_axis=0).reshape(send.shape)]
    ppermute x2, starting transfers between devices: 6.1 us -> 9.22 us  [body(): far = lax.ppermute(g, 'gx', across)]
    all_to_all x1, blocking collectives: 10.8 us -> 13.2 us  [exchange(): lax.all_to_all(flat, 'gy', split_axis=0, concat_axis=0).reshape(send.shape)]
  transfers between devices with their start and end apart: 12 -> 10, of which waited for: 5 -> 3; matrix products, arithmetic and copies ran while one was open for 0% -> 0% of each run, Pallas kernels for 5% -> 5%
where the time goes in v5:
time: 91.4 us; the launch traced here: 90.8 us
  starting transfers between devices  44.2 us (48%)
  blocking collectives  28.7 us (31%)
  Pallas kernels  9.19 us (10%)
  waiting for transfers between devices  7.79 us (9%)
    all_to_all x2, blocking collectives, body(): lax.all_to_all(lf.reshape(2, 16, LANES), 'gx', split_axis=0, concat_axis=...  15.5 us
    all_to_all x1, blocking collectives, exchange(): lax.all_to_all(flat, 'gy', split_axis=0, concat_axis=0).reshape(send.shape)  13.2 us
    ppermute x1, starting transfers between devices, body(): far = lax.ppermute(velocity, 'gx', across)  12.6 us
    all_to_all x2, starting transfers between devices, exchange(): lax.all_to_all(flat, 'gy', split_axis=0, concat_axis=0).reshape(send.shape)  11.3 us
    ppermute x2, starting transfers between devices, body(): far = lax.ppermute(g, 'gx', across)  9.22 us
    pallas_call x10, Pallas kernels, call(): pl.pallas_call(kernel, out_shape=outs, in_specs=[SMEM] * len(scalars) + [...  9.19 us
    ppermute x3, starting transfers between devices, body(): near = lax.ppermute(current, 'gx', inside)  5.76 us
    all_to_all x2, waiting for transfers between devices, exchange(): lax.all_to_all(flat, 'gy', split_axis=0, concat_axis=0).reshape(send.shape)  5.33 us
  transfers between devices with their start and end apart: 10, of which 3 were waited for; matrix products, arithmetic and copies ran while one was open for 0% of the time, Pallas kernels for 5%

profile of v5, /device:TPU:8, one launch (start us, length us, event | category | flops | bytes accessed | tf_op | source)
XLA Modules:
  0.0 90.8 jit_solution(2921304922647633061)
XLA Ops:
  0.0 12.6 %collective-permute-start = (f32[3,2,192,128]{3,2,1,0:T(8,128)}, f32[3,2,192,128]{3,2,1,0:T(8,128)S(1)}, u32[]{:S(2)}, u32[]{:S(2)}) collective-permute-start(f32[3,2,192,128]{3,2,1,0:T(8,128)} %velocity.1), channel_id=1, source_target_pairs={{8,16},{16,8},{24,32},{32,24},{40,48},{48,40},{56,64},{64,56},{72,... | collective-permute-start | bytes 1769480 | tf_op jit(solution)/shard_map/ppermute | solution.py:338
  12.6 1.2 %shard_map.37 = (f32[3,2,192,128]{3,2,1,0:T(8,128)S(1)}, f32[3,2,16,128]{3,2,1,0:T(8,128)S(1)}) custom-call(f32[3,2,192,128]{3,2,1,0:T(8,128)} %velocity.1), custom_call_target="tpu_custom_call" | custom-call | flops 1000000 | bytes 4194304 | tf_op jit(solution)/shard_map/pallas_call | solution.py:305
  13.8 1.9 %collective-permute-start.1 = (f32[3,2,192,128]{3,2,1,0:T(8,128)S(1)}, f32[3,2,192,128]{3,2,1,0:T(8,128)S(1)}, u32[]{:S(2)}, u32[]{:S(2)}) collective-permute-start(f32[3,2,192,128]{3,2,1,0:T(8,128)S(1)} %get-tuple-element.32.refs_2_.refs_1_), channel_id=1, source_target_pairs={{0,8},{8,0},{16,24},{24,16},{32,40},{40,32},{48,56},{56,48},{64,72... | collective-permute-start | bytes 1769480 | tf_op jit(solution)/shard_map/ppermute | solution.py:352
  15.7 3.5 %collective-permute-start.3 = (f32[3,2,16,128]{3,2,1,0:T(8,128)S(1)}, f32[3,2,16,128]{3,2,1,0:T(8,128)S(1)}, u32[]{:S(2)}, u32[]{:S(2)}) collective-permute-start(f32[3,2,16,128]{3,2,1,0:T(8,128)S(1)} %get-tuple-element.35), channel_id=1, source_target_pairs={{1,2},{2,1},{3,4},{4,3},{5,6},{6,5},{9,10},{10,9},{11,12},{12,11},... | collective-permute-start | bytes 147464 | tf_op jit(solution)/shard_map/ppermute | solution.py:342
  19.2 1.9 %collective-permute-start.2 = (f32[3,2,16,128]{3,2,1,0:T(8,128)S(1)}, f32[3,2,16,128]{3,2,1,0:T(8,128)S(1)}, u32[]{:S(2)}, u32[]{:S(2)}) collective-permute-start(f32[3,2,16,128]{3,2,1,0:T(8,128)S(1)} %get-tuple-element.35), channel_id=1, source_target_pairs={{0,1},{1,0},{2,3},{3,2},{4,5},{5,4},{6,7},{7,6},{8,9},{9,8},{10,11... | collective-permute-start | bytes 147464 | tf_op jit(solution)/shard_map/ppermute | solution.py:341
  21.8 1.0 %shard_map.38 = (f32[3,2,192,128]{3,2,1,0:T(8,128)S(1)}, f32[192,192]{1,0:T(8,128)S(1)}, f32[3,2,192,128]{3,2,1,0:T(8,128)S(1)}) custom-call(f32[1]{0:T(128)S(6)} %copy.4.refs_0_, f32[3,192,192]{2,1,0:T(8,128)} %refs_1_.5, f32[3,2,192,128]{3,2,1,0:T(8,128)S(1)} %get-tuple-element.32.refs_2_.refs_1_), custom_call_target="tpu_custom_call" | custom-call | flops 100000000 | bytes 4194304 | tf_op jit(solution)/shard_map/pallas_call | solution.py:305
  22.7 0.0 collective-permute-done.3.refs_7_
  22.7 2.4 %collective-permute-done.2.refs_6_ = f32[3,2,16,128]{3,2,1,0:T(8,128)S(1)} collective-permute-done((f32[3,2,16,128]{3,2,1,0:T(8,128)S(1)}, f32[3,2,16,128]{3,2,1,0:T(8,128)S(1)}, u32[]{:S(2)}, u32[]{:S(2)}) %collective-permute-start.2) | collective-permute-done | bytes 49184 | tf_op jit(solution)/shard_map/ppermute | solution.py:341
  25.2 0.0 collective-permute-done.refs_2_
  25.2 0.0 collective-permute-done.1.refs_3_
  25.2 1.4 %shard_map.39 = (f32[3,2,192,128]{3,2,1,0:T(8,128)S(1)}, f32[2,192,128]{2,1,0:T(8,128)S(1)}, f32[3,2,192,128]{3,2,1,0:T(8,128)S(1)}, f32[8,3,8,128]{3,2,1,0:T(8,128)}) custom-call(f32[1]{0:T(128)S(6)} %copy.4.refs_0_, f32[3,2,192,128]{3,2,1,0:T(8,128)S(1)} %get-tuple-element.32.refs_2_.refs_1_, f32[3,2,192,128]{3,2,1,0:T(8,128)S(1)} %collective-permute-done.refs_2_, ...), custom_call_target="tpu_custom_call" | custom-call | flops 1000000000 | bytes 4194304 | tf_op jit(solution)/shard_map/pallas_call | solution.py:305
  26.6 6.5 %all-to-all-start = ((f32[8,24,128]{2,1,0:T(8,128)}), f32[8,24,128]{2,1,0:T(8,128)S(1)}, u32[]{:S(2)}, u32[]{:S(2)}) async-start(f32[8,24,128]{2,1,0:T(8,128)} %bitcast), calls=%async_computation | async-start | bytes 196608 | tf_op jit(solution)/shard_map/all_to_all | solution.py:322
  33.1 2.6 %collective-permute-start.4 = (f32[3,2,192,128]{3,2,1,0:T(8,128)S(1)}, f32[3,2,192,128]{3,2,1,0:T(8,128)S(1)}, u32[]{:S(2)}, u32[]{:S(2)}) collective-permute-start(f32[3,2,192,128]{3,2,1,0:T(8,128)S(1)} %get-tuple-element.37.g_ref), channel_id=1, source_target_pairs={{8,16},{16,8},{24,32},{32,24},{40,48},{48,40},{56,64},{64,56},{72,... | collective-permute-start | bytes 1769480 | tf_op jit(solution)/shard_map/ppermute | solution.py:370
  35.7 4.7 %all-to-all-done = f32[8,24,128]{2,1,0:T(8,128)S(1)} async-done(((f32[8,24,128]{2,1,0:T(8,128)}), f32[8,24,128]{2,1,0:T(8,128)S(1)}, u32[]{:S(2)}, u32[]{:S(2)}) %all-to-all-start) | async-done | bytes 98336 | tf_op jit(solution)/shard_map/all_to_all | solution.py:322
  40.4 0.2 shard_map.40
  40.6 1.9 %collective-permute-start.5 = (f32[3,2,192,128]{3,2,1,0:T(8,128)S(1)}, f32[3,2,192,128]{3,2,1,0:T(8,128)S(1)}, u32[]{:S(2)}, u32[]{:S(2)}) collective-permute-start(f32[3,2,192,128]{3,2,1,0:T(8,128)S(1)} %get-tuple-element.39.refs_2_.refs_1_), channel_id=1, source_target_pairs={{0,8},{8,0},{16,24},{24,16},{32,40},{40,32},{48,56},{56,48},{64,72... | collective-permute-start | bytes 1769480 | tf_op jit(solution)/shard_map/ppermute | solution.py:352
  42.6 7.7 %all_to_all.25 = f32[2,16,128]{2,1,0:T(8,128)S(1)} all-to-all(f32[2,16,128]{2,1,0:T(8,128)S(1)} %bitcast.18), channel_id=1, replica_groups={{8,16},{24,32},{40,48},{56,64},{72,80},{88,96},{104,112},{120,128},{136..., dimensions={0} | all-to-all | bytes 32768 | tf_op jit(solution)/shard_map/all_to_all | solution.py:347
  50.3 1.0 %shard_map.41 = (f32[3,2,192,128]{3,2,1,0:T(8,128)S(1)}, f32[192,192]{1,0:T(8,128)S(1)}, f32[3,2,192,128]{3,2,1,0:T(8,128)S(1)}) custom-call(f32[1]{0:T(128)S(6)} %copy.4.refs_0_, f32[3,192,192]{2,1,0:T(8,128)} %refs_1_.5, f32[3,2,192,128]{3,2,1,0:T(8,128)S(1)} %get-tuple-element.39.refs_2_.refs_1_, f32[4,8,128]{2,1,0:T(8,128)S(1)} %get-tuple-element.40.refs_3_, ...), custom_call_target="tpu_custom_call" | custom-call | flops 100000000 | bytes 4194304 | tf_op jit(solution)/shard_map/pallas_call | solution.py:305
  51.2 0.0 collective-permute-done.4.refs_2_
  51.2 0.0 collective-permute-done.5.refs_3_
  51.2 1.4 %shard_map.42 = (f32[3,2,192,128]{3,2,1,0:T(8,128)S(1)}, f32[2,192,128]{2,1,0:T(8,128)S(1)}, f32[3,2,192,128]{3,2,1,0:T(8,128)S(1)}, f32[8,3,8,128]{3,2,1,0:T(8,128)}) custom-call(f32[1]{0:T(128)S(6)} %copy.4.refs_0_, f32[3,2,192,128]{3,2,1,0:T(8,128)S(1)} %get-tuple-element.39.refs_2_.refs_1_, f32[3,2,192,128]{3,2,1,0:T(8,128)S(1)} %collective-permute-done.4.refs_2_, ...), custom_call_target="tpu_custom_call" | custom-call | flops 1000000000 | bytes 4194304 | tf_op jit(solution)/shard_map/pallas_call | solution.py:305
  52.7 4.7 %all-to-all-start.2 = ((f32[8,24,128]{2,1,0:T(8,128)}), f32[8,24,128]{2,1,0:T(8,128)S(1)}, u32[]{:S(2)}, u32[]{:S(2)}) async-start(f32[8,24,128]{2,1,0:T(8,128)} %bitcast.4), calls=%async_computation.2 | async-start | bytes 196608 | tf_op jit(solution)/shard_map/all_to_all | solution.py:322
  57.4 6.7 %collective-permute-start.6 = (f32[3,2,192,128]{3,2,1,0:T(8,128)S(1)}, f32[3,2,192,128]{3,2,1,0:T(8,128)S(1)}, u32[]{:S(2)}, u32[]{:S(2)}) collective-permute-start(f32[3,2,192,128]{3,2,1,0:T(8,128)S(1)} %get-tuple-element.47.g_ref), channel_id=1, source_target_pairs={{8,16},{16,8},{24,32},{32,24},{40,48},{48,40},{56,64},{64,56},{72,... | collective-permute-start | bytes 1769480 | tf_op jit(solution)/shard_map/ppermute | solution.py:370
  64.1 0.6 all-to-all-done.2
  64.7 0.2 shard_map.43
  64.9 1.9 %collective-permute-start.7 = (f32[3,2,192,128]{3,2,1,0:T(8,128)S(1)}, f32[3,2,192,128]{3,2,1,0:T(8,128)S(1)}, u32[]{:S(2)}, u32[]{:S(2)}) collective-permute-start(f32[3,2,192,128]{3,2,1,0:T(8,128)S(1)} %get-tuple-element.49.refs_2_.refs_1_), channel_id=1, source_target_pairs={{0,8},{8,0},{16,24},{24,16},{32,40},{40,32},{48,56},{56,48},{64,72... | collective-permute-start | bytes 1769480 | tf_op jit(solution)/shard_map/ppermute | solution.py:352
  66.9 7.8 %all_to_all.26 = f32[2,16,128]{2,1,0:T(8,128)S(1)} all-to-all(f32[2,16,128]{2,1,0:T(8,128)S(1)} %bitcast.19), channel_id=1, replica_groups={{8,16},{24,32},{40,48},{56,64},{72,80},{88,96},{104,112},{120,128},{136..., dimensions={0} | all-to-all | bytes 32768 | tf_op jit(solution)/shard_map/all_to_all | solution.py:347
  74.7 0.9 %shard_map.44 = (f32[3,2,192,128]{3,2,1,0:T(8,128)S(1)}, f32[192,192]{1,0:T(8,128)S(1)}) custom-call(f32[1]{0:T(128)S(6)} %copy.4.refs_0_, f32[3,192,192]{2,1,0:T(8,128)} %refs_1_.5, f32[3,2,192,128]{3,2,1,0:T(8,128)S(1)} %get-tuple-element.49.refs_2_.refs_1_, f32[4,8,128]{2,1,0:T(8,128)S(1)} %get-tuple-element.50.refs_3_, ...), custom_call_target="tpu_custom_call" | custom-call | flops 100000000 | bytes 4194304 | tf_op jit(solution)/shard_map/pallas_call | solution.py:305
  75.6 0.0 collective-permute-done.6.refs_2_
  75.6 0.0 collective-permute-done.7.refs_3_
  75.6 0.9 %shard_map.45 = (f32[3,2,192,128]{3,2,1,0:T(8,128)S(1)}, f32[2,192,128]{2,1,0:T(8,128)S(1)}, f32[8,2,8,128]{3,2,1,0:T(8,128)S(1)}) custom-call(f32[1]{0:T(128)S(6)} %copy.4.refs_0_, f32[3,2,192,128]{3,2,1,0:T(8,128)S(1)} %get-tuple-element.49.refs_2_.refs_1_, f32[3,2,192,128]{3,2,1,0:T(8,128)S(1)} %collective-permute-done.6.refs_2_, ...), custom_call_target="tpu_custom_call" | custom-call | flops 1000000000 | bytes 4194304 | tf_op jit(solution)/shard_map/pallas_call | solution.py:305
  76.6 13.2 %all_to_all.27 = f32[8,16,128]{2,1,0:T(8,128)S(1)} all-to-all(f32[8,16,128]{2,1,0:T(8,128)S(1)} %bitcast.17), channel_id=1, replica_groups=mesh['gx'=64,'gy'=8] {'gy'}, dimensions={0} | all-to-all | bytes 131072 | tf_op jit(solution)/shard_map/all_to_all | solution.py:322
  89.8 1.0 %shard_map.46 = f32[3,2,192,128]{3,2,1,0:T(8,128)} custom-call(f32[8,2,8,128]{3,2,1,0:T(8,128)S(1)} %bitcast.12, f32[3,2,192,128]{3,2,1,0:T(8,128)S(1)} %get-tuple-element.57.g_ref, f32[2,192,128]{2,1,0:T(8,128)S(1)} %get-tuple-element.58.vw_ref), custom_call_target="tpu_custom_call" | custom-call | flops 100000000 | bytes 4194304 | tf_op jit(solution)/shard_map/pallas_call | solution.py:305
Async XLA Ops:
  0.0 25.2 %collective-permute-start = (f32[3,2,192,128]{3,2,1,0:T(8,128)}, f32[3,2,192,128]{3,2,1,0:T(8,128)S(1)}, u32[]{:S(2)}, u32[]{:S(2)}) collective-permute-start(f32[3,2,192,128]{3,2,1,0:T(8,128)} %velocity.1), channel_id=1, source_target_pairs={{8,16},{16,8},{24,32},{32,24},{40,48},{48,40},{56,64},{64,56},{72,... | collective-permute-start | bytes 1769480 | tf_op jit(solution)/shard_map/ppermute | solution.py:338
  13.8 11.4 %collective-permute-start.1 = (f32[3,2,192,128]{3,2,1,0:T(8,128)S(1)}, f32[3,2,192,128]{3,2,1,0:T(8,128)S(1)}, u32[]{:S(2)}, u32[]{:S(2)}) collective-permute-start(f32[3,2,192,128]{3,2,1,0:T(8,128)S(1)} %get-tuple-element.32.refs_2_.refs_1_), channel_id=1, source_target_pairs={{0,8},{8,0},{16,24},{24,16},{32,40},{40,32},{48,56},{56,48},{64,72... | collective-permute-start | bytes 1769480 | tf_op jit(solution)/shard_map/ppermute | solution.py:352
  15.7 7.0 %collective-permute-start.3 = (f32[3,2,16,128]{3,2,1,0:T(8,128)S(1)}, f32[3,2,16,128]{3,2,1,0:T(8,128)S(1)}, u32[]{:S(2)}, u32[]{:S(2)}) collective-permute-start(f32[3,2,16,128]{3,2,1,0:T(8,128)S(1)} %get-tuple-element.35), channel_id=1, source_target_pairs={{1,2},{2,1},{3,4},{4,3},{5,6},{6,5},{9,10},{10,9},{11,12},{12,11},... | collective-permute-start | bytes 147464 | tf_op jit(solution)/shard_map/ppermute | solution.py:342
  19.2 6.0 %collective-permute-start.2 = (f32[3,2,16,128]{3,2,1,0:T(8,128)S(1)}, f32[3,2,16,128]{3,2,1,0:T(8,128)S(1)}, u32[]{:S(2)}, u32[]{:S(2)}) collective-permute-start(f32[3,2,16,128]{3,2,1,0:T(8,128)S(1)} %get-tuple-element.35), channel_id=1, source_target_pairs={{0,1},{1,0},{2,3},{3,2},{4,5},{5,4},{6,7},{7,6},{8,9},{9,8},{10,11... | collective-permute-start | bytes 147464 | tf_op jit(solution)/shard_map/ppermute | solution.py:341
  26.6 13.8 %all-to-all-start = ((f32[8,24,128]{2,1,0:T(8,128)}), f32[8,24,128]{2,1,0:T(8,128)S(1)}, u32[]{:S(2)}, u32[]{:S(2)}) async-start(f32[8,24,128]{2,1,0:T(8,128)} %bitcast), calls=%async_computation | async-start | bytes 196608 | tf_op jit(solution)/shard_map/all_to_all | solution.py:322
  33.1 18.1 %collective-permute-start.4 = (f32[3,2,192,128]{3,2,1,0:T(8,128)S(1)}, f32[3,2,192,128]{3,2,1,0:T(8,128)S(1)}, u32[]{:S(2)}, u32[]{:S(2)}) collective-permute-start(f32[3,2,192,128]{3,2,1,0:T(8,128)S(1)} %get-tuple-element.37.g_ref), channel_id=1, source_target_pairs={{8,16},{16,8},{24,32},{32,24},{40,48},{48,40},{56,64},{64,56},{72,... | collective-permute-start | bytes 1769480 | tf_op jit(solution)/shard_map/ppermute | solution.py:370
  40.6 10.6 %collective-permute-start.5 = (f32[3,2,192,128]{3,2,1,0:T(8,128)S(1)}, f32[3,2,192,128]{3,2,1,0:T(8,128)S(1)}, u32[]{:S(2)}, u32[]{:S(2)}) collective-permute-start(f32[3,2,192,128]{3,2,1,0:T(8,128)S(1)} %get-tuple-element.39.refs_2_.refs_1_), channel_id=1, source_target_pairs={{0,8},{8,0},{16,24},{24,16},{32,40},{40,32},{48,56},{56,48},{64,72... | collective-permute-start | bytes 1769480 | tf_op jit(solution)/shard_map/ppermute | solution.py:352
  52.7 12.0 %all-to-all-start.2 = ((f32[8,24,128]{2,1,0:T(8,128)}), f32[8,24,128]{2,1,0:T(8,128)S(1)}, u32[]{:S(2)}, u32[]{:S(2)}) async-start(f32[8,24,128]{2,1,0:T(8,128)} %bitcast.4), calls=%async_computation.2 | async-start | bytes 196608 | tf_op jit(solution)/shard_map/all_to_all | solution.py:322
  57.4 18.2 %collective-permute-start.6 = (f32[3,2,192,128]{3,2,1,0:T(8,128)S(1)}, f32[3,2,192,128]{3,2,1,0:T(8,128)S(1)}, u32[]{:S(2)}, u32[]{:S(2)}) collective-permute-start(f32[3,2,192,128]{3,2,1,0:T(8,128)S(1)} %get-tuple-element.47.g_ref), channel_id=1, source_target_pairs={{8,16},{16,8},{24,32},{32,24},{40,48},{48,40},{56,64},{64,56},{72,... | collective-permute-start | bytes 1769480 | tf_op jit(solution)/shard_map/ppermute | solution.py:370
  64.9 10.7 %collective-permute-start.7 = (f32[3,2,192,128]{3,2,1,0:T(8,128)S(1)}, f32[3,2,192,128]{3,2,1,0:T(8,128)S(1)}, u32[]{:S(2)}, u32[]{:S(2)}) collective-permute-start(f32[3,2,192,128]{3,2,1,0:T(8,128)S(1)} %get-tuple-element.49.refs_2_.refs_1_), channel_id=1, source_target_pairs={{0,8},{8,0},{16,24},{24,16},{32,40},{40,32},{48,56},{56,48},{64,72... | collective-permute-start | bytes 1769480 | tf_op jit(solution)/shard_map/ppermute | solution.py:352

commit v6 on v5

--- a/solution.py
+++ b/solution.py
@@ -55,7 +55,7 @@
         stiff_ref, inverses, u_ref, *refs = refs
         ends_ref = old_ref = None
     else:
-        stiff_ref, inverses, u_ref, ends_ref, old_share, old_ref, _, *refs = refs
+        stiff_ref, inverses, u_ref, ends_ref, old_share, old_ref, *refs = refs
     if step < SUBSTEPS - 1:
         part_ref, inv_ref, share_ref, pad, sem = refs
     else:
@@ -120,7 +120,6 @@
         adv_ref = None
     own = lax.axis_index("gy")
     odd = lax.rem(lax.axis_index("gx"), 2) > 0
-    partner = jnp.where(odd, 1, 0)
     stiff = stiff_ref[0]
 
     for r in range(0, CY, CHUNK):
@@ -129,13 +128,12 @@
         minus = [2.0 * courant[0] * jnp.minimum(u_ref[0, x, rows, :], 0.0) for x in range(2)]
         if step > 0:
             v, w = old_vw[0, rows, :], old_vw[1, rows, :]
-            low_far, high_far = far_lf[partner, 0], far_lf[partner, 1]
         for c in range(3):
             away = [far[c, x, rows, :] for x in range(2)]
             if step > 0:
                 for x in range(2):
                     line = 2 * c + x
-                    away[x] = away[x] - v * low_far[line : line + 1, :] - w * high_far[line : line + 1, :]
+                    away[x] = away[x] - v * far_lf[0, line : line + 1, :] - w * far_lf[1, line : line + 1, :]
             close = [near[c, x, rows, :] for x in range(2)]
             low = [jnp.where(odd, close[x], away[x]) for x in range(2)]
             high = [jnp.where(odd, away[x], close[x]) for x in range(2)]
@@ -280,9 +278,8 @@
         for c in range(3):
             pltpu.make_async_copy(u_ref.at[c], out_ref.at[c], sems.at[c]).wait()
     if ends_ref is not None:
-        for side in range(2):
-            lf_ref[side, 0] = lower
-            lf_ref[side, 1] = upper
+        lf_ref[0] = lower
+        lf_ref[1] = upper
         before = jnp.maximum(own - 1, 0)
         behind = jnp.minimum(own + 1, 7)
         row = got[before, 2]
@@ -343,11 +340,8 @@
             own_args = [current]
             more_args = [pair_y, other_y]
         else:
-            pairs = [[a, (a + 1) % gx] for a in range(1, gx, 2)]
-            far_lf = lax.all_to_all(
-                lf.reshape(2, 16, LANES), "gx", split_axis=0, concat_axis=0, axis_index_groups=pairs
-            ).reshape(2, 2, 8, LANES)
-            own_args = [current, ends, share, adv, far_lf]
+            far_lf = lax.ppermute(lf, "gx", across)
+            own_args = [current, ends, share, adv]
             more_args = [far_lf, vw]
         near = lax.ppermute(current, "gx", inside)
         pad = [scratch(3, 2, CY + 16, LANES), pltpu.SemaphoreType.DMA]
@@ -374,7 +368,7 @@
             outs = [jax.ShapeDtypeStruct((3, 2, CY, LANES), jnp.float32)]
             edge = edge + [scratch(3, 2, CY, LANES), pltpu.SemaphoreType.DMA((3,))]
             return call(correct, [got, g, vw], outs, edge, 10**8, hbm_outs=1)[0]
-        outs = [field, f32(4, 8, LANES), f32(2, 2, 8, LANES)]
+        outs = [field, f32(4, 8, LANES), f32(2, 8, LANES)]
         current, ends, lf = call(correct, [got, g, vw], outs, edge, 10**8)
 
 

time: 91.4 us -> 88.1 us (0.964)
  blocking collectives: 28.7 us -> 10.8 us
  waiting for transfers between devices: 7.79 us -> 19.6 us
  starting transfers between devices: 44.2 us -> 47.1 us
    all_to_all x2 -> x0, blocking collectives: 15.5 us -> none  [body(): lax.all_to_all(lf.reshape(2, 16, LANES), 'gx', split_axis=0, concat_axis=...]
    ppermute x0 -> x2, waiting for transfers between devices: none -> 8.7 us  [body(): far_lf = lax.ppermute(lf, 'gx', across)]
    ppermute x0 -> x2, starting transfers between devices: none -> 5.94 us  [body(): far_lf = lax.ppermute(lf, 'gx', across)]
    ppermute x2, starting transfers between devices: 9.22 us -> 6.1 us  [body(): far = lax.ppermute(g, 'gx', across)]
    all_to_all x2, waiting for transfers between devices: 5.33 us -> 8.46 us  [exchange(): lax.all_to_all(flat, 'gy', split_axis=0, concat_axis=0).reshape(send.shape)]
    all_to_all x1, blocking collectives: 13.2 us -> 10.8 us  [exchange(): lax.all_to_all(flat, 'gy', split_axis=0, concat_axis=0).reshape(send.shape)]
  transfers between devices with their start and end apart: 10 -> 12, of which waited for: 3 -> 5; matrix products, arithmetic and copies ran while one was open for 0% -> 0% of each run, Pallas kernels for 5% -> 5%
where the time goes in v6:
time: 88.1 us; the launch traced here: 87.5 us
  starting transfers between devices  47.1 us (53%)
  waiting for transfers between devices  19.6 us (22%)
  blocking collectives  10.8 us (12%)
  Pallas kernels  9.22 us (10%)
    ppermute x1, starting transfers between devices, body(): far = lax.ppermute(velocity, 'gx', across)  12.6 us
    all_to_all x2, starting transfers between devices, exchange(): lax.all_to_all(flat, 'gy', split_axis=0, concat_axis=0).reshape(send.shape)  11.3 us
    all_to_all x1, blocking collectives, exchange(): lax.all_to_all(flat, 'gy', split_axis=0, concat_axis=0).reshape(send.shape)  10.8 us
    pallas_call x10, Pallas kernels, call(): pl.pallas_call(kernel, out_shape=outs, in_specs=[SMEM] * len(scalars) + [...  9.22 us
    ppermute x2, waiting for transfers between devices, body(): far_lf = lax.ppermute(lf, 'gx', across)  8.7 us
    all_to_all x2, waiting for transfers between devices, exchange(): lax.all_to_all(flat, 'gy', split_axis=0, concat_axis=0).reshape(send.shape)  8.46 us
    ppermute x2, starting transfers between devices, body(): far = lax.ppermute(g, 'gx', across)  6.1 us
    ppermute x2, starting transfers between devices, body(): far_lf = lax.ppermute(lf, 'gx', across)  5.94 us
  transfers between devices with their start and end apart: 12, of which 5 were waited for; matrix products, arithmetic and copies ran while one was open for 0% of the time, Pallas kernels for 5%

profile of v6, /device:TPU:8, one launch (start us, length us, event | category | flops | bytes accessed | tf_op | source)
XLA Modules:
  0.0 87.5 jit_solution(626874194777254679)
XLA Ops:
  0.0 12.6 %collective-permute-start = (f32[3,2,192,128]{3,2,1,0:T(8,128)}, f32[3,2,192,128]{3,2,1,0:T(8,128)S(1)}, u32[]{:S(2)}, u32[]{:S(2)}) collective-permute-start(f32[3,2,192,128]{3,2,1,0:T(8,128)} %velocity.1), channel_id=1, source_target_pairs={{8,16},{16,8},{24,32},{32,24},{40,48},{48,40},{56,64},{64,56},{72,... | collective-permute-start | bytes 1769480 | tf_op jit(solution)/shard_map/ppermute | solution.py:335
  12.6 1.2 %shard_map.37 = (f32[3,2,192,128]{3,2,1,0:T(8,128)S(1)}, f32[3,2,16,128]{3,2,1,0:T(8,128)S(1)}) custom-call(f32[3,2,192,128]{3,2,1,0:T(8,128)} %velocity.1), custom_call_target="tpu_custom_call" | custom-call | flops 1000000 | bytes 4194304 | tf_op jit(solution)/shard_map/pallas_call | solution.py:302
  13.8 1.9 %collective-permute-start.1 = (f32[3,2,192,128]{3,2,1,0:T(8,128)S(1)}, f32[3,2,192,128]{3,2,1,0:T(8,128)S(1)}, u32[]{:S(2)}, u32[]{:S(2)}) collective-permute-start(f32[3,2,192,128]{3,2,1,0:T(8,128)S(1)} %get-tuple-element.32.refs_2_.refs_1_), channel_id=1, source_target_pairs={{0,8},{8,0},{16,24},{24,16},{32,40},{40,32},{48,56},{56,48},{64,72... | collective-permute-start | bytes 1769480 | tf_op jit(solution)/shard_map/ppermute | solution.py:346
  15.7 3.5 %collective-permute-start.3 = (f32[3,2,16,128]{3,2,1,0:T(8,128)S(1)}, f32[3,2,16,128]{3,2,1,0:T(8,128)S(1)}, u32[]{:S(2)}, u32[]{:S(2)}) collective-permute-start(f32[3,2,16,128]{3,2,1,0:T(8,128)S(1)} %get-tuple-element.35), channel_id=1, source_target_pairs={{1,2},{2,1},{3,4},{4,3},{5,6},{6,5},{9,10},{10,9},{11,12},{12,11},... | collective-permute-start | bytes 147464 | tf_op jit(solution)/shard_map/ppermute | solution.py:339
  19.2 1.9 %collective-permute-start.2 = (f32[3,2,16,128]{3,2,1,0:T(8,128)S(1)}, f32[3,2,16,128]{3,2,1,0:T(8,128)S(1)}, u32[]{:S(2)}, u32[]{:S(2)}) collective-permute-start(f32[3,2,16,128]{3,2,1,0:T(8,128)S(1)} %get-tuple-element.35), channel_id=1, source_target_pairs={{0,1},{1,0},{2,3},{3,2},{4,5},{5,4},{6,7},{7,6},{8,9},{9,8},{10,11... | collective-permute-start | bytes 147464 | tf_op jit(solution)/shard_map/ppermute | solution.py:338
  21.8 1.0 %shard_map.38 = (f32[3,2,192,128]{3,2,1,0:T(8,128)S(1)}, f32[192,192]{1,0:T(8,128)S(1)}, f32[3,2,192,128]{3,2,1,0:T(8,128)S(1)}) custom-call(f32[1]{0:T(128)S(6)} %copy.4.refs_0_, f32[3,192,192]{2,1,0:T(8,128)} %refs_1_.5, f32[3,2,192,128]{3,2,1,0:T(8,128)S(1)} %get-tuple-element.32.refs_2_.refs_1_), custom_call_target="tpu_custom_call" | custom-call | flops 100000000 | bytes 4194304 | tf_op jit(solution)/shard_map/pallas_call | solution.py:302
  22.7 0.0 collective-permute-done.3.refs_7_
  22.7 2.4 %collective-permute-done.2.refs_6_ = f32[3,2,16,128]{3,2,1,0:T(8,128)S(1)} collective-permute-done((f32[3,2,16,128]{3,2,1,0:T(8,128)S(1)}, f32[3,2,16,128]{3,2,1,0:T(8,128)S(1)}, u32[]{:S(2)}, u32[]{:S(2)}) %collective-permute-start.2) | collective-permute-done | bytes 49184 | tf_op jit(solution)/shard_map/ppermute | solution.py:338
  25.2 0.0 collective-permute-done.refs_2_
  25.2 0.0 collective-permute-done.1.refs_3_
  25.2 1.4 %shard_map.39 = (f32[3,2,192,128]{3,2,1,0:T(8,128)S(1)}, f32[2,192,128]{2,1,0:T(8,128)S(1)}, f32[3,2,192,128]{3,2,1,0:T(8,128)S(1)}, f32[8,3,8,128]{3,2,1,0:T(8,128)}) custom-call(f32[1]{0:T(128)S(6)} %copy.4.refs_0_, f32[3,2,192,128]{3,2,1,0:T(8,128)S(1)} %get-tuple-element.32.refs_2_.refs_1_, f32[3,2,192,128]{3,2,1,0:T(8,128)S(1)} %collective-permute-done.refs_2_, ...), custom_call_target="tpu_custom_call" | custom-call | flops 1000000000 | bytes 4194304 | tf_op jit(solution)/shard_map/pallas_call | solution.py:302
  26.6 6.5 %all-to-all-start = ((f32[8,24,128]{2,1,0:T(8,128)}), f32[8,24,128]{2,1,0:T(8,128)S(1)}, u32[]{:S(2)}, u32[]{:S(2)}) async-start(f32[8,24,128]{2,1,0:T(8,128)} %bitcast), calls=%async_computation | async-start | bytes 196608 | tf_op jit(solution)/shard_map/all_to_all | solution.py:319
  33.1 2.6 %collective-permute-start.4 = (f32[3,2,192,128]{3,2,1,0:T(8,128)S(1)}, f32[3,2,192,128]{3,2,1,0:T(8,128)S(1)}, u32[]{:S(2)}, u32[]{:S(2)}) collective-permute-start(f32[3,2,192,128]{3,2,1,0:T(8,128)S(1)} %get-tuple-element.37.g_ref), channel_id=1, source_target_pairs={{8,16},{16,8},{24,32},{32,24},{40,48},{48,40},{56,64},{64,56},{72,... | collective-permute-start | bytes 1769480 | tf_op jit(solution)/shard_map/ppermute | solution.py:364
  35.7 4.7 %all-to-all-done = f32[8,24,128]{2,1,0:T(8,128)S(1)} async-done(((f32[8,24,128]{2,1,0:T(8,128)}), f32[8,24,128]{2,1,0:T(8,128)S(1)}, u32[]{:S(2)}, u32[]{:S(2)}) %all-to-all-start) | async-done | bytes 98336 | tf_op jit(solution)/shard_map/all_to_all | solution.py:319
  40.4 0.2 shard_map.40
  40.6 1.9 %collective-permute-start.5 = (f32[3,2,192,128]{3,2,1,0:T(8,128)S(1)}, f32[3,2,192,128]{3,2,1,0:T(8,128)S(1)}, u32[]{:S(2)}, u32[]{:S(2)}) collective-permute-start(f32[3,2,192,128]{3,2,1,0:T(8,128)S(1)} %get-tuple-element.39.refs_2_.refs_1_), channel_id=1, source_target_pairs={{0,8},{8,0},{16,24},{24,16},{32,40},{40,32},{48,56},{56,48},{64,72... | collective-permute-start | bytes 1769480 | tf_op jit(solution)/shard_map/ppermute | solution.py:346
  42.6 3.3 %collective-permute-start.6 = (f32[2,8,128]{2,1,0:T(8,128)S(1)}, f32[2,8,128]{2,1,0:T(8,128)S(1)}, u32[]{:S(2)}, u32[]{:S(2)}) collective-permute-start(f32[2,8,128]{2,1,0:T(8,128)S(1)} %get-tuple-element.45), channel_id=1, source_target_pairs={{8,16},{16,8},{24,32},{32,24},{40,48},{48,40},{56,64},{64,56},{72,... | collective-permute-start | bytes 24584 | tf_op jit(solution)/shard_map/ppermute | solution.py:343
  45.9 1.0 %shard_map.41 = (f32[3,2,192,128]{3,2,1,0:T(8,128)S(1)}, f32[192,192]{1,0:T(8,128)S(1)}, f32[3,2,192,128]{3,2,1,0:T(8,128)S(1)}) custom-call(f32[1]{0:T(128)S(6)} %copy.4.refs_0_, f32[3,192,192]{2,1,0:T(8,128)} %refs_1_.5, f32[3,2,192,128]{3,2,1,0:T(8,128)S(1)} %get-tuple-element.39.refs_2_.refs_1_, f32[4,8,128]{2,1,0:T(8,128)S(1)} %get-tuple-element.40.refs_3_, ...), custom_call_target="tpu_custom_call" | custom-call | flops 100000000 | bytes 4194304 | tf_op jit(solution)/shard_map/pallas_call | solution.py:302
  46.8 4.0 %collective-permute-done.6.refs_6_ = f32[2,8,128]{2,1,0:T(8,128)S(1)} collective-permute-done((f32[2,8,128]{2,1,0:T(8,128)S(1)}, f32[2,8,128]{2,1,0:T(8,128)S(1)}, u32[]{:S(2)}, u32[]{:S(2)}) %collective-permute-start.6) | collective-permute-done | bytes 8224 | tf_op jit(solution)/shard_map/ppermute | solution.py:343
  50.8 0.0 collective-permute-done.4.refs_2_
  50.9 0.0 collective-permute-done.5.refs_3_
  50.9 1.4 %shard_map.42 = (f32[3,2,192,128]{3,2,1,0:T(8,128)S(1)}, f32[2,192,128]{2,1,0:T(8,128)S(1)}, f32[3,2,192,128]{3,2,1,0:T(8,128)S(1)}, f32[8,3,8,128]{3,2,1,0:T(8,128)}) custom-call(f32[1]{0:T(128)S(6)} %copy.4.refs_0_, f32[3,2,192,128]{3,2,1,0:T(8,128)S(1)} %get-tuple-element.39.refs_2_.refs_1_, f32[3,2,192,128]{3,2,1,0:T(8,128)S(1)} %collective-permute-done.4.refs_2_, ...), custom_call_target="tpu_custom_call" | custom-call | flops 1000000000 | bytes 4194304 | tf_op jit(solution)/shard_map/pallas_call | solution.py:302
  52.3 4.7 %all-to-all-start.1 = ((f32[8,24,128]{2,1,0:T(8,128)}), f32[8,24,128]{2,1,0:T(8,128)S(1)}, u32[]{:S(2)}, u32[]{:S(2)}) async-start(f32[8,24,128]{2,1,0:T(8,128)} %bitcast.2), calls=%async_computation.1 | async-start | bytes 196608 | tf_op jit(solution)/shard_map/all_to_all | solution.py:319
  57.0 3.5 %collective-permute-start.7 = (f32[3,2,192,128]{3,2,1,0:T(8,128)S(1)}, f32[3,2,192,128]{3,2,1,0:T(8,128)S(1)}, u32[]{:S(2)}, u32[]{:S(2)}) collective-permute-start(f32[3,2,192,128]{3,2,1,0:T(8,128)S(1)} %get-tuple-element.47.g_ref), channel_id=1, source_target_pairs={{8,16},{16,8},{24,32},{32,24},{40,48},{48,40},{56,64},{64,56},{72,... | collective-permute-start | bytes 1769480 | tf_op jit(solution)/shard_map/ppermute | solution.py:364
  60.6 3.8 %all-to-all-done.1 = f32[8,24,128]{2,1,0:T(8,128)S(1)} async-done(((f32[8,24,128]{2,1,0:T(8,128)}), f32[8,24,128]{2,1,0:T(8,128)S(1)}, u32[]{:S(2)}, u32[]{:S(2)}) %all-to-all-start.1) | async-done | bytes 98336 | tf_op jit(solution)/shard_map/all_to_all | solution.py:319
  64.3 0.2 shard_map.43
  64.6 1.9 %collective-permute-start.8 = (f32[3,2,192,128]{3,2,1,0:T(8,128)S(1)}, f32[3,2,192,128]{3,2,1,0:T(8,128)S(1)}, u32[]{:S(2)}, u32[]{:S(2)}) collective-permute-start(f32[3,2,192,128]{3,2,1,0:T(8,128)S(1)} %get-tuple-element.49.refs_2_.refs_1_), channel_id=1, source_target_pairs={{0,8},{8,0},{16,24},{24,16},{32,40},{40,32},{48,56},{56,48},{64,72... | collective-permute-start | bytes 1769480 | tf_op jit(solution)/shard_map/ppermute | solution.py:346
  66.5 2.6 %collective-permute-start.9 = (f32[2,8,128]{2,1,0:T(8,128)S(1)}, f32[2,8,128]{2,1,0:T(8,128)S(1)}, u32[]{:S(2)}, u32[]{:S(2)}) collective-permute-start(f32[2,8,128]{2,1,0:T(8,128)S(1)} %get-tuple-element.55), channel_id=1, source_target_pairs={{8,16},{16,8},{24,32},{32,24},{40,48},{48,40},{56,64},{64,56},{72,... | collective-permute-start | bytes 24584 | tf_op jit(solution)/shard_map/ppermute | solution.py:343
  69.1 0.9 %shard_map.44 = (f32[3,2,192,128]{3,2,1,0:T(8,128)S(1)}, f32[192,192]{1,0:T(8,128)S(1)}) custom-call(f32[1]{0:T(128)S(6)} %copy.4.refs_0_, f32[3,192,192]{2,1,0:T(8,128)} %refs_1_.5, f32[3,2,192,128]{3,2,1,0:T(8,128)S(1)} %get-tuple-element.49.refs_2_.refs_1_, f32[4,8,128]{2,1,0:T(8,128)S(1)} %get-tuple-element.50.refs_3_, ...), custom_call_target="tpu_custom_call" | custom-call | flops 100000000 | bytes 4194304 | tf_op jit(solution)/shard_map/pallas_call | solution.py:302
  70.1 4.7 %collective-permute-done.9.refs_6_ = f32[2,8,128]{2,1,0:T(8,128)S(1)} collective-permute-done((f32[2,8,128]{2,1,0:T(8,128)S(1)}, f32[2,8,128]{2,1,0:T(8,128)S(1)}, u32[]{:S(2)}, u32[]{:S(2)}) %collective-permute-start.9) | collective-permute-done | bytes 8224 | tf_op jit(solution)/shard_map/ppermute | solution.py:343
  74.8 0.0 collective-permute-done.7.refs_2_
  74.8 0.0 collective-permute-done.8.refs_3_
  74.8 0.9 %shard_map.45 = (f32[3,2,192,128]{3,2,1,0:T(8,128)S(1)}, f32[2,192,128]{2,1,0:T(8,128)S(1)}, f32[8,2,8,128]{3,2,1,0:T(8,128)S(1)}) custom-call(f32[1]{0:T(128)S(6)} %copy.4.refs_0_, f32[3,2,192,128]{3,2,1,0:T(8,128)S(1)} %get-tuple-element.49.refs_2_.refs_1_, f32[3,2,192,128]{3,2,1,0:T(8,128)S(1)} %collective-permute-done.7.refs_2_, ...), custom_call_target="tpu_custom_call" | custom-call | flops 1000000000 | bytes 4194304 | tf_op jit(solution)/shard_map/pallas_call | solution.py:302
  75.7 10.8 %all_to_all.15 = f32[8,16,128]{2,1,0:T(8,128)S(1)} all-to-all(f32[8,16,128]{2,1,0:T(8,128)S(1)} %bitcast.9), channel_id=1, replica_groups=mesh['gx'=64,'gy'=8] {'gy'}, dimensions={0} | all-to-all | bytes 131072 | tf_op jit(solution)/shard_map/all_to_all | solution.py:319
  86.5 1.0 %shard_map.46 = f32[3,2,192,128]{3,2,1,0:T(8,128)} custom-call(f32[8,2,8,128]{3,2,1,0:T(8,128)S(1)} %bitcast.8, f32[3,2,192,128]{3,2,1,0:T(8,128)S(1)} %get-tuple-element.57.g_ref, f32[2,192,128]{2,1,0:T(8,128)S(1)} %get-tuple-element.58.vw_ref), custom_call_target="tpu_custom_call" | custom-call | flops 100000000 | bytes 4194304 | tf_op jit(solution)/shard_map/pallas_call | solution.py:302
Async XLA Ops:
  0.0 25.2 %collective-permute-start = (f32[3,2,192,128]{3,2,1,0:T(8,128)}, f32[3,2,192,128]{3,2,1,0:T(8,128)S(1)}, u32[]{:S(2)}, u32[]{:S(2)}) collective-permute-start(f32[3,2,192,128]{3,2,1,0:T(8,128)} %velocity.1), channel_id=1, source_target_pairs={{8,16},{16,8},{24,32},{32,24},{40,48},{48,40},{56,64},{64,56},{72,... | collective-permute-start | bytes 1769480 | tf_op jit(solution)/shard_map/ppermute | solution.py:335
  13.8 11.4 %collective-permute-start.1 = (f32[3,2,192,128]{3,2,1,0:T(8,128)S(1)}, f32[3,2,192,128]{3,2,1,0:T(8,128)S(1)}, u32[]{:S(2)}, u32[]{:S(2)}) collective-permute-start(f32[3,2,192,128]{3,2,1,0:T(8,128)S(1)} %get-tuple-element.32.refs_2_.refs_1_), channel_id=1, source_target_pairs={{0,8},{8,0},{16,24},{24,16},{32,40},{40,32},{48,56},{56,48},{64,72... | collective-permute-start | bytes 1769480 | tf_op jit(solution)/shard_map/ppermute | solution.py:346
  15.7 7.0 %collective-permute-start.3 = (f32[3,2,16,128]{3,2,1,0:T(8,128)S(1)}, f32[3,2,16,128]{3,2,1,0:T(8,128)S(1)}, u32[]{:S(2)}, u32[]{:S(2)}) collective-permute-start(f32[3,2,16,128]{3,2,1,0:T(8,128)S(1)} %get-tuple-element.35), channel_id=1, source_target_pairs={{1,2},{2,1},{3,4},{4,3},{5,6},{6,5},{9,10},{10,9},{11,12},{12,11},... | collective-permute-start | bytes 147464 | tf_op jit(solution)/shard_map/ppermute | solution.py:339
  19.2 6.0 %collective-permute-start.2 = (f32[3,2,16,128]{3,2,1,0:T(8,128)S(1)}, f32[3,2,16,128]{3,2,1,0:T(8,128)S(1)}, u32[]{:S(2)}, u32[]{:S(2)}) collective-permute-start(f32[3,2,16,128]{3,2,1,0:T(8,128)S(1)} %get-tuple-element.35), channel_id=1, source_target_pairs={{0,1},{1,0},{2,3},{3,2},{4,5},{5,4},{6,7},{7,6},{8,9},{9,8},{10,11... | collective-permute-start | bytes 147464 | tf_op jit(solution)/shard_map/ppermute | solution.py:338
  26.6 13.8 %all-to-all-start = ((f32[8,24,128]{2,1,0:T(8,128)}), f32[8,24,128]{2,1,0:T(8,128)S(1)}, u32[]{:S(2)}, u32[]{:S(2)}) async-start(f32[8,24,128]{2,1,0:T(8,128)} %bitcast), calls=%async_computation | async-start | bytes 196608 | tf_op jit(solution)/shard_map/all_to_all | solution.py:319
  33.1 17.7 %collective-permute-start.4 = (f32[3,2,192,128]{3,2,1,0:T(8,128)S(1)}, f32[3,2,192,128]{3,2,1,0:T(8,128)S(1)}, u32[]{:S(2)}, u32[]{:S(2)}) collective-permute-start(f32[3,2,192,128]{3,2,1,0:T(8,128)S(1)} %get-tuple-element.37.g_ref), channel_id=1, source_target_pairs={{8,16},{16,8},{24,32},{32,24},{40,48},{48,40},{56,64},{64,56},{72,... | collective-permute-start | bytes 1769480 | tf_op jit(solution)/shard_map/ppermute | solution.py:364
  40.6 10.2 %collective-permute-start.5 = (f32[3,2,192,128]{3,2,1,0:T(8,128)S(1)}, f32[3,2,192,128]{3,2,1,0:T(8,128)S(1)}, u32[]{:S(2)}, u32[]{:S(2)}) collective-permute-start(f32[3,2,192,128]{3,2,1,0:T(8,128)S(1)} %get-tuple-element.39.refs_2_.refs_1_), channel_id=1, source_target_pairs={{0,8},{8,0},{16,24},{24,16},{32,40},{40,32},{48,56},{56,48},{64,72... | collective-permute-start | bytes 1769480 | tf_op jit(solution)/shard_map/ppermute | solution.py:346
  42.6 8.3 %collective-permute-start.6 = (f32[2,8,128]{2,1,0:T(8,128)S(1)}, f32[2,8,128]{2,1,0:T(8,128)S(1)}, u32[]{:S(2)}, u32[]{:S(2)}) collective-permute-start(f32[2,8,128]{2,1,0:T(8,128)S(1)} %get-tuple-element.45), channel_id=1, source_target_pairs={{8,16},{16,8},{24,32},{32,24},{40,48},{48,40},{56,64},{64,56},{72,... | collective-permute-start | bytes 24584 | tf_op jit(solution)/shard_map/ppermute | solution.py:343
  52.3 12.0 %all-to-all-start.1 = ((f32[8,24,128]{2,1,0:T(8,128)}), f32[8,24,128]{2,1,0:T(8,128)S(1)}, u32[]{:S(2)}, u32[]{:S(2)}) async-start(f32[8,24,128]{2,1,0:T(8,128)} %bitcast.2), calls=%async_computation.1 | async-start | bytes 196608 | tf_op jit(solution)/shard_map/all_to_all | solution.py:319
  57.0 17.7 %collective-permute-start.7 = (f32[3,2,192,128]{3,2,1,0:T(8,128)S(1)}, f32[3,2,192,128]{3,2,1,0:T(8,128)S(1)}, u32[]{:S(2)}, u32[]{:S(2)}) collective-permute-start(f32[3,2,192,128]{3,2,1,0:T(8,128)S(1)} %get-tuple-element.47.g_ref), channel_id=1, source_target_pairs={{8,16},{16,8},{24,32},{32,24},{40,48},{48,40},{56,64},{64,56},{72,... | collective-permute-start | bytes 1769480 | tf_op jit(solution)/shard_map/ppermute | solution.py:364
  64.6 10.2 %collective-permute-start.8 = (f32[3,2,192,128]{3,2,1,0:T(8,128)S(1)}, f32[3,2,192,128]{3,2,1,0:T(8,128)S(1)}, u32[]{:S(2)}, u32[]{:S(2)}) collective-permute-start(f32[3,2,192,128]{3,2,1,0:T(8,128)S(1)} %get-tuple-element.49.refs_2_.refs_1_), channel_id=1, source_target_pairs={{0,8},{8,0},{16,24},{24,16},{32,40},{40,32},{48,56},{56,48},{64,72... | collective-permute-start | bytes 1769480 | tf_op jit(solution)/shard_map/ppermute | solution.py:346
  66.5 8.3 %collective-permute-start.9 = (f32[2,8,128]{2,1,0:T(8,128)S(1)}, f32[2,8,128]{2,1,0:T(8,128)S(1)}, u32[]{:S(2)}, u32[]{:S(2)}) collective-permute-start(f32[2,8,128]{2,1,0:T(8,128)S(1)} %get-tuple-element.55), channel_id=1, source_target_pairs={{8,16},{16,8},{24,32},{32,24},{40,48},{48,40},{56,64},{64,56},{72,... | collective-permute-start | bytes 24584 | tf_op jit(solution)/shard_map/ppermute | solution.py:343

commit v7 on v6

--- a/solution.py
+++ b/solution.py
@@ -38,10 +38,10 @@
     return [(c, x) for c in range(3) for x in range(2)]
 
 
-def pack_kernel(velocity, u_ref, rows_ref, sems):
+def pack_kernel(velocity, u_ref, top_ref, bottom_ref, sems):
     copies = [
-        pltpu.make_async_copy(velocity.at[:, :, pl.ds(0, 8), :], rows_ref.at[:, :, pl.ds(0, 8), :], sems.at[0]),
-        pltpu.make_async_copy(velocity.at[:, :, pl.ds(CY - 8, 8), :], rows_ref.at[:, :, pl.ds(8, 8), :], sems.at[1]),
+        pltpu.make_async_copy(velocity.at[:, :, pl.ds(0, 8), :], top_ref, sems.at[0]),
+        pltpu.make_async_copy(velocity.at[:, :, pl.ds(CY - 8, 8), :], bottom_ref, sems.at[1]),
         pltpu.make_async_copy(velocity, u_ref, sems.at[2]),
     ]
     for copy in copies:
@@ -112,7 +112,7 @@
     if step > 0:
         far_lf, old_vw, *refs = refs
     else:
-        pair_y, other_y, *refs = refs
+        before, behind, *refs = refs
     if step < SUBSTEPS - 1:
         g_ref, vw_ref, adv_ref, send_ref, rhs, packed, sems = refs
     else:
@@ -147,10 +147,8 @@
                     adv_ref[c, x, rows, :] = adv
 
     if step == 0:
-        odd_y = lax.rem(own, 2) > 0
         for c, x in lines():
-            low = jnp.where(odd_y, pair_y[c, x, 8:16, :], other_y[c, x, 8:16, :])
-            high = jnp.where(odd_y, other_y[c, x, 0:8, :], pair_y[c, x, 0:8, :])
+            low, high = before[c, x], behind[c, x]
             y2, y1, w1, w2 = low[6:7], low[7:8], high[0:1], high[1:2]
             for row, viscous, up, down in (
                 (0, y1, 0.25 * y2 - y1, None),
@@ -333,12 +331,12 @@
         last = step == SUBSTEPS - 1
         if step == 0:
             far = lax.ppermute(velocity, "gx", across)
-            outs = [field, f32(3, 2, 16, LANES)]
-            current, rows = call(pack_kernel, [], outs, [pltpu.SemaphoreType.DMA((3,))], 10**6, large=[velocity])
-            pair_y = lax.ppermute(rows, "gy", swaps(gy, 0, False))
-            other_y = lax.ppermute(rows, "gy", swaps(gy, 1, False))
+            outs = [field] + [f32(3, 2, 8, LANES)] * 2
+            current, top, bottom = call(pack_kernel, [], outs, [pltpu.SemaphoreType.DMA((3,))], 10**6, large=[velocity])
+            before = lax.ppermute(bottom, "gy", [(k, k + 1) for k in range(gy - 1)])
+            behind = lax.ppermute(top, "gy", [(k + 1, k) for k in range(gy - 1)])
             own_args = [current]
-            more_args = [pair_y, other_y]
+            more_args = [before, behind]
         else:
             far_lf = lax.ppermute(lf, "gx", across)
             own_args = [current, ends, share, adv]

time: 88.1 us -> 89.1 us (1.011)
    all_to_all x2, starting transfers between devices: 11.3 us -> 12.5 us  [exchange(): lax.all_to_all(flat, 'gy', split_axis=0, concat_axis=0).reshape(send.shape)]
where the time goes in v7:
time: 89.1 us; the launch traced here: 88.4 us
  starting transfers between devices  47.4 us (53%)
  waiting for transfers between devices  20.2 us (23%)
  blocking collectives  10.8 us (12%)
  Pallas kernels  9.22 us (10%)
    ppermute x1, starting transfers between devices, body(): far = lax.ppermute(velocity, 'gx', across)  12.6 us
    all_to_all x2, starting transfers between devices, exchange(): lax.all_to_all(flat, 'gy', split_axis=0, concat_axis=0).reshape(send.shape)  12.5 us
    all_to_all x1, blocking collectives, exchange(): lax.all_to_all(flat, 'gy', split_axis=0, concat_axis=0).reshape(send.shape)  10.8 us
    ppermute x2, waiting for transfers between devices, body(): far_lf = lax.ppermute(lf, 'gx', across)  9.29 us
    pallas_call x10, Pallas kernels, call(): pl.pallas_call(kernel, out_shape=outs, in_specs=[SMEM] * len(scalars) + [...  9.22 us
    all_to_all x2, waiting for transfers between devices, exchange(): lax.all_to_all(flat, 'gy', split_axis=0, concat_axis=0).reshape(send.shape)  9.12 us
    ppermute x3, starting transfers between devices, body(): near = lax.ppermute(current, 'gx', inside)  5.76 us
    ppermute x2, starting transfers between devices, body(): far = lax.ppermute(g, 'gx', across)  5.43 us
  transfers between devices with their start and end apart: 12, of which 5 were waited for; matrix products, arithmetic and copies ran while one was open for 0% of the time, Pallas kernels for 5%

profile of v7, /device:TPU:8, one launch (start us, length us, event | category | flops | bytes accessed | tf_op | source)
XLA Modules:
  0.0 88.4 jit_solution(2547366637061620135)
XLA Ops:
  0.0 12.6 %collective-permute-start = (f32[3,2,192,128]{3,2,1,0:T(8,128)}, f32[3,2,192,128]{3,2,1,0:T(8,128)S(1)}, u32[]{:S(2)}, u32[]{:S(2)}) collective-permute-start(f32[3,2,192,128]{3,2,1,0:T(8,128)} %velocity.1), channel_id=1, source_target_pairs={{8,16},{16,8},{24,32},{32,24},{40,48},{48,40},{56,64},{64,56},{72,... | collective-permute-start | bytes 1769480 | tf_op jit(solution)/shard_map/ppermute | solution.py:333
  12.6 1.2 %shard_map.37 = (f32[3,2,192,128]{3,2,1,0:T(8,128)S(1)}, f32[3,2,8,128]{3,2,1,0:T(8,128)S(1)}, f32[3,2,8,128]{3,2,1,0:T(8,128)S(1)}) custom-call(f32[3,2,192,128]{3,2,1,0:T(8,128)} %velocity.1), custom_call_target="tpu_custom_call" | custom-call | flops 1000000 | bytes 4194304 | tf_op jit(solution)/shard_map/pallas_call | solution.py:300
  13.8 1.9 %collective-permute-start.1 = (f32[3,2,192,128]{3,2,1,0:T(8,128)S(1)}, f32[3,2,192,128]{3,2,1,0:T(8,128)S(1)}, u32[]{:S(2)}, u32[]{:S(2)}) collective-permute-start(f32[3,2,192,128]{3,2,1,0:T(8,128)S(1)} %get-tuple-element.33.refs_2_.refs_1_), channel_id=1, source_target_pairs={{0,8},{8,0},{16,24},{24,16},{32,40},{40,32},{48,56},{56,48},{64,72... | collective-permute-start | bytes 1769480 | tf_op jit(solution)/shard_map/ppermute | solution.py:344
  15.7 3.5 %collective-permute-start.2 = (f32[3,2,8,128]{3,2,1,0:T(8,128)S(1)}, f32[3,2,8,128]{3,2,1,0:T(8,128)S(1)}, u32[]{:S(2)}, u32[]{:S(2)}) collective-permute-start(f32[3,2,8,128]{3,2,1,0:T(8,128)S(1)} %get-tuple-element.36), channel_id=1, source_target_pairs={{0,1},{1,2},{2,3},{3,4},{4,5},{5,6},{6,7},{8,9},{9,10},{10,11},{11... | collective-permute-start | bytes 73736 | tf_op jit(solution)/shard_map/ppermute | solution.py:336
  19.2 2.4 %collective-permute-start.3 = (f32[3,2,8,128]{3,2,1,0:T(8,128)S(1)}, f32[3,2,8,128]{3,2,1,0:T(8,128)S(1)}, u32[]{:S(2)}, u32[]{:S(2)}) collective-permute-start(f32[3,2,8,128]{3,2,1,0:T(8,128)S(1)} %get-tuple-element.37), channel_id=1, source_target_pairs={{1,0},{2,1},{3,2},{4,3},{5,4},{6,5},{7,6},{9,8},{10,9},{11,10},{12... | collective-permute-start | bytes 73736 | tf_op jit(solution)/shard_map/ppermute | solution.py:337
  22.2 1.0 %shard_map.38 = (f32[3,2,192,128]{3,2,1,0:T(8,128)S(1)}, f32[192,192]{1,0:T(8,128)S(1)}, f32[3,2,192,128]{3,2,1,0:T(8,128)S(1)}) custom-call(f32[1]{0:T(128)S(6)} %copy.4.refs_0_, f32[3,192,192]{2,1,0:T(8,128)} %refs_1_.5, f32[3,2,192,128]{3,2,1,0:T(8,128)S(1)} %get-tuple-element.33.refs_2_.refs_1_), custom_call_target="tpu_custom_call" | custom-call | flops 100000000 | bytes 4194304 | tf_op jit(solution)/shard_map/pallas_call | solution.py:300
  23.2 0.0 collective-permute-done.2.refs_6_
  23.2 1.7 %collective-permute-done.3.refs_7_ = f32[3,2,8,128]{3,2,1,0:T(8,128)S(1)} collective-permute-done((f32[3,2,8,128]{3,2,1,0:T(8,128)S(1)}, f32[3,2,8,128]{3,2,1,0:T(8,128)S(1)}, u32[]{:S(2)}, u32[]{:S(2)}) %collective-permute-start.3) | collective-permute-done | bytes 24608 | tf_op jit(solution)/shard_map/ppermute | solution.py:337
  24.9 0.0 collective-permute-done.refs_2_
  24.9 0.0 collective-permute-done.1.refs_3_
  24.9 1.4 %shard_map.39 = (f32[3,2,192,128]{3,2,1,0:T(8,128)S(1)}, f32[2,192,128]{2,1,0:T(8,128)S(1)}, f32[3,2,192,128]{3,2,1,0:T(8,128)S(1)}, f32[8,3,8,128]{3,2,1,0:T(8,128)}) custom-call(f32[1]{0:T(128)S(6)} %copy.4.refs_0_, f32[3,2,192,128]{3,2,1,0:T(8,128)S(1)} %get-tuple-element.33.refs_2_.refs_1_, f32[3,2,192,128]{3,2,1,0:T(8,128)S(1)} %collective-permute-done.refs_2_, ...), custom_call_target="tpu_custom_call" | custom-call | flops 1000000000 | bytes 4194304 | tf_op jit(solution)/shard_map/pallas_call | solution.py:300
  26.3 7.8 %all-to-all-start = ((f32[8,24,128]{2,1,0:T(8,128)}), f32[8,24,128]{2,1,0:T(8,128)S(1)}, u32[]{:S(2)}, u32[]{:S(2)}) async-start(f32[8,24,128]{2,1,0:T(8,128)} %bitcast), calls=%async_computation | async-start | bytes 196608 | tf_op jit(solution)/shard_map/all_to_all | solution.py:317
  34.1 1.9 %collective-permute-start.4 = (f32[3,2,192,128]{3,2,1,0:T(8,128)S(1)}, f32[3,2,192,128]{3,2,1,0:T(8,128)S(1)}, u32[]{:S(2)}, u32[]{:S(2)}) collective-permute-start(f32[3,2,192,128]{3,2,1,0:T(8,128)S(1)} %get-tuple-element.39.g_ref), channel_id=1, source_target_pairs={{8,16},{16,8},{24,32},{32,24},{40,48},{48,40},{56,64},{64,56},{72,... | collective-permute-start | bytes 1769480 | tf_op jit(solution)/shard_map/ppermute | solution.py:362
  36.0 5.4 %all-to-all-done = f32[8,24,128]{2,1,0:T(8,128)S(1)} async-done(((f32[8,24,128]{2,1,0:T(8,128)}), f32[8,24,128]{2,1,0:T(8,128)S(1)}, u32[]{:S(2)}, u32[]{:S(2)}) %all-to-all-start) | async-done | bytes 98336 | tf_op jit(solution)/shard_map/all_to_all | solution.py:317
  41.3 0.2 shard_map.40
  41.6 1.9 %collective-permute-start.5 = (f32[3,2,192,128]{3,2,1,0:T(8,128)S(1)}, f32[3,2,192,128]{3,2,1,0:T(8,128)S(1)}, u32[]{:S(2)}, u32[]{:S(2)}) collective-permute-start(f32[3,2,192,128]{3,2,1,0:T(8,128)S(1)} %get-tuple-element.41.refs_2_.refs_1_), channel_id=1, source_target_pairs={{0,8},{8,0},{16,24},{24,16},{32,40},{40,32},{48,56},{56,48},{64,72... | collective-permute-start | bytes 1769480 | tf_op jit(solution)/shard_map/ppermute | solution.py:344
  43.5 2.7 %collective-permute-start.6 = (f32[2,8,128]{2,1,0:T(8,128)S(1)}, f32[2,8,128]{2,1,0:T(8,128)S(1)}, u32[]{:S(2)}, u32[]{:S(2)}) collective-permute-start(f32[2,8,128]{2,1,0:T(8,128)S(1)} %get-tuple-element.47), channel_id=1, source_target_pairs={{8,16},{16,8},{24,32},{32,24},{40,48},{48,40},{56,64},{64,56},{72,... | collective-permute-start | bytes 24584 | tf_op jit(solution)/shard_map/ppermute | solution.py:341
  46.2 1.0 %shard_map.41 = (f32[3,2,192,128]{3,2,1,0:T(8,128)S(1)}, f32[192,192]{1,0:T(8,128)S(1)}, f32[3,2,192,128]{3,2,1,0:T(8,128)S(1)}) custom-call(f32[1]{0:T(128)S(6)} %copy.4.refs_0_, f32[3,192,192]{2,1,0:T(8,128)} %refs_1_.5, f32[3,2,192,128]{3,2,1,0:T(8,128)S(1)} %get-tuple-element.41.refs_2_.refs_1_, f32[4,8,128]{2,1,0:T(8,128)S(1)} %get-tuple-element.42.refs_3_, ...), custom_call_target="tpu_custom_call" | custom-call | flops 100000000 | bytes 4194304 | tf_op jit(solution)/shard_map/pallas_call | solution.py:300
  47.2 4.6 %collective-permute-done.6.refs_6_ = f32[2,8,128]{2,1,0:T(8,128)S(1)} collective-permute-done((f32[2,8,128]{2,1,0:T(8,128)S(1)}, f32[2,8,128]{2,1,0:T(8,128)S(1)}, u32[]{:S(2)}, u32[]{:S(2)}) %collective-permute-start.6) | collective-permute-done | bytes 8224 | tf_op jit(solution)/shard_map/ppermute | solution.py:341
  51.8 0.0 collective-permute-done.4.refs_2_
  51.8 0.0 collective-permute-done.5.refs_3_
  51.8 1.4 %shard_map.42 = (f32[3,2,192,128]{3,2,1,0:T(8,128)S(1)}, f32[2,192,128]{2,1,0:T(8,128)S(1)}, f32[3,2,192,128]{3,2,1,0:T(8,128)S(1)}, f32[8,3,8,128]{3,2,1,0:T(8,128)}) custom-call(f32[1]{0:T(128)S(6)} %copy.4.refs_0_, f32[3,2,192,128]{3,2,1,0:T(8,128)S(1)} %get-tuple-element.41.refs_2_.refs_1_, f32[3,2,192,128]{3,2,1,0:T(8,128)S(1)} %collective-permute-done.4.refs_2_, ...), custom_call_target="tpu_custom_call" | custom-call | flops 1000000000 | bytes 4194304 | tf_op jit(solution)/shard_map/pallas_call | solution.py:300
  53.3 4.7 %all-to-all-start.1 = ((f32[8,24,128]{2,1,0:T(8,128)}), f32[8,24,128]{2,1,0:T(8,128)S(1)}, u32[]{:S(2)}, u32[]{:S(2)}) async-start(f32[8,24,128]{2,1,0:T(8,128)} %bitcast.2), calls=%async_computation.1 | async-start | bytes 196608 | tf_op jit(solution)/shard_map/all_to_all | solution.py:317
  58.0 3.5 %collective-permute-start.7 = (f32[3,2,192,128]{3,2,1,0:T(8,128)S(1)}, f32[3,2,192,128]{3,2,1,0:T(8,128)S(1)}, u32[]{:S(2)}, u32[]{:S(2)}) collective-permute-start(f32[3,2,192,128]{3,2,1,0:T(8,128)S(1)} %get-tuple-element.49.g_ref), channel_id=1, source_target_pairs={{8,16},{16,8},{24,32},{32,24},{40,48},{48,40},{56,64},{64,56},{72,... | collective-permute-start | bytes 1769480 | tf_op jit(solution)/shard_map/ppermute | solution.py:362
  61.5 3.8 %all-to-all-done.1 = f32[8,24,128]{2,1,0:T(8,128)S(1)} async-done(((f32[8,24,128]{2,1,0:T(8,128)}), f32[8,24,128]{2,1,0:T(8,128)S(1)}, u32[]{:S(2)}, u32[]{:S(2)}) %all-to-all-start.1) | async-done | bytes 98336 | tf_op jit(solution)/shard_map/all_to_all | solution.py:317
  65.3 0.2 shard_map.43
  65.5 1.9 %collective-permute-start.8 = (f32[3,2,192,128]{3,2,1,0:T(8,128)S(1)}, f32[3,2,192,128]{3,2,1,0:T(8,128)S(1)}, u32[]{:S(2)}, u32[]{:S(2)}) collective-permute-start(f32[3,2,192,128]{3,2,1,0:T(8,128)S(1)} %get-tuple-element.51.refs_2_.refs_1_), channel_id=1, source_target_pairs={{0,8},{8,0},{16,24},{24,16},{32,40},{40,32},{48,56},{56,48},{64,72... | collective-permute-start | bytes 1769480 | tf_op jit(solution)/shard_map/ppermute | solution.py:344
  67.4 2.6 %collective-permute-start.9 = (f32[2,8,128]{2,1,0:T(8,128)S(1)}, f32[2,8,128]{2,1,0:T(8,128)S(1)}, u32[]{:S(2)}, u32[]{:S(2)}) collective-permute-start(f32[2,8,128]{2,1,0:T(8,128)S(1)} %get-tuple-element.57), channel_id=1, source_target_pairs={{8,16},{16,8},{24,32},{32,24},{40,48},{48,40},{56,64},{64,56},{72,... | collective-permute-start | bytes 24584 | tf_op jit(solution)/shard_map/ppermute | solution.py:341
  70.1 0.9 %shard_map.44 = (f32[3,2,192,128]{3,2,1,0:T(8,128)S(1)}, f32[192,192]{1,0:T(8,128)S(1)}) custom-call(f32[1]{0:T(128)S(6)} %copy.4.refs_0_, f32[3,192,192]{2,1,0:T(8,128)} %refs_1_.5, f32[3,2,192,128]{3,2,1,0:T(8,128)S(1)} %get-tuple-element.51.refs_2_.refs_1_, f32[4,8,128]{2,1,0:T(8,128)S(1)} %get-tuple-element.52.refs_3_, ...), custom_call_target="tpu_custom_call" | custom-call | flops 100000000 | bytes 4194304 | tf_op jit(solution)/shard_map/pallas_call | solution.py:300
  71.0 4.7 %collective-permute-done.9.refs_6_ = f32[2,8,128]{2,1,0:T(8,128)S(1)} collective-permute-done((f32[2,8,128]{2,1,0:T(8,128)S(1)}, f32[2,8,128]{2,1,0:T(8,128)S(1)}, u32[]{:S(2)}, u32[]{:S(2)}) %collective-permute-start.9) | collective-permute-done | bytes 8224 | tf_op jit(solution)/shard_map/ppermute | solution.py:341
  75.7 0.0 collective-permute-done.7.refs_2_
  75.7 0.0 collective-permute-done.8.refs_3_
  75.7 0.9 %shard_map.45 = (f32[3,2,192,128]{3,2,1,0:T(8,128)S(1)}, f32[2,192,128]{2,1,0:T(8,128)S(1)}, f32[8,2,8,128]{3,2,1,0:T(8,128)S(1)}) custom-call(f32[1]{0:T(128)S(6)} %copy.4.refs_0_, f32[3,2,192,128]{3,2,1,0:T(8,128)S(1)} %get-tuple-element.51.refs_2_.refs_1_, f32[3,2,192,128]{3,2,1,0:T(8,128)S(1)} %collective-permute-done.7.refs_2_, ...), custom_call_target="tpu_custom_call" | custom-call | flops 1000000000 | bytes 4194304 | tf_op jit(solution)/shard_map/pallas_call | solution.py:300
  76.7 10.8 %all_to_all.15 = f32[8,16,128]{2,1,0:T(8,128)S(1)} all-to-all(f32[8,16,128]{2,1,0:T(8,128)S(1)} %bitcast.9), channel_id=1, replica_groups=mesh['gx'=64,'gy'=8] {'gy'}, dimensions={0} | all-to-all | bytes 131072 | tf_op jit(solution)/shard_map/all_to_all | solution.py:317
  87.5 1.0 %shard_map.46 = f32[3,2,192,128]{3,2,1,0:T(8,128)} custom-call(f32[8,2,8,128]{3,2,1,0:T(8,128)S(1)} %bitcast.8, f32[3,2,192,128]{3,2,1,0:T(8,128)S(1)} %get-tuple-element.59.g_ref, f32[2,192,128]{2,1,0:T(8,128)S(1)} %get-tuple-element.60.vw_ref), custom_call_target="tpu_custom_call" | custom-call | flops 100000000 | bytes 4194304 | tf_op jit(solution)/shard_map/pallas_call | solution.py:300
Async XLA Ops:
  0.0 24.9 %collective-permute-start = (f32[3,2,192,128]{3,2,1,0:T(8,128)}, f32[3,2,192,128]{3,2,1,0:T(8,128)S(1)}, u32[]{:S(2)}, u32[]{:S(2)}) collective-permute-start(f32[3,2,192,128]{3,2,1,0:T(8,128)} %velocity.1), channel_id=1, source_target_pairs={{8,16},{16,8},{24,32},{32,24},{40,48},{48,40},{56,64},{64,56},{72,... | collective-permute-start | bytes 1769480 | tf_op jit(solution)/shard_map/ppermute | solution.py:333
  13.8 11.1 %collective-permute-start.1 = (f32[3,2,192,128]{3,2,1,0:T(8,128)S(1)}, f32[3,2,192,128]{3,2,1,0:T(8,128)S(1)}, u32[]{:S(2)}, u32[]{:S(2)}) collective-permute-start(f32[3,2,192,128]{3,2,1,0:T(8,128)S(1)} %get-tuple-element.33.refs_2_.refs_1_), channel_id=1, source_target_pairs={{0,8},{8,0},{16,24},{24,16},{32,40},{40,32},{48,56},{56,48},{64,72... | collective-permute-start | bytes 1769480 | tf_op jit(solution)/shard_map/ppermute | solution.py:344
  15.7 7.5 %collective-permute-start.2 = (f32[3,2,8,128]{3,2,1,0:T(8,128)S(1)}, f32[3,2,8,128]{3,2,1,0:T(8,128)S(1)}, u32[]{:S(2)}, u32[]{:S(2)}) collective-permute-start(f32[3,2,8,128]{3,2,1,0:T(8,128)S(1)} %get-tuple-element.36), channel_id=1, source_target_pairs={{0,1},{1,2},{2,3},{3,4},{4,5},{5,6},{6,7},{8,9},{9,10},{10,11},{11... | collective-permute-start | bytes 73736 | tf_op jit(solution)/shard_map/ppermute | solution.py:336
  19.2 5.7 %collective-permute-start.3 = (f32[3,2,8,128]{3,2,1,0:T(8,128)S(1)}, f32[3,2,8,128]{3,2,1,0:T(8,128)S(1)}, u32[]{:S(2)}, u32[]{:S(2)}) collective-permute-start(f32[3,2,8,128]{3,2,1,0:T(8,128)S(1)} %get-tuple-element.37), channel_id=1, source_target_pairs={{1,0},{2,1},{3,2},{4,3},{5,4},{6,5},{7,6},{9,8},{10,9},{11,10},{12... | collective-permute-start | bytes 73736 | tf_op jit(solution)/shard_map/ppermute | solution.py:337
  26.3 15.0 %all-to-all-start = ((f32[8,24,128]{2,1,0:T(8,128)}), f32[8,24,128]{2,1,0:T(8,128)S(1)}, u32[]{:S(2)}, u32[]{:S(2)}) async-start(f32[8,24,128]{2,1,0:T(8,128)} %bitcast), calls=%async_computation | async-start | bytes 196608 | tf_op jit(solution)/shard_map/all_to_all | solution.py:317
  34.1 17.7 %collective-permute-start.4 = (f32[3,2,192,128]{3,2,1,0:T(8,128)S(1)}, f32[3,2,192,128]{3,2,1,0:T(8,128)S(1)}, u32[]{:S(2)}, u32[]{:S(2)}) collective-permute-start(f32[3,2,192,128]{3,2,1,0:T(8,128)S(1)} %get-tuple-element.39.g_ref), channel_id=1, source_target_pairs={{8,16},{16,8},{24,32},{32,24},{40,48},{48,40},{56,64},{64,56},{72,... | collective-permute-start | bytes 1769480 | tf_op jit(solution)/shard_map/ppermute | solution.py:362
  41.6 10.2 %collective-permute-start.5 = (f32[3,2,192,128]{3,2,1,0:T(8,128)S(1)}, f32[3,2,192,128]{3,2,1,0:T(8,128)S(1)}, u32[]{:S(2)}, u32[]{:S(2)}) collective-permute-start(f32[3,2,192,128]{3,2,1,0:T(8,128)S(1)} %get-tuple-element.41.refs_2_.refs_1_), channel_id=1, source_target_pairs={{0,8},{8,0},{16,24},{24,16},{32,40},{40,32},{48,56},{56,48},{64,72... | collective-permute-start | bytes 1769480 | tf_op jit(solution)/shard_map/ppermute | solution.py:344
  43.5 8.3 %collective-permute-start.6 = (f32[2,8,128]{2,1,0:T(8,128)S(1)}, f32[2,8,128]{2,1,0:T(8,128)S(1)}, u32[]{:S(2)}, u32[]{:S(2)}) collective-permute-start(f32[2,8,128]{2,1,0:T(8,128)S(1)} %get-tuple-element.47), channel_id=1, source_target_pairs={{8,16},{16,8},{24,32},{32,24},{40,48},{48,40},{56,64},{64,56},{72,... | collective-permute-start | bytes 24584 | tf_op jit(solution)/shard_map/ppermute | solution.py:341
  53.3 12.0 %all-to-all-start.1 = ((f32[8,24,128]{2,1,0:T(8,128)}), f32[8,24,128]{2,1,0:T(8,128)S(1)}, u32[]{:S(2)}, u32[]{:S(2)}) async-start(f32[8,24,128]{2,1,0:T(8,128)} %bitcast.2), calls=%async_computation.1 | async-start | bytes 196608 | tf_op jit(solution)/shard_map/all_to_all | solution.py:317
  58.0 17.7 %collective-permute-start.7 = (f32[3,2,192,128]{3,2,1,0:T(8,128)S(1)}, f32[3,2,192,128]{3,2,1,0:T(8,128)S(1)}, u32[]{:S(2)}, u32[]{:S(2)}) collective-permute-start(f32[3,2,192,128]{3,2,1,0:T(8,128)S(1)} %get-tuple-element.49.g_ref), channel_id=1, source_target_pairs={{8,16},{16,8},{24,32},{32,24},{40,48},{48,40},{56,64},{64,56},{72,... | collective-permute-start | bytes 1769480 | tf_op jit(solution)/shard_map/ppermute | solution.py:362
  65.5 10.2 %collective-permute-start.8 = (f32[3,2,192,128]{3,2,1,0:T(8,128)S(1)}, f32[3,2,192,128]{3,2,1,0:T(8,128)S(1)}, u32[]{:S(2)}, u32[]{:S(2)}) collective-permute-start(f32[3,2,192,128]{3,2,1,0:T(8,128)S(1)} %get-tuple-element.51.refs_2_.refs_1_), channel_id=1, source_target_pairs={{0,8},{8,0},{16,24},{24,16},{32,40},{40,32},{48,56},{56,48},{64,72... | collective-permute-start | bytes 1769480 | tf_op jit(solution)/shard_map/ppermute | solution.py:344
  67.4 8.3 %collective-permute-start.9 = (f32[2,8,128]{2,1,0:T(8,128)S(1)}, f32[2,8,128]{2,1,0:T(8,128)S(1)}, u32[]{:S(2)}, u32[]{:S(2)}) collective-permute-start(f32[2,8,128]{2,1,0:T(8,128)S(1)} %get-tuple-element.57), channel_id=1, source_target_pairs={{8,16},{16,8},{24,32},{32,24},{40,48},{48,40},{56,64},{64,56},{72,... | collective-permute-start | bytes 24584 | tf_op jit(solution)/shard_map/ppermute | solution.py:341

commit v8 on v6

--- a/solution.py
+++ b/solution.py
@@ -272,11 +272,11 @@
             low = lower[line : line + 1, :]
             high = upper[line : line + 1, :]
             u_ref[c, x] = g_ref[c, x] - vw_ref[0] * low - vw_ref[1] * high
-        if ends_ref is None:
-            pltpu.make_async_copy(u_ref.at[c], out_ref.at[c], sems.at[c]).start()
+            if ends_ref is None:
+                pltpu.make_async_copy(u_ref.at[c, x], out_ref.at[c, x], sems.at[line]).start()
     if ends_ref is None:
-        for c in range(3):
-            pltpu.make_async_copy(u_ref.at[c], out_ref.at[c], sems.at[c]).wait()
+        for c, x in lines():
+            pltpu.make_async_copy(u_ref.at[c, x], out_ref.at[c, x], sems.at[2 * c + x]).wait()
     if ends_ref is not None:
         lf_ref[0] = lower
         lf_ref[1] = upper
@@ -366,7 +366,7 @@
         edge = [scratch(12, 8, LANES)] * 2
         if last:
             outs = [jax.ShapeDtypeStruct((3, 2, CY, LANES), jnp.float32)]
-            edge = edge + [scratch(3, 2, CY, LANES), pltpu.SemaphoreType.DMA((3,))]
+            edge = edge + [scratch(3, 2, CY, LANES), pltpu.SemaphoreType.DMA((6,))]
             return call(correct, [got, g, vw], outs, edge, 10**8, hbm_outs=1)[0]
         outs = [field, f32(4, 8, LANES), f32(2, 8, LANES)]
         current, ends, lf = call(correct, [got, g, vw], outs, edge, 10**8)

time: 88.1 us -> 88.1 us (level)
  no operation moved by 1% of the time
where the time goes in v8:
time: 88.1 us; the launch traced here: 87.5 us
  starting transfers between devices  47.1 us (53%)
  waiting for transfers between devices  19.6 us (22%)
  blocking collectives  10.8 us (12%)
  Pallas kernels  9.23 us (10%)
    ppermute x1, starting transfers between devices, body(): far = lax.ppermute(velocity, 'gx', across)  12.6 us
    all_to_all x2, starting transfers between devices, exchange(): lax.all_to_all(flat, 'gy', split_axis=0, concat_axis=0).reshape(send.shape)  11.3 us
    all_to_all x1, blocking collectives, exchange(): lax.all_to_all(flat, 'gy', split_axis=0, concat_axis=0).reshape(send.shape)  10.8 us
    pallas_call x10, Pallas kernels, call(): pl.pallas_call(kernel, out_shape=outs, in_specs=[SMEM] * len(scalars) + [...  9.23 us
    ppermute x2, waiting for transfers between devices, body(): far_lf = lax.ppermute(lf, 'gx', across)  8.7 us
    all_to_all x2, waiting for transfers between devices, exchange(): lax.all_to_all(flat, 'gy', split_axis=0, concat_axis=0).reshape(send.shape)  8.46 us
    ppermute x2, starting transfers between devices, body(): far = lax.ppermute(g, 'gx', across)  6.1 us
    ppermute x2, starting transfers between devices, body(): far_lf = lax.ppermute(lf, 'gx', across)  5.94 us
  transfers between devices with their start and end apart: 12, of which 5 were waited for; matrix products, arithmetic and copies ran while one was open for 0% of the time, Pallas kernels for 5%

profile of v8, /device:TPU:8, one launch (start us, length us, event | category | flops | bytes accessed | tf_op | source)
XLA Modules:
  0.0 87.5 jit_solution(4800208787745045181)
XLA Ops:
  0.0 12.6 %collective-permute-start = (f32[3,2,192,128]{3,2,1,0:T(8,128)}, f32[3,2,192,128]{3,2,1,0:T(8,128)S(1)}, u32[]{:S(2)}, u32[]{:S(2)}) collective-permute-start(f32[3,2,192,128]{3,2,1,0:T(8,128)} %velocity.1), channel_id=1, source_target_pairs={{8,16},{16,8},{24,32},{32,24},{40,48},{48,40},{56,64},{64,56},{72,... | collective-permute-start | bytes 1769480 | tf_op jit(solution)/shard_map/ppermute | solution.py:335
  12.6 1.2 %shard_map.37 = (f32[3,2,192,128]{3,2,1,0:T(8,128)S(1)}, f32[3,2,16,128]{3,2,1,0:T(8,128)S(1)}) custom-call(f32[3,2,192,128]{3,2,1,0:T(8,128)} %velocity.1), custom_call_target="tpu_custom_call" | custom-call | flops 1000000 | bytes 4194304 | tf_op jit(solution)/shard_map/pallas_call | solution.py:302
  13.8 1.9 %collective-permute-start.1 = (f32[3,2,192,128]{3,2,1,0:T(8,128)S(1)}, f32[3,2,192,128]{3,2,1,0:T(8,128)S(1)}, u32[]{:S(2)}, u32[]{:S(2)}) collective-permute-start(f32[3,2,192,128]{3,2,1,0:T(8,128)S(1)} %get-tuple-element.32.refs_2_.refs_1_), channel_id=1, source_target_pairs={{0,8},{8,0},{16,24},{24,16},{32,40},{40,32},{48,56},{56,48},{64,72... | collective-permute-start | bytes 1769480 | tf_op jit(solution)/shard_map/ppermute | solution.py:346
  15.7 3.5 %collective-permute-start.3 = (f32[3,2,16,128]{3,2,1,0:T(8,128)S(1)}, f32[3,2,16,128]{3,2,1,0:T(8,128)S(1)}, u32[]{:S(2)}, u32[]{:S(2)}) collective-permute-start(f32[3,2,16,128]{3,2,1,0:T(8,128)S(1)} %get-tuple-element.35), channel_id=1, source_target_pairs={{1,2},{2,1},{3,4},{4,3},{5,6},{6,5},{9,10},{10,9},{11,12},{12,11},... | collective-permute-start | bytes 147464 | tf_op jit(solution)/shard_map/ppermute | solution.py:339
  19.2 1.9 %collective-permute-start.2 = (f32[3,2,16,128]{3,2,1,0:T(8,128)S(1)}, f32[3,2,16,128]{3,2,1,0:T(8,128)S(1)}, u32[]{:S(2)}, u32[]{:S(2)}) collective-permute-start(f32[3,2,16,128]{3,2,1,0:T(8,128)S(1)} %get-tuple-element.35), channel_id=1, source_target_pairs={{0,1},{1,0},{2,3},{3,2},{4,5},{5,4},{6,7},{7,6},{8,9},{9,8},{10,11... | collective-permute-start | bytes 147464 | tf_op jit(solution)/shard_map/ppermute | solution.py:338
  21.8 1.0 %shard_map.38 = (f32[3,2,192,128]{3,2,1,0:T(8,128)S(1)}, f32[192,192]{1,0:T(8,128)S(1)}, f32[3,2,192,128]{3,2,1,0:T(8,128)S(1)}) custom-call(f32[1]{0:T(128)S(6)} %copy.4.refs_0_, f32[3,192,192]{2,1,0:T(8,128)} %refs_1_.5, f32[3,2,192,128]{3,2,1,0:T(8,128)S(1)} %get-tuple-element.32.refs_2_.refs_1_), custom_call_target="tpu_custom_call" | custom-call | flops 100000000 | bytes 4194304 | tf_op jit(solution)/shard_map/pallas_call | solution.py:302
  22.7 0.0 collective-permute-done.3.refs_7_
  22.7 2.4 %collective-permute-done.2.refs_6_ = f32[3,2,16,128]{3,2,1,0:T(8,128)S(1)} collective-permute-done((f32[3,2,16,128]{3,2,1,0:T(8,128)S(1)}, f32[3,2,16,128]{3,2,1,0:T(8,128)S(1)}, u32[]{:S(2)}, u32[]{:S(2)}) %collective-permute-start.2) | collective-permute-done | bytes 49184 | tf_op jit(solution)/shard_map/ppermute | solution.py:338
  25.2 0.0 collective-permute-done.refs_2_
  25.2 0.0 collective-permute-done.1.refs_3_
  25.2 1.4 %shard_map.39 = (f32[3,2,192,128]{3,2,1,0:T(8,128)S(1)}, f32[2,192,128]{2,1,0:T(8,128)S(1)}, f32[3,2,192,128]{3,2,1,0:T(8,128)S(1)}, f32[8,3,8,128]{3,2,1,0:T(8,128)}) custom-call(f32[1]{0:T(128)S(6)} %copy.4.refs_0_, f32[3,2,192,128]{3,2,1,0:T(8,128)S(1)} %get-tuple-element.32.refs_2_.refs_1_, f32[3,2,192,128]{3,2,1,0:T(8,128)S(1)} %collective-permute-done.refs_2_, ...), custom_call_target="tpu_custom_call" | custom-call | flops 1000000000 | bytes 4194304 | tf_op jit(solution)/shard_map/pallas_call | solution.py:302
  26.6 6.5 %all-to-all-start = ((f32[8,24,128]{2,1,0:T(8,128)}), f32[8,24,128]{2,1,0:T(8,128)S(1)}, u32[]{:S(2)}, u32[]{:S(2)}) async-start(f32[8,24,128]{2,1,0:T(8,128)} %bitcast), calls=%async_computation | async-start | bytes 196608 | tf_op jit(solution)/shard_map/all_to_all | solution.py:319
  33.1 2.6 %collective-permute-start.4 = (f32[3,2,192,128]{3,2,1,0:T(8,128)S(1)}, f32[3,2,192,128]{3,2,1,0:T(8,128)S(1)}, u32[]{:S(2)}, u32[]{:S(2)}) collective-permute-start(f32[3,2,192,128]{3,2,1,0:T(8,128)S(1)} %get-tuple-element.37.g_ref), channel_id=1, source_target_pairs={{8,16},{16,8},{24,32},{32,24},{40,48},{48,40},{56,64},{64,56},{72,... | collective-permute-start | bytes 1769480 | tf_op jit(solution)/shard_map/ppermute | solution.py:364
  35.7 4.7 %all-to-all-done = f32[8,24,128]{2,1,0:T(8,128)S(1)} async-done(((f32[8,24,128]{2,1,0:T(8,128)}), f32[8,24,128]{2,1,0:T(8,128)S(1)}, u32[]{:S(2)}, u32[]{:S(2)}) %all-to-all-start) | async-done | bytes 98336 | tf_op jit(solution)/shard_map/all_to_all | solution.py:319
  40.4 0.2 shard_map.40
  40.6 1.9 %collective-permute-start.5 = (f32[3,2,192,128]{3,2,1,0:T(8,128)S(1)}, f32[3,2,192,128]{3,2,1,0:T(8,128)S(1)}, u32[]{:S(2)}, u32[]{:S(2)}) collective-permute-start(f32[3,2,192,128]{3,2,1,0:T(8,128)S(1)} %get-tuple-element.39.refs_2_.refs_1_), channel_id=1, source_target_pairs={{0,8},{8,0},{16,24},{24,16},{32,40},{40,32},{48,56},{56,48},{64,72... | collective-permute-start | bytes 1769480 | tf_op jit(solution)/shard_map/ppermute | solution.py:346
  42.6 3.3 %collective-permute-start.6 = (f32[2,8,128]{2,1,0:T(8,128)S(1)}, f32[2,8,128]{2,1,0:T(8,128)S(1)}, u32[]{:S(2)}, u32[]{:S(2)}) collective-permute-start(f32[2,8,128]{2,1,0:T(8,128)S(1)} %get-tuple-element.45), channel_id=1, source_target_pairs={{8,16},{16,8},{24,32},{32,24},{40,48},{48,40},{56,64},{64,56},{72,... | collective-permute-start | bytes 24584 | tf_op jit(solution)/shard_map/ppermute | solution.py:343
  45.9 1.0 %shard_map.41 = (f32[3,2,192,128]{3,2,1,0:T(8,128)S(1)}, f32[192,192]{1,0:T(8,128)S(1)}, f32[3,2,192,128]{3,2,1,0:T(8,128)S(1)}) custom-call(f32[1]{0:T(128)S(6)} %copy.4.refs_0_, f32[3,192,192]{2,1,0:T(8,128)} %refs_1_.5, f32[3,2,192,128]{3,2,1,0:T(8,128)S(1)} %get-tuple-element.39.refs_2_.refs_1_, f32[4,8,128]{2,1,0:T(8,128)S(1)} %get-tuple-element.40.refs_3_, ...), custom_call_target="tpu_custom_call" | custom-call | flops 100000000 | bytes 4194304 | tf_op jit(solution)/shard_map/pallas_call | solution.py:302
  46.8 4.0 %collective-permute-done.6.refs_6_ = f32[2,8,128]{2,1,0:T(8,128)S(1)} collective-permute-done((f32[2,8,128]{2,1,0:T(8,128)S(1)}, f32[2,8,128]{2,1,0:T(8,128)S(1)}, u32[]{:S(2)}, u32[]{:S(2)}) %collective-permute-start.6) | collective-permute-done | bytes 8224 | tf_op jit(solution)/shard_map/ppermute | solution.py:343
  50.8 0.0 collective-permute-done.4.refs_2_
  50.9 0.0 collective-permute-done.5.refs_3_
  50.9 1.4 %shard_map.42 = (f32[3,2,192,128]{3,2,1,0:T(8,128)S(1)}, f32[2,192,128]{2,1,0:T(8,128)S(1)}, f32[3,2,192,128]{3,2,1,0:T(8,128)S(1)}, f32[8,3,8,128]{3,2,1,0:T(8,128)}) custom-call(f32[1]{0:T(128)S(6)} %copy.4.refs_0_, f32[3,2,192,128]{3,2,1,0:T(8,128)S(1)} %get-tuple-element.39.refs_2_.refs_1_, f32[3,2,192,128]{3,2,1,0:T(8,128)S(1)} %collective-permute-done.4.refs_2_, ...), custom_call_target="tpu_custom_call" | custom-call | flops 1000000000 | bytes 4194304 | tf_op jit(solution)/shard_map/pallas_call | solution.py:302
  52.3 4.7 %all-to-all-start.1 = ((f32[8,24,128]{2,1,0:T(8,128)}), f32[8,24,128]{2,1,0:T(8,128)S(1)}, u32[]{:S(2)}, u32[]{:S(2)}) async-start(f32[8,24,128]{2,1,0:T(8,128)} %bitcast.2), calls=%async_computation.1 | async-start | bytes 196608 | tf_op jit(solution)/shard_map/all_to_all | solution.py:319
  57.0 3.5 %collective-permute-start.7 = (f32[3,2,192,128]{3,2,1,0:T(8,128)S(1)}, f32[3,2,192,128]{3,2,1,0:T(8,128)S(1)}, u32[]{:S(2)}, u32[]{:S(2)}) collective-permute-start(f32[3,2,192,128]{3,2,1,0:T(8,128)S(1)} %get-tuple-element.47.g_ref), channel_id=1, source_target_pairs={{8,16},{16,8},{24,32},{32,24},{40,48},{48,40},{56,64},{64,56},{72,... | collective-permute-start | bytes 1769480 | tf_op jit(solution)/shard_map/ppermute | solution.py:364
  60.6 3.8 %all-to-all-done.1 = f32[8,24,128]{2,1,0:T(8,128)S(1)} async-done(((f32[8,24,128]{2,1,0:T(8,128)}), f32[8,24,128]{2,1,0:T(8,128)S(1)}, u32[]{:S(2)}, u32[]{:S(2)}) %all-to-all-start.1) | async-done | bytes 98336 | tf_op jit(solution)/shard_map/all_to_all | solution.py:319
  64.3 0.2 shard_map.43
  64.6 1.9 %collective-permute-start.8 = (f32[3,2,192,128]{3,2,1,0:T(8,128)S(1)}, f32[3,2,192,128]{3,2,1,0:T(8,128)S(1)}, u32[]{:S(2)}, u32[]{:S(2)}) collective-permute-start(f32[3,2,192,128]{3,2,1,0:T(8,128)S(1)} %get-tuple-element.49.refs_2_.refs_1_), channel_id=1, source_target_pairs={{0,8},{8,0},{16,24},{24,16},{32,40},{40,32},{48,56},{56,48},{64,72... | collective-permute-start | bytes 1769480 | tf_op jit(solution)/shard_map/ppermute | solution.py:346
  66.5 2.6 %collective-permute-start.9 = (f32[2,8,128]{2,1,0:T(8,128)S(1)}, f32[2,8,128]{2,1,0:T(8,128)S(1)}, u32[]{:S(2)}, u32[]{:S(2)}) collective-permute-start(f32[2,8,128]{2,1,0:T(8,128)S(1)} %get-tuple-element.55), channel_id=1, source_target_pairs={{8,16},{16,8},{24,32},{32,24},{40,48},{48,40},{56,64},{64,56},{72,... | collective-permute-start | bytes 24584 | tf_op jit(solution)/shard_map/ppermute | solution.py:343
  69.1 0.9 %shard_map.44 = (f32[3,2,192,128]{3,2,1,0:T(8,128)S(1)}, f32[192,192]{1,0:T(8,128)S(1)}) custom-call(f32[1]{0:T(128)S(6)} %copy.4.refs_0_, f32[3,192,192]{2,1,0:T(8,128)} %refs_1_.5, f32[3,2,192,128]{3,2,1,0:T(8,128)S(1)} %get-tuple-element.49.refs_2_.refs_1_, f32[4,8,128]{2,1,0:T(8,128)S(1)} %get-tuple-element.50.refs_3_, ...), custom_call_target="tpu_custom_call" | custom-call | flops 100000000 | bytes 4194304 | tf_op jit(solution)/shard_map/pallas_call | solution.py:302
  70.1 4.7 %collective-permute-done.9.refs_6_ = f32[2,8,128]{2,1,0:T(8,128)S(1)} collective-permute-done((f32[2,8,128]{2,1,0:T(8,128)S(1)}, f32[2,8,128]{2,1,0:T(8,128)S(1)}, u32[]{:S(2)}, u32[]{:S(2)}) %collective-permute-start.9) | collective-permute-done | bytes 8224 | tf_op jit(solution)/shard_map/ppermute | solution.py:343
  74.8 0.0 collective-permute-done.7.refs_2_
  74.8 0.0 collective-permute-done.8.refs_3_
  74.8 0.9 %shard_map.45 = (f32[3,2,192,128]{3,2,1,0:T(8,128)S(1)}, f32[2,192,128]{2,1,0:T(8,128)S(1)}, f32[8,2,8,128]{3,2,1,0:T(8,128)S(1)}) custom-call(f32[1]{0:T(128)S(6)} %copy.4.refs_0_, f32[3,2,192,128]{3,2,1,0:T(8,128)S(1)} %get-tuple-element.49.refs_2_.refs_1_, f32[3,2,192,128]{3,2,1,0:T(8,128)S(1)} %collective-permute-done.7.refs_2_, ...), custom_call_target="tpu_custom_call" | custom-call | flops 1000000000 | bytes 4194304 | tf_op jit(solution)/shard_map/pallas_call | solution.py:302
  75.7 10.8 %all_to_all.15 = f32[8,16,128]{2,1,0:T(8,128)S(1)} all-to-all(f32[8,16,128]{2,1,0:T(8,128)S(1)} %bitcast.9), channel_id=1, replica_groups=mesh['gx'=64,'gy'=8] {'gy'}, dimensions={0} | all-to-all | bytes 131072 | tf_op jit(solution)/shard_map/all_to_all | solution.py:319
  86.5 1.0 %shard_map.46 = f32[3,2,192,128]{3,2,1,0:T(8,128)} custom-call(f32[8,2,8,128]{3,2,1,0:T(8,128)S(1)} %bitcast.8, f32[3,2,192,128]{3,2,1,0:T(8,128)S(1)} %get-tuple-element.57.g_ref, f32[2,192,128]{2,1,0:T(8,128)S(1)} %get-tuple-element.58.vw_ref), custom_call_target="tpu_custom_call" | custom-call | flops 100000000 | bytes 4194304 | tf_op jit(solution)/shard_map/pallas_call | solution.py:302
Async XLA Ops:
  0.0 25.2 %collective-permute-start = (f32[3,2,192,128]{3,2,1,0:T(8,128)}, f32[3,2,192,128]{3,2,1,0:T(8,128)S(1)}, u32[]{:S(2)}, u32[]{:S(2)}) collective-permute-start(f32[3,2,192,128]{3,2,1,0:T(8,128)} %velocity.1), channel_id=1, source_target_pairs={{8,16},{16,8},{24,32},{32,24},{40,48},{48,40},{56,64},{64,56},{72,... | collective-permute-start | bytes 1769480 | tf_op jit(solution)/shard_map/ppermute | solution.py:335
  13.8 11.4 %collective-permute-start.1 = (f32[3,2,192,128]{3,2,1,0:T(8,128)S(1)}, f32[3,2,192,128]{3,2,1,0:T(8,128)S(1)}, u32[]{:S(2)}, u32[]{:S(2)}) collective-permute-start(f32[3,2,192,128]{3,2,1,0:T(8,128)S(1)} %get-tuple-element.32.refs_2_.refs_1_), channel_id=1, source_target_pairs={{0,8},{8,0},{16,24},{24,16},{32,40},{40,32},{48,56},{56,48},{64,72... | collective-permute-start | bytes 1769480 | tf_op jit(solution)/shard_map/ppermute | solution.py:346
  15.7 7.0 %collective-permute-start.3 = (f32[3,2,16,128]{3,2,1,0:T(8,128)S(1)}, f32[3,2,16,128]{3,2,1,0:T(8,128)S(1)}, u32[]{:S(2)}, u32[]{:S(2)}) collective-permute-start(f32[3,2,16,128]{3,2,1,0:T(8,128)S(1)} %get-tuple-element.35), channel_id=1, source_target_pairs={{1,2},{2,1},{3,4},{4,3},{5,6},{6,5},{9,10},{10,9},{11,12},{12,11},... | collective-permute-start | bytes 147464 | tf_op jit(solution)/shard_map/ppermute | solution.py:339
  19.2 6.0 %collective-permute-start.2 = (f32[3,2,16,128]{3,2,1,0:T(8,128)S(1)}, f32[3,2,16,128]{3,2,1,0:T(8,128)S(1)}, u32[]{:S(2)}, u32[]{:S(2)}) collective-permute-start(f32[3,2,16,128]{3,2,1,0:T(8,128)S(1)} %get-tuple-element.35), channel_id=1, source_target_pairs={{0,1},{1,0},{2,3},{3,2},{4,5},{5,4},{6,7},{7,6},{8,9},{9,8},{10,11... | collective-permute-start | bytes 147464 | tf_op jit(solution)/shard_map/ppermute | solution.py:338
  26.6 13.8 %all-to-all-start = ((f32[8,24,128]{2,1,0:T(8,128)}), f32[8,24,128]{2,1,0:T(8,128)S(1)}, u32[]{:S(2)}, u32[]{:S(2)}) async-start(f32[8,24,128]{2,1,0:T(8,128)} %bitcast), calls=%async_computation | async-start | bytes 196608 | tf_op jit(solution)/shard_map/all_to_all | solution.py:319
  33.1 17.7 %collective-permute-start.4 = (f32[3,2,192,128]{3,2,1,0:T(8,128)S(1)}, f32[3,2,192,128]{3,2,1,0:T(8,128)S(1)}, u32[]{:S(2)}, u32[]{:S(2)}) collective-permute-start(f32[3,2,192,128]{3,2,1,0:T(8,128)S(1)} %get-tuple-element.37.g_ref), channel_id=1, source_target_pairs={{8,16},{16,8},{24,32},{32,24},{40,48},{48,40},{56,64},{64,56},{72,... | collective-permute-start | bytes 1769480 | tf_op jit(solution)/shard_map/ppermute | solution.py:364
  40.6 10.2 %collective-permute-start.5 = (f32[3,2,192,128]{3,2,1,0:T(8,128)S(1)}, f32[3,2,192,128]{3,2,1,0:T(8,128)S(1)}, u32[]{:S(2)}, u32[]{:S(2)}) collective-permute-start(f32[3,2,192,128]{3,2,1,0:T(8,128)S(1)} %get-tuple-element.39.refs_2_.refs_1_), channel_id=1, source_target_pairs={{0,8},{8,0},{16,24},{24,16},{32,40},{40,32},{48,56},{56,48},{64,72... | collective-permute-start | bytes 1769480 | tf_op jit(solution)/shard_map/ppermute | solution.py:346
  42.6 8.3 %collective-permute-start.6 = (f32[2,8,128]{2,1,0:T(8,128)S(1)}, f32[2,8,128]{2,1,0:T(8,128)S(1)}, u32[]{:S(2)}, u32[]{:S(2)}) collective-permute-start(f32[2,8,128]{2,1,0:T(8,128)S(1)} %get-tuple-element.45), channel_id=1, source_target_pairs={{8,16},{16,8},{24,32},{32,24},{40,48},{48,40},{56,64},{64,56},{72,... | collective-permute-start | bytes 24584 | tf_op jit(solution)/shard_map/ppermute | solution.py:343
  52.3 12.0 %all-to-all-start.1 = ((f32[8,24,128]{2,1,0:T(8,128)}), f32[8,24,128]{2,1,0:T(8,128)S(1)}, u32[]{:S(2)}, u32[]{:S(2)}) async-start(f32[8,24,128]{2,1,0:T(8,128)} %bitcast.2), calls=%async_computation.1 | async-start | bytes 196608 | tf_op jit(solution)/shard_map/all_to_all | solution.py:319
  57.0 17.7 %collective-permute-start.7 = (f32[3,2,192,128]{3,2,1,0:T(8,128)S(1)}, f32[3,2,192,128]{3,2,1,0:T(8,128)S(1)}, u32[]{:S(2)}, u32[]{:S(2)}) collective-permute-start(f32[3,2,192,128]{3,2,1,0:T(8,128)S(1)} %get-tuple-element.47.g_ref), channel_id=1, source_target_pairs={{8,16},{16,8},{24,32},{32,24},{40,48},{48,40},{56,64},{64,56},{72,... | collective-permute-start | bytes 1769480 | tf_op jit(solution)/shard_map/ppermute | solution.py:364
  64.6 10.2 %collective-permute-start.8 = (f32[3,2,192,128]{3,2,1,0:T(8,128)S(1)}, f32[3,2,192,128]{3,2,1,0:T(8,128)S(1)}, u32[]{:S(2)}, u32[]{:S(2)}) collective-permute-start(f32[3,2,192,128]{3,2,1,0:T(8,128)S(1)} %get-tuple-element.49.refs_2_.refs_1_), channel_id=1, source_target_pairs={{0,8},{8,0},{16,24},{24,16},{32,40},{40,32},{48,56},{56,48},{64,72... | collective-permute-start | bytes 1769480 | tf_op jit(solution)/shard_map/ppermute | solution.py:346
  66.5 8.3 %collective-permute-start.9 = (f32[2,8,128]{2,1,0:T(8,128)S(1)}, f32[2,8,128]{2,1,0:T(8,128)S(1)}, u32[]{:S(2)}, u32[]{:S(2)}) collective-permute-start(f32[2,8,128]{2,1,0:T(8,128)S(1)} %get-tuple-element.55), channel_id=1, source_target_pairs={{8,16},{16,8},{24,32},{32,24},{40,48},{48,40},{56,64},{64,56},{72,... | collective-permute-start | bytes 24584 | tf_op jit(solution)/shard_map/ppermute | solution.py:343
